TPU v7x, 32 devices: a whole 2x2x4 slice. The times are simulated.
32 devices in a mesh: groups: 2 (over x), seq: 16 (over z, y, core).
Axes of the slice: x: 2, y: 2, z: 4, core: 2. Of those that a mesh axis runs over, the one named last changes fastest.
Arguments:
- hidden: bfloat16 [4096, 8192], P(('groups', 'seq')), parts along dimension 0, may hold values from -6 to 6
- q_base: bfloat16 [4096, 8192], P(('groups', 'seq')), parts along dimension 0, may hold values from -8 to 8
- base_key_weight: bfloat16 [4096, 1024], P(('groups', 'seq')), parts along dimension 0, may hold values from -8 to 8
- base_value_weight: bfloat16 [4096, 1024], P(('groups', 'seq')), parts along dimension 0, may hold values from -6 to 6
- shrink_a: bfloat16 [32, 8192, 192], P('groups', 'seq'), parts along dimension 0, may hold values from -0.0625 to 0.0625
- expand_q: bfloat16 [32, 64, 8192], P('groups', None, 'seq'), parts along dimension 0, may hold values from -0.375 to 0.375
- key_value_up_weight: bfloat16 [32, 64, 2048], P('groups'), parts along dimension 0, may hold values from -0.375 to 0.375
- block_request: int32 [64], P('groups'), parts along dimension 0, may hold values from 0 to 7, never falling along the last dimension, each value on 1 to 16 neighbouring positions
- request_adapter: int32 [16], P('groups'), parts along dimension 0, may hold values from 0 to 15
Outputs:
- attended: bfloat16 [4096, 8192], P(('groups', 'seq')), parts along dimension 0
There are 2 independent parts, one for each index of `groups`. A program takes and returns all parts, laid end to end along the dimension named above; each array names one. Nothing has to cross between parts.
Inputs may be any that keep to these rules, and one draw needn't show every extreme that they name: `block_request`: each request holds 1 to 16 consecutive blocks, request numbers never fall along the blocks, and some request holds exactly 16 blocks.
All inputs are finite; a program needn't handle non-finite values.
Results may differ from a plain program's by a relative error of at most 0.012.
The roundings to bfloat16 on the way count: a program that leaves them out, or rounds other values in their place, can miss the bound.
Values may be sent and summed in bfloat16 or wider, within the bound.
No kernel may reach another device: no remote copies, remote signals or barrier semaphores. Data moves between devices by JAX's collectives and lax.ppermute only.
A program may use at most 128 MiB of HBM per device.

v0:
```python
import functools
import math

import jax
import jax.numpy as jnp
from jax import lax
from jax.experimental import pallas as pl
from jax.experimental.pallas import tpu as pltpu
from jax.sharding import PartitionSpec as P

KEY_VALUE_HEADS = 8
HEAD_SIZE = 128
ADAPTER_RANK = 64
MOST_BLOCKS_CAP = 32
CORES = 2
PLANE = 4
KEY_CHUNK = 512
KEY_STEP = 512
NT = (((1,), (1,)), ((), ()))
TN = (((0,), (0,)), ((), ()))


def split_kernel(hidden_ref, key_ref, value_ref, sent_ref, kv_ref, rows_ref, both_ref, in_sems, out_sems):
    parts, _, span = rows_ref.shape
    width = key_ref.shape[1]
    fetches = [
        pltpu.make_async_copy(key_ref, both_ref.at[:, pl.ds(0, width)], in_sems.at[parts]),
        pltpu.make_async_copy(value_ref, both_ref.at[:, pl.ds(width, width)], in_sems.at[parts + 1]),
    ]
    fetches += [
        pltpu.make_async_copy(hidden_ref.at[:, pl.ds(i * span, span)], rows_ref.at[i], in_sems.at[i])
        for i in range(parts)
    ]
    for fetch in fetches:
        fetch.start()
    fetches[0].wait()
    fetches[1].wait()
    puts = [pltpu.make_async_copy(both_ref, kv_ref, out_sems.at[parts])]
    puts[0].start()
    for i in range(parts):
        fetches[2 + i].wait()
        put = pltpu.make_async_copy(rows_ref.at[i], sent_ref.at[i], out_sems.at[i])
        put.start()
        puts.append(put)
    for put in puts:
        put.wait()


def split(hidden, base_key, base_value, parts):
    tokens, width = hidden.shape
    span = width // parts
    kv_width = base_key.shape[1]
    return pl.pallas_call(
        split_kernel,
        out_shape=(
            jax.ShapeDtypeStruct((parts, tokens, span), hidden.dtype),
            jax.ShapeDtypeStruct((tokens, 2 * kv_width), hidden.dtype),
        ),
        in_specs=[pl.BlockSpec(memory_space=pl.ANY)] * 3,
        out_specs=(pl.BlockSpec(memory_space=pl.ANY),) * 2,
        scratch_shapes=[
            pltpu.VMEM((parts, tokens, span), hidden.dtype),
            pltpu.VMEM((tokens, 2 * kv_width), hidden.dtype),
            pltpu.SemaphoreType.DMA((parts + 2,)),
            pltpu.SemaphoreType.DMA((parts + 1,)),
        ],
        name="split",
    )(hidden, base_key, base_value)


def shrink_kernel(block_len, place_ref, request_ref, adapter_ref, rows_ref, own_ref, other_ref, out_ref):
    sources, tokens, features = rows_ref.shape
    per_device = tokens // block_len
    half = features // CORES
    core = lax.rem(place_ref[0], CORES)
    own_columns = pl.ds(pl.multiple_of(core * half, half), half)
    other_columns = pl.ds(pl.multiple_of((1 - core) * half, half), half)
    first = pl.program_id(0) * sources
    for source in range(sources):
        device = (first + source) * CORES + core
        for part in range(per_device):
            adapter = adapter_ref[request_ref[device * per_device + part]]
            span = pl.ds(part * block_len, block_len)
            total = lax.dot_general(
                own_ref[adapter], rows_ref[source, span, own_columns], NT, preferred_element_type=jnp.float32
            ) + lax.dot_general(
                other_ref[adapter], rows_ref[source, span, other_columns], NT, preferred_element_type=jnp.float32
            )
            out_ref[source, :, span] = total.astype(out_ref.dtype)


def shrink(rows, own, other, place, block_request, request_adapter, block_len):
    chips, tokens, features = rows.shape
    adapters, width, half = own.shape
    steps = min(2, chips)
    sources = chips // steps
    return pl.pallas_call(
        functools.partial(shrink_kernel, block_len),
        out_shape=jax.ShapeDtypeStruct((chips, width, tokens), jnp.bfloat16),
        grid_spec=pltpu.PrefetchScalarGridSpec(
            num_scalar_prefetch=3,
            grid=(steps,),
            in_specs=[
                pl.BlockSpec((sources, tokens, features), lambda i, me, br, ra: (i, 0, 0)),
                pl.BlockSpec((adapters, width, half), lambda i, me, br, ra: (0, 0, 0)),
                pl.BlockSpec((adapters, width, half), lambda i, me, br, ra: (0, 0, 0)),
            ],
            out_specs=pl.BlockSpec((sources, width, tokens), lambda i, me, br, ra: (i, 0, 0)),
        ),
        cost_estimate=pl.CostEstimate(
            flops=2 * chips * tokens * features * width,
            bytes_accessed=2 * (rows.size + own.size + other.size),
            transcendentals=0,
        ),
        name="shrink",
    )(place, block_request, request_adapter, rows, own, other)


def finish_kernel(block_len, planes, place_ref, request_ref, adapter_ref, near_ref, flipped_ref, up_ref, *rest):
    pieces = planes * PLANE
    piece_refs = rest[:pieces]
    out_ref, base_ref, done_ref, in_sems, out_sems = rest[pieces:]
    tokens = piece_refs[0].shape[0]
    per_device = tokens // block_len
    rank = ADAPTER_RANK
    width = base_ref.shape[2] // 2
    me = place_ref[0]
    within = lax.rem(me, PLANE)
    for index in range(pieces):
        pltpu.make_async_copy(piece_refs[index], base_ref.at[index], in_sems.at[index]).start()
    for index in range(pieces):
        back, flip = index // PLANE, index % PLANE
        low_ref = flipped_ref if flip % CORES else near_ref
        low_index = back * (PLANE // CORES) + flip // CORES
        place = within ^ flip
        device = me - within - back * PLANE + place
        pltpu.make_async_copy(piece_refs[index], base_ref.at[index], in_sems.at[index]).wait()
        for part in range(per_device):
            adapter = adapter_ref[request_ref[jnp.maximum(device * per_device + part, 0)]]
            span = pl.ds(part * block_len, block_len)
            for which in range(2):
                columns = pl.ds(which * width, width)
                delta = lax.dot_general(
                    low_ref[low_index, pl.ds(which * rank, rank), span],
                    up_ref[adapter, :, columns],
                    TN,
                    preferred_element_type=jnp.float32,
                )
                done_ref[index, span, columns] = (
                    base_ref[index, span, columns].astype(jnp.float32) + delta
                ).astype(done_ref.dtype)
        slot = (planes - 1 - back) * PLANE + place
        pltpu.make_async_copy(
            done_ref.at[index], out_ref.at[pl.ds(pl.multiple_of(slot * tokens, tokens), tokens), :], out_sems.at[index]
        ).start()
    for index in range(pieces):
        pltpu.make_async_copy(done_ref.at[index], out_ref.at[pl.ds(0, tokens), :], out_sems.at[index]).wait()


def finish(pieces, near, flipped, up_weight, place, block_request, request_adapter, block_len, planes):
    tokens, width = pieces[0].shape
    count = len(pieces)
    return pl.pallas_call(
        functools.partial(finish_kernel, block_len, planes),
        out_shape=jax.ShapeDtypeStruct((count * tokens, width), jnp.bfloat16),
        grid_spec=pltpu.PrefetchScalarGridSpec(
            num_scalar_prefetch=3,
            grid=(1,),
            in_specs=[
                pl.BlockSpec(near.shape, lambda i, me, br, ra: (0, 0, 0)),
                pl.BlockSpec(near.shape, lambda i, me, br, ra: (0, 0, 0)),
                pl.BlockSpec(up_weight.shape, lambda i, me, br, ra: (0, 0, 0)),
            ]
            + [pl.BlockSpec(memory_space=pl.ANY)] * count,
            out_specs=pl.BlockSpec(memory_space=pl.ANY),
            scratch_shapes=[
                pltpu.VMEM((count, tokens, width), jnp.bfloat16),
                pltpu.VMEM((count, tokens, width), jnp.bfloat16),
                pltpu.SemaphoreType.DMA((count,)),
                pltpu.SemaphoreType.DMA((count,)),
            ],
        ),
        cost_estimate=pl.CostEstimate(
            flops=2 * count * tokens * width * ADAPTER_RANK, bytes_accessed=4 * count * tokens * width, transcendentals=0
        ),
        name="finish",
    )(place, block_request, request_adapter, near, flipped, up_weight, *pieces)


def attend_kernel(
    block_len, most_blocks, planes, piece, piece_count,
    place_ref, request_ref, q_ref, low_ref, up_ref, key_ref, value_ref, *rest,
):
    done_ref = rest[0] if piece > 0 else None
    out_ref, query_ref, total_ref, score_ref, top_ref, sum_ref = rest[-6:]
    tokens = q_ref.shape[0]
    per_device = tokens // block_len
    me = place_ref[0]
    within = lax.rem(me, PLANE)
    sources = up_ref.shape[0]
    span = up_ref.shape[3]
    heads = span // HEAD_SIZE
    group = sources * heads
    rows = group * block_len
    offsets = [(source * piece_count + piece) * span for source in range(sources)]
    for part in range(per_device):
        own_rows = pl.ds(part * block_len, block_len)
        for source in range(sources):
            columns = pl.ds(offsets[source], span)
            delta = lax.dot_general(
                low_ref[:, own_rows], up_ref[source, part], TN, preferred_element_type=jnp.float32
            )
            query = (q_ref[own_rows, columns].astype(jnp.float32) + delta).astype(jnp.bfloat16)
            for at in range(heads):
                row = part * rows + (source * heads + at) * block_len
                query_ref[pl.ds(row, block_len), :] = query[:, at * HEAD_SIZE : (at + 1) * HEAD_SIZE]

    first_block = me * per_device
    request = request_ref[first_block]
    count = jnp.int32(1)
    for back in range(1, most_blocks):
        earlier = request_ref[jnp.maximum(first_block - back, 0)]
        count = count + ((first_block >= back) & (earlier == request)).astype(jnp.int32)
    window_first = ((planes - 1) * PLANE + within) * per_device
    end = (window_first + per_device) * block_len
    starts = [(window_first - count + 1) * block_len]
    for part in range(1, per_device):
        same = request_ref[first_block + part] == request_ref[first_block + part - 1]
        starts.append(jnp.where(same, starts[-1], (window_first + part) * block_len))
    all_same = request_ref[first_block + per_device - 1] == request
    chunks = lax.div(end - starts[0] + (KEY_CHUNK - 1), KEY_CHUNK)
    factor = math.log2(math.e) / math.sqrt(HEAD_SIZE)

    def score(step, slot, parts, first, masked):
        stop = end - step * KEY_CHUNK
        start = stop - KEY_CHUNK
        if masked:
            start = jnp.maximum(start, 0)
        start = pl.multiple_of(start, block_len)
        for part in parts:
            columns = pl.ds(part * rows, rows)
            top = None
            for at in range(0, KEY_CHUNK, KEY_STEP):
                keys = key_ref[pl.ds(start + at, KEY_STEP), :]
                scores = lax.dot_general(keys, query_ref[columns, :], NT, preferred_element_type=jnp.float32)
                if masked:
                    key_at = start + at + lax.broadcasted_iota(jnp.int32, (KEY_STEP, 1), 0)
                    allowed = (key_at >= starts[part]) & (key_at < stop)
                    if first and at >= KEY_CHUNK - tokens - KEY_STEP + 1:
                        key_at = start + at + lax.broadcasted_iota(jnp.int32, scores.shape, 0)
                        query_at = (window_first + part) * block_len + lax.rem(
                            lax.broadcasted_iota(jnp.int32, scores.shape, 1), block_len
                        )
                        allowed = allowed & (key_at <= query_at)
                    scores = jnp.where(allowed, scores, -1e30)
                score_ref[slot, pl.ds(at, KEY_STEP), columns] = scores
                high = jnp.max(scores, axis=0, keepdims=True)
                top = high if top is None else jnp.maximum(top, high)
            if first:
                top_ref[slot, :, columns] = top
            else:
                top_ref[slot, :, columns] = jnp.maximum(top, top_ref[1 - slot, :, columns])

    def gather(step, slot, parts, first, masked):
        stop = end - step * KEY_CHUNK
        start = stop - KEY_CHUNK
        if masked:
            start = jnp.maximum(start, 0)
        start = pl.multiple_of(start, block_len)
        for part in parts:
            columns = pl.ds(part * rows, rows)
            top = top_ref[slot, :, columns]
            sums = None
            product = None
            for at in range(0, KEY_CHUNK, KEY_STEP):
                weights = jnp.exp2((score_ref[slot, pl.ds(at, KEY_STEP), columns] - top) * factor)
                more = jnp.sum(weights, axis=0, keepdims=True)
                values = value_ref[pl.ds(start + at, KEY_STEP), :]
                extra = lax.dot_general(
                    values, weights.astype(jnp.bfloat16), TN, preferred_element_type=jnp.float32
                )
                sums = more if sums is None else sums + more
                product = extra if product is None else product + extra
            if not first:
                fade = jnp.exp2((top_ref[1 - slot, :, columns] - top) * factor)
                sums = sums + sum_ref[:, columns] * fade
                product = product + total_ref[:, columns] * fade
            sum_ref[:, columns] = sums
            total_ref[:, columns] = product

    every = list(range(per_device))
    leading = every[: max(1, per_device - 1)]
    score(0, 0, every, True, True)

    @pl.when(chunks == 1)
    def _():
        gather(0, 0, every, True, True)

    @pl.when((chunks > 1) & all_same)
    def _():
        @pl.when(chunks == 2)
        def _():
            for part in every:
                score(1, 1, [part], False, True)
                gather(0, 0, [part], True, True)

        @pl.when(chunks > 2)
        def _():
            for part in every:
                score(1, 1, [part], False, False)
                gather(0, 0, [part], True, True)

            @pl.loop(2, chunks)
            def _(step):
                slot = lax.rem(step, 2)
                for part in every:
                    score(step, slot, [part], False, True)
                    gather(step - 1, 1 - slot, [part], False, False)

        gather(chunks - 1, lax.rem(chunks - 1, 2), every, False, True)

    @pl.when((chunks > 1) & jnp.logical_not(all_same))
    def _():
        gather(0, 0, every, True, True)

        @pl.loop(1, chunks)
        def _(step):
            slot = lax.rem(step, 2)
            score(step, slot, leading, False, True)
            gather(step, slot, leading, False, True)

    for part in every:
        columns = pl.ds(part * rows, rows)
        span_rows = pl.ds(part * block_len, block_len)
        result = (total_ref[:, columns] / sum_ref[:, columns]).T.astype(out_ref.dtype)
        for source in range(sources):
            for at in range(heads):
                row = (source * heads + at) * block_len
                out_ref[span_rows, pl.ds(offsets[source] + at * HEAD_SIZE, HEAD_SIZE)] = result[
                    row : row + block_len
                ]
    for source in range(sources):
        for other in range(piece):
            columns = pl.ds((source * piece_count + other) * span, span)
            out_ref[:, columns] = done_ref[:, columns]


def attend(q_base, low, up_rows, kv, place, block_request, block_len, most_blocks, planes, piece, piece_count, done):
    tokens, width = q_base.shape
    devices, per_device, rank, span = up_rows.shape
    window = kv.shape[0]
    head_span = width // KEY_VALUE_HEADS
    sources = devices // KEY_VALUE_HEADS
    lanes = tokens * sources * span // HEAD_SIZE
    earlier = [] if done is None else [done]
    return pl.pallas_call(
        functools.partial(attend_kernel, block_len, most_blocks, planes, piece, piece_count),
        out_shape=jax.ShapeDtypeStruct((tokens, width), jnp.bfloat16),
        grid_spec=pltpu.PrefetchScalarGridSpec(
            num_scalar_prefetch=2,
            grid=(KEY_VALUE_HEADS,),
            in_specs=[
                pl.BlockSpec((tokens, head_span), lambda m, me, br: (0, m)),
                pl.BlockSpec((rank, tokens), lambda m, me, br: (0, 0)),
                pl.BlockSpec((sources, per_device, rank, span), lambda m, me, br: (m, 0, 0, 0)),
                pl.BlockSpec((window, HEAD_SIZE), lambda m, me, br: (0, m)),
                pl.BlockSpec((window, HEAD_SIZE), lambda m, me, br: (0, KEY_VALUE_HEADS + m)),
            ]
            + [pl.BlockSpec((tokens, head_span), lambda m, me, br: (0, m))] * len(earlier),
            out_specs=pl.BlockSpec((tokens, head_span), lambda m, me, br: (0, m)),
            scratch_shapes=[
                pltpu.VMEM((lanes, HEAD_SIZE), jnp.bfloat16),
                pltpu.VMEM((HEAD_SIZE, lanes), jnp.float32),
                pltpu.VMEM((2, KEY_CHUNK, lanes), jnp.float32),
                pltpu.VMEM((2, 1, lanes), jnp.float32),
                pltpu.VMEM((1, lanes), jnp.float32),
            ],
        ),
        input_output_aliases={7: 0} if earlier else {},
        cost_estimate=pl.CostEstimate(
            flops=2 * tokens * width * window // piece_count,
            bytes_accessed=(16 << 20) // piece_count,
            transcendentals=(8 << 20) // piece_count,
        ),
        name="attend",
    )(place, block_request, q_base, low, up_rows, kv, kv, *earlier)


def body(
    hidden,
    q_base,
    base_key_weight,
    base_value_weight,
    shrink_a,
    expand_q,
    key_value_up_weight,
    block_request,
    request_adapter,
):
    tokens = hidden.shape[0]
    devices = lax.axis_size("seq")
    me = lax.axis_index("seq")
    place = me.astype(jnp.int32).reshape(1)
    block_count = block_request.shape[0]
    block_len = tokens * devices // block_count
    per_device = tokens // block_len
    most_blocks = min(MOST_BLOCKS_CAP, block_count // 2)
    hops = -(-(most_blocks - 1) // (PLANE * per_device))
    planes = hops + 1
    chips = devices // CORES
    same_core = [[chip * CORES + core for chip in range(chips)] for core in range(CORES)]
    forward = [(i, i + PLANE) for i in range(devices - PLANE)]
    swap_row = [(i, i ^ CORES) for i in range(devices)]
    swap_core = [(i, i ^ 1) for i in range(devices)]

    sent, kv = split(hidden, base_key_weight, base_value_weight, chips)
    rows = lax.all_to_all(
        sent, "seq", split_axis=0, concat_axis=0, axis_index_groups=same_core, tiled=True
    )
    down = jnp.swapaxes(shrink_a, 1, 2)
    other_down = lax.ppermute(down, "seq", swap_core)

    pieces = []
    own = kv
    for back in range(planes):
        if back > 0:
            own = lax.ppermute(own, "seq", forward)
        across = lax.ppermute(own, "seq", swap_row)
        flipped = lax.ppermute(own, "seq", swap_core)
        both = lax.ppermute(across, "seq", swap_core)
        pieces += [own, flipped, across, both]

    partials = shrink(rows, down, other_down, place, block_request, request_adapter, block_len)
    received = lax.all_to_all(
        partials, "seq", split_axis=0, concat_axis=0, axis_index_groups=same_core, tiled=True
    )

    piece_count = 1
    span = expand_q.shape[2] // piece_count
    adapter_of = jnp.sum(
        jnp.where(
            block_request[:, None] == jnp.arange(request_adapter.shape[0], dtype=jnp.int32)[None, :],
            request_adapter[None, :],
            0,
        ),
        axis=1,
    )
    up_pieces = []
    for piece in range(piece_count):
        picked = expand_q[:, :, piece * span : (piece + 1) * span][adapter_of]
        picked = picked.reshape(devices, per_device, ADAPTER_RANK, span)
        up_pieces.append(lax.all_to_all(picked, "seq", split_axis=0, concat_axis=0, tiled=True))

    low = jnp.sum(received.astype(jnp.float32), axis=0).astype(jnp.bfloat16)
    low_kv = low[ADAPTER_RANK:]
    near = []
    for back in range(planes):
        for flip in (0, CORES):
            if back == 0 and flip == 0:
                near.append(low_kv)
                continue
            pairs = [(i, (i ^ flip) + back * PLANE) for i in range(devices - back * PLANE)]
            near.append(lax.ppermute(low_kv, "seq", pairs))
    near = jnp.stack(near)
    flipped = lax.ppermute(near, "seq", swap_core)

    window = finish(
        pieces, near, flipped, key_value_up_weight, place, block_request, request_adapter, block_len, planes
    )
    out = None
    for piece in range(piece_count):
        out = attend(
            q_base, low[:ADAPTER_RANK], up_pieces[piece], window, place, block_request,
            block_len, most_blocks, planes, piece, piece_count, out,
        )
    return out


def solution(mesh):
    return jax.shard_map(
        body,
        mesh=mesh,
        in_specs=(
            P(("groups", "seq"), None),
            P(("groups", "seq"), None),
            P(("groups", "seq"), None),
            P(("groups", "seq"), None),
            P("groups", "seq", None),
            P("groups", None, "seq"),
            P("groups", None, None),
            P("groups"),
            P("groups"),
        ),
        out_specs=P(("groups", "seq"), None),
        check_vma=False,
    )
```

profile of v0, /device:TPU:19, one launch (start us, length us, event | category | flops | bytes accessed | tf_op | source)
XLA Modules:
  0.0 236.1 jit_solution(10673768451365307995)
XLA Ops:
  0.0 0.0 copy-start
  0.0 2.8 %split.1 = (bf16[8,128,1024]{2,1,0:T(8,128)(2,1)}, bf16[128,2048]{1,0:T(8,128)(2,1)}) custom-call(bf16[128,8192]{1,0:T(8,128)(2,1)} %hidden_ref.1, bf16[128,1024]{1,0:T(8,128)(2,1)} %key_ref.1, bf16[128,1024]{1,0:T(8,128)(2,1)} %value_ref.1), custom_call_target="tpu_custom_call" | custom-call | tf_op jit(solution)/shard_map/split/pallas_call | solution.py:53
  2.8 5.6 %all-to-all-start = ((bf16[8,128,1024]{2,1,0:T(8,128)(2,1)}), bf16[8,128,1024]{2,1,0:T(8,128)(2,1)S(1)}, u32[]{:S(2)}, u32[]{:S(2)}) async-start(bf16[8,128,1024]{2,1,0:T(8,128)(2,1)} %get-tuple-element.7), calls=%async_computation | async-start | bytes 4194304 | tf_op jit(solution)/shard_map/all_to_all | solution.py:417
  8.4 1.2 collective-permute-start
  9.6 5.6 %collective-permute-done.other_ref = bf16[16,192,512]{2,1,0:T(8,128)(2,1)} collective-permute-done((bf16[16,192,512]{2,1,0:T(8,128)(2,1)}, bf16[16,192,512]{2,1,0:T(8,128)(2,1)}, u32[]{:S(2)}, u32[]{:S(2)}) %collective-permute-start) | collective-permute-done | bytes 3145760 | tf_op jit(solution)/shard_map/ppermute | solution.py:421
  15.3 37.6 %all-to-all-done.rows_ref = bf16[8,128,1024]{2,1,0:T(8,128)(2,1)S(1)} async-done(((bf16[8,128,1024]{2,1,0:T(8,128)(2,1)}), bf16[8,128,1024]{2,1,0:T(8,128)(2,1)S(1)}, u32[]{:S(2)}, u32[]{:S(2)}) %all-to-all-start) | async-done | bytes 2097184 | tf_op jit(solution)/shard_map/all_to_all | solution.py:417
  52.8 0.0 copy-start.1
  52.8 1.3 copy-done.1
  54.1 0.0 copy-start.5
  54.1 0.0 copy-start.6
  54.1 6.8 %shrink.1 = bf16[8,192,128]{2,1,0:T(8,128)(2,1)} custom-call(s32[1]{0:T(128)} %bitcast.place_ref, s32[32]{0:T(128)} %request_ref.5, s32[8]{0:T(128)} %adapter_ref.3, bf16[8,128,1024]{2,1,0:T(8,128)(2,1)} %copy-done.1, bf16[16,192,512]{2,1,0:T(8,128)(2,1)} %bitcast.20, bf16[16,192,512]{2,1,0:T(8,128)(2,1)} %collective-permute-done.other_ref), custom_call_target="tpu_custom_call" | custom-call | flops 402653184 | bytes 8388608 | tf_op jit(solution)/shard_map/shrink/pallas_call | solution.py:97
  60.9 7.6 %all-to-all-start.1 = ((bf16[8,192,128]{2,1,0:T(8,128)(2,1)}), bf16[8,192,128]{2,1,0:T(8,128)(2,1)S(1)}, u32[]{:S(2)}, u32[]{:S(2)}) async-start(bf16[8,192,128]{2,1,0:T(8,128)(2,1)} %shrink.1), calls=%async_computation.1 | async-start | bytes 786432 | tf_op jit(solution)/shard_map/all_to_all | solution.py:434
  68.5 0.0 copy-done.5
  68.5 0.0 copy-done.6
  68.5 0.1 select_reduce_fusion
  68.6 0.0 copy-done
  68.6 2.0 gather_fusion
  70.6 7.7 %all-to-all-done.1 = bf16[8,192,128]{2,1,0:T(8,128)(2,1)S(1)} async-done(((bf16[8,192,128]{2,1,0:T(8,128)(2,1)}), bf16[8,192,128]{2,1,0:T(8,128)(2,1)S(1)}, u32[]{:S(2)}, u32[]{:S(2)}) %all-to-all-start.1) | async-done | bytes 393248 | tf_op jit(solution)/shard_map/all_to_all | solution.py:434
  78.3 6.4 %all-to-all-start.2 = ((bf16[16,2,64,512]{3,2,1,0:T(8,128)(2,1)}), bf16[16,2,64,512]{3,2,1,0:T(8,128)(2,1)S(1)}, u32[]{:S(2)}, u32[]{:S(2)}) async-start(bf16[16,2,64,512]{3,2,1,0:T(8,128)(2,1)} %bitcast.4), calls=%async_computation.2 | async-start | bytes 4194304 | tf_op jit(solution)/shard_map/all_to_all | solution.py:452
  84.7 3.1 %collective-permute-start.10 = (bf16[128,2048]{1,0:T(8,128)(2,1)}, bf16[128,2048]{1,0:T(8,128)(2,1)}, u32[]{:S(2)}, u32[]{:S(2)}) collective-permute-start(bf16[128,2048]{1,0:T(8,128)(2,1)} %get-tuple-element.8.rest_0_), channel_id=1, source_target_pairs={{0,4},{1,5},{2,6},{3,7},{4,8},{5,9},{6,10},{7,11},{8,12},{9,13},{1... | collective-permute-start | bytes 1572872 | tf_op jit(solution)/shard_map/ppermute | solution.py:427
  87.8 54.5 %collective-permute-done.10.rest_4_ = bf16[128,2048]{1,0:T(8,128)(2,1)} collective-permute-done((bf16[128,2048]{1,0:T(8,128)(2,1)}, bf16[128,2048]{1,0:T(8,128)(2,1)}, u32[]{:S(2)}, u32[]{:S(2)}) %collective-permute-start.10) | collective-permute-done | bytes 524320 | tf_op jit(solution)/shard_map/ppermute | solution.py:427
  142.3 1.9 collective-permute-start.14
  144.2 1.3 collective-permute-start.8
  145.4 1.3 collective-permute-start.7
  146.7 0.3 collective-permute-start.12
  147.0 10.0 %collective-permute-done.14.rest_8_ = bf16[128,2048]{1,0:T(8,128)(2,1)} collective-permute-done((bf16[128,2048]{1,0:T(8,128)(2,1)}, bf16[128,2048]{1,0:T(8,128)(2,1)}, u32[]{:S(2)}, u32[]{:S(2)}) %collective-permute-start.14) | collective-permute-done | bytes 524320 | tf_op jit(solution)/shard_map/ppermute | solution.py:427
  157.0 1.2 collective-permute-start.16
  158.2 0.7 reduce_sum.23
  158.8 0.8 slice.11
  159.6 0.3 collective-permute-start.1
  159.9 0.8 bitcast_dynamic-update-slice_fusion.5
  160.6 19.6 %collective-permute-done.1 = bf16[128,128]{1,0:T(8,128)(2,1)S(1)} collective-permute-done((bf16[128,128]{1,0:T(8,128)(2,1)S(1)}, bf16[128,128]{1,0:T(8,128)(2,1)S(1)}, u32[]{:S(2)}, u32[]{:S(2)}) %collective-permute-start.1) | collective-permute-done | bytes 32800 | tf_op jit(solution)/shard_map/ppermute | solution.py:463
  180.2 1.9 collective-permute-start.2
  182.2 2.7 %collective-permute-done.2 = bf16[128,128]{1,0:T(8,128)(2,1)S(1)} collective-permute-done((bf16[128,128]{1,0:T(8,128)(2,1)S(1)}, bf16[128,128]{1,0:T(8,128)(2,1)S(1)}, u32[]{:S(2)}, u32[]{:S(2)}) %collective-permute-start.2) | collective-permute-done | bytes 32800 | tf_op jit(solution)/shard_map/ppermute | solution.py:463
  184.9 2.8 %collective-permute-start.3 = (bf16[128,128]{1,0:T(8,128)(2,1)S(1)}, bf16[128,128]{1,0:T(8,128)(2,1)S(1)}, u32[]{:S(2)}, u32[]{:S(2)}) collective-permute-start(bf16[128,128]{1,0:T(8,128)(2,1)S(1)} %slice.11), channel_id=1, source_target_pairs={{0,6},{1,7},{2,4},{3,5},{4,10},{5,11},{6,8},{7,9},{8,14},{9,15},{1... | collective-permute-start | bytes 98312 | tf_op jit(solution)/shard_map/ppermute | solution.py:463
  187.7 0.0 collective-permute-done.8.rest_2_
  187.7 2.9 %collective-permute-start.11 = (bf16[128,2048]{1,0:T(8,128)(2,1)}, bf16[128,2048]{1,0:T(8,128)(2,1)}, u32[]{:S(2)}, u32[]{:S(2)}) collective-permute-start(bf16[128,2048]{1,0:T(8,128)(2,1)} %collective-permute-done.10.rest_4_), channel_id=1, source_target_pairs={{0,1},{1,0},{2,3},{3,2},{4,5},{5,4},{6,7},{7,6},{8,9},{9,8},{10,11... | collective-permute-start | bytes 1572872 | tf_op jit(solution)/shard_map/ppermute | solution.py:429
  190.7 0.0 collective-permute-done.7.rest_1_
  190.7 1.3 collective-permute-start.4
  192.0 0.0 collective-permute-done.3
  192.0 1.3 collective-permute-start.5
  193.3 0.0 collective-permute-done.12.rest_6_
  193.3 2.5 %collective-permute-start.9 = (bf16[128,2048]{1,0:T(8,128)(2,1)}, bf16[128,2048]{1,0:T(8,128)(2,1)}, u32[]{:S(2)}, u32[]{:S(2)}) collective-permute-start(bf16[128,2048]{1,0:T(8,128)(2,1)} %collective-permute-done.8.rest_2_), channel_id=1, source_target_pairs={{0,1},{1,0},{2,3},{3,2},{4,5},{5,4},{6,7},{7,6},{8,9},{9,8},{10,11... | collective-permute-start | bytes 1572872 | tf_op jit(solution)/shard_map/ppermute | solution.py:430
  195.8 0.0 collective-permute-done.16.rest_10_
  195.8 0.1 collective-permute-start.15
  195.9 0.3 collective-permute-done.4
  196.3 1.2 collective-permute-start.13
  197.4 1.0 collective-permute-done.5
  198.4 3.6 %collective-permute-start.17 = (bf16[128,2048]{1,0:T(8,128)(2,1)}, bf16[128,2048]{1,0:T(8,128)(2,1)}, u32[]{:S(2)}, u32[]{:S(2)}) collective-permute-start(bf16[128,2048]{1,0:T(8,128)(2,1)} %collective-permute-done.16.rest_10_), channel_id=1, source_target_pairs={{0,1},{1,0},{2,3},{3,2},{4,5},{5,4},{6,7},{7,6},{8,9},{9,8},{10,11... | collective-permute-start | bytes 1572872 | tf_op jit(solution)/shard_map/ppermute | solution.py:430
  202.1 0.0 collective-permute-done.11.rest_5_
  202.1 0.1 collective-permute-start.6
  202.2 1.3 slice.10.low_ref
  203.5 0.0 collective-permute-done.9.rest_3_
  203.5 0.0 collective-permute-done.15.rest_9_
  203.5 0.0 collective-permute-done.13.rest_7_
  203.5 0.4 collective-permute-done.17.rest_11_
  203.9 0.1 collective-permute-done.6.flipped_ref
  204.1 0.0 copy-done.3
  204.1 0.7 copy-done.4
  204.8 9.1 %finish.1.key_ref.value_ref = bf16[1536,2048]{1,0:T(8,128)(2,1)} custom-call(s32[1]{0:T(128)} %bitcast.place_ref, s32[32]{0:T(128)} %request_ref.5, s32[8]{0:T(128)} %adapter_ref.3, bf16[6,128,128]{2,1,0:T(8,128)(2,1)} %copy-done.3, bf16[6,128,128]{2,1,0:T(8,128)(2,1)} %copy-done.4, bf16[16,64,2048]{2,1,0:T(8,128)(2,1)} %up_ref.1, ...), custom_call_target="tpu_custom_call" | custom-call | flops 402653184 | bytes 12582912 | tf_op jit(solution)/shard_map/finish/pallas_call | solution.py:163
  213.9 0.0 all-to-all-done.2.up_ref
  213.9 0.0 copy-start.2
  213.9 1.4 copy-done.2
  215.3 20.8 %attend.1 = bf16[128,8192]{1,0:T(8,128)(2,1)} custom-call(s32[1]{0:T(128)} %bitcast.place_ref, s32[32]{0:T(128)} %request_ref.5, bf16[128,8192]{1,0:T(8,128)(2,1)} %q_ref.1, bf16[64,128]{1,0:T(8,128)(2,1)} %slice.10.low_ref, bf16[16,2,64,512]{3,2,1,0:T(8,128)(2,1)} %copy-done.2, bf16[1536,2048]{1,0:T(8,128)(2,1)} %finish.1.key_ref.value_ref, ...), custom_call_target="tpu_custom_call" | custom-call | flops 3221225472 | bytes 16777216 | tf_op jit(solution)/shard_map/attend/pallas_call | solution.py:356
  (9 shorter events, 0.1 us)
Async XLA Ops:
  0.0 68.6 %copy-start = (bf16[16,64,512]{2,1,0:T(8,128)(2,1)S(1)}, bf16[16,64,512]{2,1,0:T(8,128)(2,1)}, u32[]{:S(2)}) copy-start(bf16[16,64,512]{2,1,0:T(8,128)(2,1)} %param.14) | copy-start | bytes 3145732
  2.8 50.1 %all-to-all-start = ((bf16[8,128,1024]{2,1,0:T(8,128)(2,1)}), bf16[8,128,1024]{2,1,0:T(8,128)(2,1)S(1)}, u32[]{:S(2)}, u32[]{:S(2)}) async-start(bf16[8,128,1024]{2,1,0:T(8,128)(2,1)} %get-tuple-element.7), calls=%async_computation | async-start | bytes 4194304 | tf_op jit(solution)/shard_map/all_to_all | solution.py:417
  8.4 6.9 %collective-permute-start = (bf16[16,192,512]{2,1,0:T(8,128)(2,1)}, bf16[16,192,512]{2,1,0:T(8,128)(2,1)}, u32[]{:S(2)}, u32[]{:S(2)}) collective-permute-start(bf16[16,192,512]{2,1,0:T(8,128)(2,1)} %bitcast.19), channel_id=1, source_target_pairs={{0,1},{1,0},{2,3},{3,2},{4,5},{5,4},{6,7},{7,6},{8,9},{9,8},{10,11... | collective-permute-start | bytes 9437192 | tf_op jit(solution)/shard_map/ppermute | solution.py:421
  52.8 1.3 copy-start.1
  54.1 14.4 %copy-start.5 = (s32[32]{0:T(128)S(1)}, s32[32]{0:T(128)}, u32[]{:S(2)}) copy-start(s32[32]{0:T(128)} %request_ref.5) | copy-start | bytes 388
  54.1 14.4 %copy-start.6 = (s32[8]{0:T(128)S(1)}, s32[8]{0:T(128)}, u32[]{:S(2)}) copy-start(s32[8]{0:T(128)} %adapter_ref.3) | copy-start | bytes 100
  60.9 17.4 %all-to-all-start.1 = ((bf16[8,192,128]{2,1,0:T(8,128)(2,1)}), bf16[8,192,128]{2,1,0:T(8,128)(2,1)S(1)}, u32[]{:S(2)}, u32[]{:S(2)}) async-start(bf16[8,192,128]{2,1,0:T(8,128)(2,1)} %shrink.1), calls=%async_computation.1 | async-start | bytes 786432 | tf_op jit(solution)/shard_map/all_to_all | solution.py:434
  78.3 135.5 %all-to-all-start.2 = ((bf16[16,2,64,512]{3,2,1,0:T(8,128)(2,1)}), bf16[16,2,64,512]{3,2,1,0:T(8,128)(2,1)S(1)}, u32[]{:S(2)}, u32[]{:S(2)}) async-start(bf16[16,2,64,512]{3,2,1,0:T(8,128)(2,1)} %bitcast.4), calls=%async_computation.2 | async-start | bytes 4194304 | tf_op jit(solution)/shard_map/all_to_all | solution.py:452
  84.7 57.6 %collective-permute-start.10 = (bf16[128,2048]{1,0:T(8,128)(2,1)}, bf16[128,2048]{1,0:T(8,128)(2,1)}, u32[]{:S(2)}, u32[]{:S(2)}) collective-permute-start(bf16[128,2048]{1,0:T(8,128)(2,1)} %get-tuple-element.8.rest_0_), channel_id=1, source_target_pairs={{0,4},{1,5},{2,6},{3,7},{4,8},{5,9},{6,10},{7,11},{8,12},{9,13},{1... | collective-permute-start | bytes 1572872 | tf_op jit(solution)/shard_map/ppermute | solution.py:427
  142.3 14.7 %collective-permute-start.14 = (bf16[128,2048]{1,0:T(8,128)(2,1)}, bf16[128,2048]{1,0:T(8,128)(2,1)}, u32[]{:S(2)}, u32[]{:S(2)}) collective-permute-start(bf16[128,2048]{1,0:T(8,128)(2,1)} %collective-permute-done.10.rest_4_), channel_id=1, source_target_pairs={{0,4},{1,5},{2,6},{3,7},{4,8},{5,9},{6,10},{7,11},{8,12},{9,13},{1... | collective-permute-start | bytes 1572872 | tf_op jit(solution)/shard_map/ppermute | solution.py:427
  144.2 43.6 %collective-permute-start.8 = (bf16[128,2048]{1,0:T(8,128)(2,1)}, bf16[128,2048]{1,0:T(8,128)(2,1)}, u32[]{:S(2)}, u32[]{:S(2)}) collective-permute-start(bf16[128,2048]{1,0:T(8,128)(2,1)} %get-tuple-element.8.rest_0_), channel_id=1, source_target_pairs={{0,2},{1,3},{2,0},{3,1},{4,6},{5,7},{6,4},{7,5},{8,10},{9,11},{10,... | collective-permute-start | bytes 1572872 | tf_op jit(solution)/shard_map/ppermute | solution.py:428
  145.4 45.2 %collective-permute-start.7 = (bf16[128,2048]{1,0:T(8,128)(2,1)}, bf16[128,2048]{1,0:T(8,128)(2,1)}, u32[]{:S(2)}, u32[]{:S(2)}) collective-permute-start(bf16[128,2048]{1,0:T(8,128)(2,1)} %get-tuple-element.8.rest_0_), channel_id=1, source_target_pairs={{0,1},{1,0},{2,3},{3,2},{4,5},{5,4},{6,7},{7,6},{8,9},{9,8},{10,11... | collective-permute-start | bytes 1572872 | tf_op jit(solution)/shard_map/ppermute | solution.py:429
  146.7 46.6 %collective-permute-start.12 = (bf16[128,2048]{1,0:T(8,128)(2,1)}, bf16[128,2048]{1,0:T(8,128)(2,1)}, u32[]{:S(2)}, u32[]{:S(2)}) collective-permute-start(bf16[128,2048]{1,0:T(8,128)(2,1)} %collective-permute-done.10.rest_4_), channel_id=1, source_target_pairs={{0,2},{1,3},{2,0},{3,1},{4,6},{5,7},{6,4},{7,5},{8,10},{9,11},{10,... | collective-permute-start | bytes 1572872 | tf_op jit(solution)/shard_map/ppermute | solution.py:428
  157.0 38.9 %collective-permute-start.16 = (bf16[128,2048]{1,0:T(8,128)(2,1)}, bf16[128,2048]{1,0:T(8,128)(2,1)}, u32[]{:S(2)}, u32[]{:S(2)}) collective-permute-start(bf16[128,2048]{1,0:T(8,128)(2,1)} %collective-permute-done.14.rest_8_), channel_id=1, source_target_pairs={{0,2},{1,3},{2,0},{3,1},{4,6},{5,7},{6,4},{7,5},{8,10},{9,11},{10,... | collective-permute-start | bytes 1572872 | tf_op jit(solution)/shard_map/ppermute | solution.py:428
  159.6 20.7 %collective-permute-start.1 = (bf16[128,128]{1,0:T(8,128)(2,1)S(1)}, bf16[128,128]{1,0:T(8,128)(2,1)S(1)}, u32[]{:S(2)}, u32[]{:S(2)}) collective-permute-start(bf16[128,128]{1,0:T(8,128)(2,1)S(1)} %slice.11), channel_id=1, source_target_pairs={{0,2},{1,3},{2,0},{3,1},{4,6},{5,7},{6,4},{7,5},{8,10},{9,11},{10,... | collective-permute-start | bytes 98312 | tf_op jit(solution)/shard_map/ppermute | solution.py:463
  180.2 4.6 %collective-permute-start.2 = (bf16[128,128]{1,0:T(8,128)(2,1)S(1)}, bf16[128,128]{1,0:T(8,128)(2,1)S(1)}, u32[]{:S(2)}, u32[]{:S(2)}) collective-permute-start(bf16[128,128]{1,0:T(8,128)(2,1)S(1)} %slice.11), channel_id=1, source_target_pairs={{0,4},{1,5},{2,6},{3,7},{4,8},{5,9},{6,10},{7,11},{8,12},{9,13},{1... | collective-permute-start | bytes 98312 | tf_op jit(solution)/shard_map/ppermute | solution.py:463
  184.9 7.1 %collective-permute-start.3 = (bf16[128,128]{1,0:T(8,128)(2,1)S(1)}, bf16[128,128]{1,0:T(8,128)(2,1)S(1)}, u32[]{:S(2)}, u32[]{:S(2)}) collective-permute-start(bf16[128,128]{1,0:T(8,128)(2,1)S(1)} %slice.11), channel_id=1, source_target_pairs={{0,6},{1,7},{2,4},{3,5},{4,10},{5,11},{6,8},{7,9},{8,14},{9,15},{1... | collective-permute-start | bytes 98312 | tf_op jit(solution)/shard_map/ppermute | solution.py:463
  187.7 14.3 %collective-permute-start.11 = (bf16[128,2048]{1,0:T(8,128)(2,1)}, bf16[128,2048]{1,0:T(8,128)(2,1)}, u32[]{:S(2)}, u32[]{:S(2)}) collective-permute-start(bf16[128,2048]{1,0:T(8,128)(2,1)} %collective-permute-done.10.rest_4_), channel_id=1, source_target_pairs={{0,1},{1,0},{2,3},{3,2},{4,5},{5,4},{6,7},{7,6},{8,9},{9,8},{10,11... | collective-permute-start | bytes 1572872 | tf_op jit(solution)/shard_map/ppermute | solution.py:429
  190.7 5.6 %collective-permute-start.4 = (bf16[128,128]{1,0:T(8,128)(2,1)S(1)}, bf16[128,128]{1,0:T(8,128)(2,1)S(1)}, u32[]{:S(2)}, u32[]{:S(2)}) collective-permute-start(bf16[128,128]{1,0:T(8,128)(2,1)S(1)} %slice.11), channel_id=1, source_target_pairs={{0,8},{1,9},{2,10},{3,11},{4,12},{5,13},{6,14},{7,15},{16,24},{17,... | collective-permute-start | bytes 98312 | tf_op jit(solution)/shard_map/ppermute | solution.py:463
  192.0 6.5 %collective-permute-start.5 = (bf16[128,128]{1,0:T(8,128)(2,1)S(1)}, bf16[128,128]{1,0:T(8,128)(2,1)S(1)}, u32[]{:S(2)}, u32[]{:S(2)}) collective-permute-start(bf16[128,128]{1,0:T(8,128)(2,1)S(1)} %slice.11), channel_id=1, source_target_pairs={{0,10},{1,11},{2,8},{3,9},{4,14},{5,15},{6,12},{7,13},{16,26},{17,... | collective-permute-start | bytes 98312 | tf_op jit(solution)/shard_map/ppermute | solution.py:463
  193.3 10.2 %collective-permute-start.9 = (bf16[128,2048]{1,0:T(8,128)(2,1)}, bf16[128,2048]{1,0:T(8,128)(2,1)}, u32[]{:S(2)}, u32[]{:S(2)}) collective-permute-start(bf16[128,2048]{1,0:T(8,128)(2,1)} %collective-permute-done.8.rest_2_), channel_id=1, source_target_pairs={{0,1},{1,0},{2,3},{3,2},{4,5},{5,4},{6,7},{7,6},{8,9},{9,8},{10,11... | collective-permute-start | bytes 1572872 | tf_op jit(solution)/shard_map/ppermute | solution.py:430
  195.8 7.6 %collective-permute-start.15 = (bf16[128,2048]{1,0:T(8,128)(2,1)}, bf16[128,2048]{1,0:T(8,128)(2,1)}, u32[]{:S(2)}, u32[]{:S(2)}) collective-permute-start(bf16[128,2048]{1,0:T(8,128)(2,1)} %collective-permute-done.14.rest_8_), channel_id=1, source_target_pairs={{0,1},{1,0},{2,3},{3,2},{4,5},{5,4},{6,7},{7,6},{8,9},{9,8},{10,11... | collective-permute-start | bytes 1572872 | tf_op jit(solution)/shard_map/ppermute | solution.py:429
  196.3 7.2 %collective-permute-start.13 = (bf16[128,2048]{1,0:T(8,128)(2,1)}, bf16[128,2048]{1,0:T(8,128)(2,1)}, u32[]{:S(2)}, u32[]{:S(2)}) collective-permute-start(bf16[128,2048]{1,0:T(8,128)(2,1)} %collective-permute-done.12.rest_6_), channel_id=1, source_target_pairs={{0,1},{1,0},{2,3},{3,2},{4,5},{5,4},{6,7},{7,6},{8,9},{9,8},{10,11... | collective-permute-start | bytes 1572872 | tf_op jit(solution)/shard_map/ppermute | solution.py:430
  198.4 5.5 %collective-permute-start.17 = (bf16[128,2048]{1,0:T(8,128)(2,1)}, bf16[128,2048]{1,0:T(8,128)(2,1)}, u32[]{:S(2)}, u32[]{:S(2)}) collective-permute-start(bf16[128,2048]{1,0:T(8,128)(2,1)} %collective-permute-done.16.rest_10_), channel_id=1, source_target_pairs={{0,1},{1,0},{2,3},{3,2},{4,5},{5,4},{6,7},{7,6},{8,9},{9,8},{10,11... | collective-permute-start | bytes 1572872 | tf_op jit(solution)/shard_map/ppermute | solution.py:430
  202.1 2.0 copy-start.3
  202.1 2.0 collective-permute-start.6
  204.1 0.7 copy-start.4
  213.9 1.4 copy-start.2
where the time goes:
time: 237 us; the launch traced here: 236 us
  waiting for transfers between devices  140 us (59%)
  starting transfers between devices  47.8 us (20%)
  Pallas kernels  39.4 us (17%)
  local copies, waits for them, and re-layouts  8.31 us (4%)
    ppermute x2, waiting for transfers between devices, body(): own = lax.ppermute(own, 'seq', forward)  64.5 us
    all_to_all x1, waiting for transfers between devices, body(): lax.all_to_all(sent, 'seq', split_axis=0, concat_axis=0, axis_index_group...  37.6 us
    ppermute x5, waiting for transfers between devices, body(): near.append(lax.ppermute(low_kv, 'seq', pairs))  23.7 us
    pallas_call x1, Pallas kernels, attend(): pl.pallas_call(functools.partial(attend_kernel, block_len, most_blocks, p...  20.8 us
    pallas_call x1, Pallas kernels, finish(): pl.pallas_call(functools.partial(finish_kernel, block_len, planes), out_s...  9.07 us
    all_to_all x1, waiting for transfers between devices, body(): lax.all_to_all(partials, 'seq', split_axis=0, concat_axis=0, axis_index_g...  7.71 us
    all_to_all x1, starting transfers between devices, body(): lax.all_to_all(partials, 'seq', split_axis=0, concat_axis=0, axis_index_g...  7.62 us
    ppermute x5, starting transfers between devices, body(): near.append(lax.ppermute(low_kv, 'seq', pairs))  7.57 us
  transfers between devices with their start and end apart: 21, of which 11 were waited for; matrix products, arithmetic and copies ran while one was open for 2% of the time, Pallas kernels for 4%

commit v1 on v0

--- a/solution.py
+++ b/solution.py
@@ -188,27 +188,27 @@
 
 
 def attend_kernel(
-    block_len, most_blocks, planes, piece, piece_count,
-    place_ref, request_ref, q_ref, low_ref, up_ref, key_ref, value_ref, *rest,
+    block_len, most_blocks, planes,
+    place_ref, request_ref, q_ref, low_ref, *rest,
 ):
-    done_ref = rest[0] if piece > 0 else None
-    out_ref, query_ref, total_ref, score_ref, top_ref, sum_ref = rest[-6:]
+    up_refs = rest[:-8]
+    key_ref, value_ref, out_ref, query_ref, total_ref, score_ref, top_ref, sum_ref = rest[-8:]
     tokens = q_ref.shape[0]
     per_device = tokens // block_len
     me = place_ref[0]
     within = lax.rem(me, PLANE)
-    sources = up_ref.shape[0]
-    span = up_ref.shape[3]
+    sources = len(up_refs)
+    span = up_refs[0].shape[4]
     heads = span // HEAD_SIZE
     group = sources * heads
     rows = group * block_len
-    offsets = [(source * piece_count + piece) * span for source in range(sources)]
+    offsets = [source * span for source in range(sources)]
     for part in range(per_device):
         own_rows = pl.ds(part * block_len, block_len)
         for source in range(sources):
             columns = pl.ds(offsets[source], span)
             delta = lax.dot_general(
-                low_ref[:, own_rows], up_ref[source, part], TN, preferred_element_type=jnp.float32
+                low_ref[:, own_rows], up_refs[source][0, 0, part], TN, preferred_element_type=jnp.float32
             )
             query = (q_ref[own_rows, columns].astype(jnp.float32) + delta).astype(jnp.bfloat16)
             for at in range(heads):
@@ -339,22 +339,26 @@
                 out_ref[span_rows, pl.ds(offsets[source] + at * HEAD_SIZE, HEAD_SIZE)] = result[
                     row : row + block_len
                 ]
-    for source in range(sources):
-        for other in range(piece):
-            columns = pl.ds((source * piece_count + other) * span, span)
-            out_ref[:, columns] = done_ref[:, columns]
-
-
-def attend(q_base, low, up_rows, kv, place, block_request, block_len, most_blocks, planes, piece, piece_count, done):
+
+
+def attend(q_base, low, up_rows, kv, place, block_request, block_len, most_blocks, planes, devices):
     tokens, width = q_base.shape
-    devices, per_device, rank, span = up_rows.shape
+    half, _, per_device, rank, span = up_rows.shape
     window = kv.shape[0]
     head_span = width // KEY_VALUE_HEADS
     sources = devices // KEY_VALUE_HEADS
-    lanes = tokens * sources * span // HEAD_SIZE
-    earlier = [] if done is None else [done]
+    lanes = tokens * head_span // HEAD_SIZE
+
+    def up_spec(source):
+        def index(m, me, br):
+            owner = m * sources + source
+            far = lax.div(owner, half) ^ lax.div(me[0], half)
+            return lax.rem(owner, half) ^ lax.rem(me[0], half), far, 0, 0, 0
+
+        return pl.BlockSpec((1, 1, per_device, rank, span), index)
+
     return pl.pallas_call(
-        functools.partial(attend_kernel, block_len, most_blocks, planes, piece, piece_count),
+        functools.partial(attend_kernel, block_len, most_blocks, planes),
         out_shape=jax.ShapeDtypeStruct((tokens, width), jnp.bfloat16),
         grid_spec=pltpu.PrefetchScalarGridSpec(
             num_scalar_prefetch=2,
@@ -362,11 +366,12 @@
             in_specs=[
                 pl.BlockSpec((tokens, head_span), lambda m, me, br: (0, m)),
                 pl.BlockSpec((rank, tokens), lambda m, me, br: (0, 0)),
-                pl.BlockSpec((sources, per_device, rank, span), lambda m, me, br: (m, 0, 0, 0)),
+            ]
+            + [up_spec(source) for source in range(sources)]
+            + [
                 pl.BlockSpec((window, HEAD_SIZE), lambda m, me, br: (0, m)),
                 pl.BlockSpec((window, HEAD_SIZE), lambda m, me, br: (0, KEY_VALUE_HEADS + m)),
-            ]
-            + [pl.BlockSpec((tokens, head_span), lambda m, me, br: (0, m))] * len(earlier),
+            ],
             out_specs=pl.BlockSpec((tokens, head_span), lambda m, me, br: (0, m)),
             scratch_shapes=[
                 pltpu.VMEM((lanes, HEAD_SIZE), jnp.bfloat16),
@@ -376,14 +381,11 @@
                 pltpu.VMEM((1, lanes), jnp.float32),
             ],
         ),
-        input_output_aliases={7: 0} if earlier else {},
         cost_estimate=pl.CostEstimate(
-            flops=2 * tokens * width * window // piece_count,
-            bytes_accessed=(16 << 20) // piece_count,
-            transcendentals=(8 << 20) // piece_count,
+            flops=2 * tokens * width * window, bytes_accessed=16 << 20, transcendentals=8 << 20
         ),
         name="attend",
-    )(place, block_request, q_base, low, up_rows, kv, kv, *earlier)
+    )(place, block_request, q_base, low, *[up_rows] * sources, kv, kv)
 
 
 def body(
@@ -414,6 +416,15 @@
     swap_core = [(i, i ^ 1) for i in range(devices)]
 
     sent, kv = split(hidden, base_key_weight, base_value_weight, chips)
+    half = devices // 2
+    near_up = expand_q[request_adapter]
+    far_up = lax.ppermute(near_up, "seq", [(i, i ^ half) for i in range(devices)])
+    targets = (me ^ jnp.arange(half, dtype=jnp.int32))[:, None] * per_device
+    wanted = block_request[targets + jnp.arange(per_device, dtype=jnp.int32)[None, :]]
+    picked = jnp.stack([near_up[wanted], far_up[wanted]], axis=1)
+    spread = [picked[0]]
+    for step in range(1, half):
+        spread.append(lax.ppermute(picked[step], "seq", [(i, i ^ step) for i in range(devices)]))
     rows = lax.all_to_all(
         sent, "seq", split_axis=0, concat_axis=0, axis_index_groups=same_core, tiled=True
     )
@@ -434,22 +445,6 @@
     received = lax.all_to_all(
         partials, "seq", split_axis=0, concat_axis=0, axis_index_groups=same_core, tiled=True
     )
-
-    piece_count = 1
-    span = expand_q.shape[2] // piece_count
-    adapter_of = jnp.sum(
-        jnp.where(
-            block_request[:, None] == jnp.arange(request_adapter.shape[0], dtype=jnp.int32)[None, :],
-            request_adapter[None, :],
-            0,
-        ),
-        axis=1,
-    )
-    up_pieces = []
-    for piece in range(piece_count):
-        picked = expand_q[:, :, piece * span : (piece + 1) * span][adapter_of]
-        picked = picked.reshape(devices, per_device, ADAPTER_RANK, span)
-        up_pieces.append(lax.all_to_all(picked, "seq", split_axis=0, concat_axis=0, tiled=True))
 
     low = jnp.sum(received.astype(jnp.float32), axis=0).astype(jnp.bfloat16)
     low_kv = low[ADAPTER_RANK:]
@@ -467,13 +462,10 @@
     window = finish(
         pieces, near, flipped, key_value_up_weight, place, block_request, request_adapter, block_len, planes
     )
-    out = None
-    for piece in range(piece_count):
-        out = attend(
-            q_base, low[:ADAPTER_RANK], up_pieces[piece], window, place, block_request,
-            block_len, most_blocks, planes, piece, piece_count, out,
-        )
-    return out
+    return attend(
+        q_base, low[:ADAPTER_RANK], jnp.stack(spread), window, place, block_request,
+        block_len, most_blocks, planes, devices,
+    )
 
 
 def solution(mesh):

time: 237 us -> 210 us (0.89)
  the two profiles are of different devices: /device:TPU:19 before, /device:TPU:25 now
where the time goes in v1:
time: 210 us; the launch traced here: 209 us
  waiting for transfers between devices  111 us (53%)
  starting transfers between devices  41.2 us (20%)
  Pallas kernels  39.6 us (19%)
  local copies, waits for them, and re-layouts  13.4 us (6%)
  other arithmetic  3.55 us (2%)
    ppermute x1, waiting for transfers between devices, body(): lax.ppermute(near_up, 'seq', [(i, i ^ half) for i in range(devices)])  65.1 us
    ppermute x7, waiting for transfers between devices, body(): lax.ppermute(picked[step], 'seq', [(i, i ^ step) for i in range(devices)])  27.3 us
    pallas_call x1, Pallas kernels, attend(): pl.pallas_call(functools.partial(attend_kernel, block_len, most_blocks, p...  21.1 us
    ppermute x2, waiting for transfers between devices, body(): own = lax.ppermute(own, 'seq', forward)  12.5 us
    pallas_call x1, Pallas kernels, finish(): pl.pallas_call(functools.partial(finish_kernel, block_len, planes), out_s...  9.06 us
    ppermute x3, starting transfers between devices, body(): both = lax.ppermute(across, 'seq', swap_core)  7.54 us
    ppermute x7, starting transfers between devices, body(): lax.ppermute(picked[step], 'seq', [(i, i ^ step) for i in range(devices)])  6.8 us
    pallas_call x1, Pallas kernels, shrink(): pl.pallas_call(functools.partial(shrink_kernel, block_len), out_shape=jax...  6.62 us
  transfers between devices with their start and end apart: 28, of which 8 were waited for; matrix products, arithmetic and copies ran while one was open for 7% of the time, Pallas kernels for 3%

profile of v1, /device:TPU:25, one launch (start us, length us, event | category | flops | bytes accessed | tf_op | source)
XLA Modules:
  0.0 209.4 jit_solution(4259478473865469816)
XLA Ops:
  0.0 2.8 %split.1 = (bf16[8,128,1024]{2,1,0:T(8,128)(2,1)}, bf16[128,2048]{1,0:T(8,128)(2,1)}) custom-call(bf16[128,8192]{1,0:T(8,128)(2,1)} %hidden_ref.1, bf16[128,1024]{1,0:T(8,128)(2,1)} %key_ref.1, bf16[128,1024]{1,0:T(8,128)(2,1)} %value_ref.1), custom_call_target="tpu_custom_call" | custom-call | tf_op jit(solution)/shard_map/split/pallas_call | solution.py:53
  2.8 0.0 copy-start.12
  2.8 0.0 copy-start.1
  2.8 5.5 %all-to-all-start = ((bf16[8,128,1024]{2,1,0:T(8,128)(2,1)}), bf16[8,128,1024]{2,1,0:T(8,128)(2,1)}, u32[]{:S(2)}, u32[]{:S(2)}) async-start(bf16[8,128,1024]{2,1,0:T(8,128)(2,1)} %get-tuple-element.7), calls=%async_computation | async-start | bytes 4194304 | tf_op jit(solution)/shard_map/all_to_all | solution.py:428
  8.3 1.2 collective-permute-start
  9.6 0.6 gather_fusion
  10.1 0.3 collective-permute-start.1
  10.5 0.1 compare_select_fusion.1
  10.6 0.1 reshape.72
  10.7 0.7 gather_fusion.1
  11.3 0.1 gather.16
  11.4 0.1 reshape.80
  11.5 1.6 gather_fusion.2
  13.1 65.1 %collective-permute-done.1 = bf16[8,64,512]{2,1,0:T(8,128)(2,1)S(1)} collective-permute-done((bf16[8,64,512]{2,1,0:T(8,128)(2,1)S(1)}, bf16[8,64,512]{2,1,0:T(8,128)(2,1)S(1)}, u32[]{:S(2)}, u32[]{:S(2)}) %collective-permute-start.1) | collective-permute-done | bytes 524320 | tf_op jit(solution)/shard_map/ppermute | solution.py:421
  78.2 1.6 gather_fusion.3
  79.8 2.8 %fusion.8 = (bf16[2,2,64,512]{3,2,1,0:T(8,128)(2,1)}, bf16[8,2,2,64,512]{4,3,2,1,0:T(8,128)(2,1)S(1)}, bf16[2,2,64,512]{3,2,1,0:T(8,128)(2,1)S(1)}, bf16[2,2,64,...) fusion(bf16[8,1,2,64,512]{4,3,2,1,0:T(8,128)(2,1)} %bitcast.49,, ...), kind=kLoop, calls=%fused_computation.27 | loop fusion | flops 4194303 | bytes 4194304 | tf_op jit(solution)/shard_map/squeeze | solution.py:427
  82.6 0.5 collective-permute-start.2
  83.1 0.4 collective-permute-start.3
  83.4 1.3 collective-permute-start.18
  84.7 1.2 collective-permute-start.16
  85.9 0.0 collective-permute-done.2
  85.9 0.9 collective-permute-start.4
  86.8 4.2 %collective-permute-done.3 = bf16[2,2,64,512]{3,2,1,0:T(8,128)(2,1)S(1)} collective-permute-done((bf16[2,2,64,512]{3,2,1,0:T(8,128)(2,1)S(1)}, bf16[2,2,64,512]{3,2,1,0:T(8,128)(2,1)S(1)}, u32[]{:S(2)}, u32[]{:S(2)}) %collective-permute-start.3) | collective-permute-done | bytes 262176 | tf_op jit(solution)/shard_map/ppermute | solution.py:427
  91.0 1.3 collective-permute-start.15
  92.3 15.6 %collective-permute-done.4 = bf16[2,2,64,512]{3,2,1,0:T(8,128)(2,1)S(1)} collective-permute-done((bf16[2,2,64,512]{3,2,1,0:T(8,128)(2,1)S(1)}, bf16[2,2,64,512]{3,2,1,0:T(8,128)(2,1)S(1)}, u32[]{:S(2)}, u32[]{:S(2)}) %collective-permute-start.4) | collective-permute-done | bytes 262176 | tf_op jit(solution)/shard_map/ppermute | solution.py:427
  108.0 1.9 collective-permute-start.6
  109.8 0.0 all-to-all-done.rows_ref
  109.8 6.6 %shrink.1 = bf16[8,192,128]{2,1,0:T(8,128)(2,1)} custom-call(s32[1]{0:T(128)} %bitcast.place_ref, s32[32]{0:T(128)} %request_ref.5, s32[8]{0:T(128)} %adapter_ref.3, bf16[8,128,1024]{2,1,0:T(8,128)(2,1)} %all-to-all-done.rows_ref, bf16[16,192,512]{2,1,0:T(8,128)(2,1)} %bitcast.51, bf16[16,192,512]{2,1,0:T(8,128)(2,1)} %collective-permute-done.other_ref), custom_call_target="tpu_custom_call" | custom-call | flops 402653184 | bytes 8388608 | tf_op jit(solution)/shard_map/shrink/pallas_call | solution.py:97
  116.5 4.7 %all-to-all-start.1 = ((bf16[8,192,128]{2,1,0:T(8,128)(2,1)}), bf16[8,192,128]{2,1,0:T(8,128)(2,1)S(1)}, u32[]{:S(2)}, u32[]{:S(2)}) async-start(bf16[8,192,128]{2,1,0:T(8,128)(2,1)} %shrink.1), calls=%async_computation.1 | async-start | bytes 786432 | tf_op jit(solution)/shard_map/all_to_all | solution.py:445
  121.1 1.2 collective-permute-start.7
  122.3 1.0 bitcast_dynamic-update-slice_fusion.3
  123.3 2.0 collective-permute-start.8
  125.3 1.3 collective-permute-start.22
  126.6 1.0 bitcast_dynamic-update-slice_fusion.2
  127.6 7.5 %collective-permute-done.7 = bf16[2,2,64,512]{3,2,1,0:T(8,128)(2,1)S(1)} collective-permute-done((bf16[2,2,64,512]{3,2,1,0:T(8,128)(2,1)}, bf16[2,2,64,512]{3,2,1,0:T(8,128)(2,1)S(1)}, u32[]{:S(2)}, u32[]{:S(2)}) %collective-permute-start.7) | collective-permute-done | bytes 262176 | tf_op jit(solution)/shard_map/ppermute | solution.py:427
  135.1 0.7 reduce_sum.12
  135.8 0.8 slice.63
  136.6 0.4 collective-permute-start.9
  136.9 0.8 bitcast_dynamic-update-slice_fusion.12
  137.7 1.1 collective-permute-start.20
  138.8 12.5 %collective-permute-done.22.rest_8_ = bf16[128,2048]{1,0:T(8,128)(2,1)} collective-permute-done((bf16[128,2048]{1,0:T(8,128)(2,1)}, bf16[128,2048]{1,0:T(8,128)(2,1)}, u32[]{:S(2)}, u32[]{:S(2)}) %collective-permute-start.22) | collective-permute-done | bytes 524320 | tf_op jit(solution)/shard_map/ppermute | solution.py:438
  151.2 1.1 collective-permute-start.24
  152.3 1.3 collective-permute-start.10
  153.6 3.6 %collective-permute-done.10 = bf16[128,128]{1,0:T(8,128)(2,1)S(1)} collective-permute-done((bf16[128,128]{1,0:T(8,128)(2,1)S(1)}, bf16[128,128]{1,0:T(8,128)(2,1)S(1)}, u32[]{:S(2)}, u32[]{:S(2)}) %collective-permute-start.10) | collective-permute-done | bytes 32800 | tf_op jit(solution)/shard_map/ppermute | solution.py:458
  157.3 1.3 collective-permute-start.11
  158.6 2.2 %collective-permute-start.19 = (bf16[128,2048]{1,0:T(8,128)(2,1)}, bf16[128,2048]{1,0:T(8,128)(2,1)S(1)}, u32[]{:S(2)}, u32[]{:S(2)}) collective-permute-start(bf16[128,2048]{1,0:T(8,128)(2,1)} %collective-permute-done.18.rest_4_), channel_id=1, source_target_pairs={{0,1},{1,0},{2,3},{3,2},{4,5},{5,4},{6,7},{7,6},{8,9},{9,8},{10,11... | collective-permute-start | bytes 1572872 | tf_op jit(solution)/shard_map/ppermute | solution.py:440
  160.8 1.3 collective-permute-start.12
  162.1 0.9 collective-permute-done.11
  162.9 1.3 collective-permute-start.13
  164.2 3.3 %collective-permute-start.17 = (bf16[128,2048]{1,0:T(8,128)(2,1)}, bf16[128,2048]{1,0:T(8,128)(2,1)S(1)}, u32[]{:S(2)}, u32[]{:S(2)}) collective-permute-start(bf16[128,2048]{1,0:T(8,128)(2,1)} %collective-permute-done.16.rest_2_), channel_id=1, source_target_pairs={{0,1},{1,0},{2,3},{3,2},{4,5},{5,4},{6,7},{7,6},{8,9},{9,8},{10,11... | collective-permute-start | bytes 1572872 | tf_op jit(solution)/shard_map/ppermute | solution.py:441
  167.6 0.1 collective-permute-start.23
  167.7 0.4 collective-permute-start.21
  168.1 1.9 collective-permute-done.13
  170.0 3.8 %collective-permute-start.25 = (bf16[128,2048]{1,0:T(8,128)(2,1)S(1)}, bf16[128,2048]{1,0:T(8,128)(2,1)S(1)}, u32[]{:S(2)}, u32[]{:S(2)}) collective-permute-start(bf16[128,2048]{1,0:T(8,128)(2,1)S(1)} %collective-permute-done.24.rest_10_), channel_id=1, source_target_pairs={{0,1},{1,0},{2,3},{3,2},{4,5},{5,4},{6,7},{7,6},{8,9},{9,8},{10,11... | collective-permute-start | bytes 1572872 | tf_op jit(solution)/shard_map/ppermute | solution.py:441
  173.8 0.1 collective-permute-start.14
  173.9 1.1 bitcast_dynamic-update-slice_fusion.rest_0_.rest_1_
  175.1 1.4 slice.48.low_ref
  176.6 0.7 copy-done.6
  177.3 0.2 copy-done.7
  177.5 0.2 copy-done.8
  177.7 0.8 copy-done.9
  178.5 0.7 copy-done.11
  179.2 9.1 %finish.1.rest_2_.rest_3_ = bf16[1536,2048]{1,0:T(8,128)(2,1)} custom-call(s32[1]{0:T(128)} %bitcast.place_ref, s32[32]{0:T(128)} %request_ref.5, s32[8]{0:T(128)} %adapter_ref.3, bf16[6,128,128]{2,1,0:T(8,128)(2,1)} %copy-done.10, bf16[6,128,128]{2,1,0:T(8,128)(2,1)} %copy-done.11, bf16[16,64,2048]{2,1,0:T(8,128)(2,1)} %up_ref.1, ...), custom_call_target="tpu_custom_call" | custom-call | flops 402653184 | bytes 12582912 | tf_op jit(solution)/shard_map/finish/pallas_call | solution.py:163
  188.2 21.1 %attend.1 = bf16[128,8192]{1,0:T(8,128)(2,1)} custom-call(s32[1]{0:T(128)} %bitcast.place_ref, s32[32]{0:T(128)} %request_ref.5, bf16[128,8192]{1,0:T(8,128)(2,1)} %q_ref.1, bf16[64,128]{1,0:T(8,128)(2,1)} %slice.48.low_ref, bf16[8,2,2,64,512]{4,3,2,1,0:T(8,128)(2,1)} %copy-done.2, bf16[8,2,2,64,512]{4,3,2,1,0:T(8,128)(2,1)} %copy-done.2, ...), custom_call_target="tpu_custom_call" | custom-call | flops 3221225472 | bytes 16777216 | tf_op jit(solution)/shard_map/attend/pallas_call | solution.py:360
  (53 shorter events, 0.2 us)
Async XLA Ops:
  0.0 9.6 %copy-start = (bf16[16,64,512]{2,1,0:T(8,128)(2,1)S(1)}, bf16[16,64,512]{2,1,0:T(8,128)(2,1)}, u32[]{:S(2)}) copy-start(bf16[16,64,512]{2,1,0:T(8,128)(2,1)} %param.14) | copy-start | bytes 3145732
  2.8 6.8 %copy-start.12 = (s32[8]{0:T(128)S(1)}, s32[8]{0:T(128)}, u32[]{:S(2)}) copy-start(s32[8]{0:T(128)} %adapter_ref.3) | copy-start | bytes 100
  2.8 7.9 %copy-start.1 = (s32[32]{0:T(128)S(1)}, s32[32]{0:T(128)}, u32[]{:S(2)}) copy-start(s32[32]{0:T(128)} %request_ref.5) | copy-start | bytes 388
  2.8 107.0 %all-to-all-start = ((bf16[8,128,1024]{2,1,0:T(8,128)(2,1)}), bf16[8,128,1024]{2,1,0:T(8,128)(2,1)}, u32[]{:S(2)}, u32[]{:S(2)}) async-start(bf16[8,128,1024]{2,1,0:T(8,128)(2,1)} %get-tuple-element.7), calls=%async_computation | async-start | bytes 4194304 | tf_op jit(solution)/shard_map/all_to_all | solution.py:428
  8.3 99.7 %collective-permute-start = (bf16[16,192,512]{2,1,0:T(8,128)(2,1)}, bf16[16,192,512]{2,1,0:T(8,128)(2,1)}, u32[]{:S(2)}, u32[]{:S(2)}) collective-permute-start(bf16[16,192,512]{2,1,0:T(8,128)(2,1)} %bitcast.50), channel_id=1, source_target_pairs={{0,1},{1,0},{2,3},{3,2},{4,5},{5,4},{6,7},{7,6},{8,9},{9,8},{10,11... | collective-permute-start | bytes 9437192 | tf_op jit(solution)/shard_map/ppermute | solution.py:432
  10.1 68.1 %collective-permute-start.1 = (bf16[8,64,512]{2,1,0:T(8,128)(2,1)S(1)}, bf16[8,64,512]{2,1,0:T(8,128)(2,1)S(1)}, u32[]{:S(2)}, u32[]{:S(2)}) collective-permute-start(bf16[8,64,512]{2,1,0:T(8,128)(2,1)S(1)} %gather_fusion), channel_id=1, source_target_pairs={{0,8},{1,9},{2,10},{3,11},{4,12},{5,13},{6,14},{7,15},{8,0},{9,1},... | collective-permute-start | bytes 1572872 | tf_op jit(solution)/shard_map/ppermute | solution.py:421
  82.6 3.3 %collective-permute-start.2 = (bf16[2,2,64,512]{3,2,1,0:T(8,128)(2,1)S(1)}, bf16[2,2,64,512]{3,2,1,0:T(8,128)(2,1)S(1)}, u32[]{:S(2)}, u32[]{:S(2)}) collective-permute-start(bf16[2,2,64,512]{3,2,1,0:T(8,128)(2,1)S(1)} %get-tuple-element.11), channel_id=1, source_target_pairs={{0,1},{1,0},{2,3},{3,2},{4,5},{5,4},{6,7},{7,6},{8,9},{9,8},{10,11... | collective-permute-start | bytes 786440 | tf_op jit(solution)/shard_map/ppermute | solution.py:427
  83.1 7.9 %collective-permute-start.3 = (bf16[2,2,64,512]{3,2,1,0:T(8,128)(2,1)S(1)}, bf16[2,2,64,512]{3,2,1,0:T(8,128)(2,1)S(1)}, u32[]{:S(2)}, u32[]{:S(2)}) collective-permute-start(bf16[2,2,64,512]{3,2,1,0:T(8,128)(2,1)S(1)} %get-tuple-element.12), channel_id=1, source_target_pairs={{0,2},{1,3},{2,0},{3,1},{4,6},{5,7},{6,4},{7,5},{8,10},{9,11},{10,... | collective-permute-start | bytes 786440 | tf_op jit(solution)/shard_map/ppermute | solution.py:427
  83.4 39.8 %collective-permute-start.18 = (bf16[128,2048]{1,0:T(8,128)(2,1)}, bf16[128,2048]{1,0:T(8,128)(2,1)}, u32[]{:S(2)}, u32[]{:S(2)}) collective-permute-start(bf16[128,2048]{1,0:T(8,128)(2,1)} %get-tuple-element.8.rest_0_), channel_id=1, source_target_pairs={{0,4},{1,5},{2,6},{3,7},{4,8},{5,9},{6,10},{7,11},{8,12},{9,13},{1... | collective-permute-start | bytes 1572872 | tf_op jit(solution)/shard_map/ppermute | solution.py:438
  84.7 53.0 %collective-permute-start.16 = (bf16[128,2048]{1,0:T(8,128)(2,1)}, bf16[128,2048]{1,0:T(8,128)(2,1)}, u32[]{:S(2)}, u32[]{:S(2)}) collective-permute-start(bf16[128,2048]{1,0:T(8,128)(2,1)} %get-tuple-element.8.rest_0_), channel_id=1, source_target_pairs={{0,2},{1,3},{2,0},{3,1},{4,6},{5,7},{6,4},{7,5},{8,10},{9,11},{10,... | collective-permute-start | bytes 1572872 | tf_op jit(solution)/shard_map/ppermute | solution.py:439
  85.9 22.1 %collective-permute-start.4 = (bf16[2,2,64,512]{3,2,1,0:T(8,128)(2,1)S(1)}, bf16[2,2,64,512]{3,2,1,0:T(8,128)(2,1)S(1)}, u32[]{:S(2)}, u32[]{:S(2)}) collective-permute-start(bf16[2,2,64,512]{3,2,1,0:T(8,128)(2,1)S(1)} %get-tuple-element.13), channel_id=1, source_target_pairs={{0,3},{1,2},{2,1},{3,0},{4,7},{5,6},{6,5},{7,4},{8,11},{9,10},{10,... | collective-permute-start | bytes 786440 | tf_op jit(solution)/shard_map/ppermute | solution.py:427
  91.0 67.6 %collective-permute-start.15 = (bf16[128,2048]{1,0:T(8,128)(2,1)}, bf16[128,2048]{1,0:T(8,128)(2,1)}, u32[]{:S(2)}, u32[]{:S(2)}) collective-permute-start(bf16[128,2048]{1,0:T(8,128)(2,1)} %get-tuple-element.8.rest_0_), channel_id=1, source_target_pairs={{0,1},{1,0},{2,3},{3,2},{4,5},{5,4},{6,7},{7,6},{8,9},{9,8},{10,11... | collective-permute-start | bytes 1572872 | tf_op jit(solution)/shard_map/ppermute | solution.py:440
  108.0 13.2 %collective-permute-start.5 = (bf16[2,2,64,512]{3,2,1,0:T(8,128)(2,1)}, bf16[2,2,64,512]{3,2,1,0:T(8,128)(2,1)}, u32[]{:S(2)}, u32[]{:S(2)}) collective-permute-start(bf16[2,2,64,512]{3,2,1,0:T(8,128)(2,1)} %get-tuple-element.14), channel_id=1, source_target_pairs={{0,4},{1,5},{2,6},{3,7},{4,0},{5,1},{6,2},{7,3},{8,12},{9,13},{10,... | collective-permute-start | bytes 786440 | tf_op jit(solution)/shard_map/ppermute | solution.py:427
  108.0 17.3 %collective-permute-start.6 = (bf16[2,2,64,512]{3,2,1,0:T(8,128)(2,1)}, bf16[2,2,64,512]{3,2,1,0:T(8,128)(2,1)}, u32[]{:S(2)}, u32[]{:S(2)}) collective-permute-start(bf16[2,2,64,512]{3,2,1,0:T(8,128)(2,1)} %get-tuple-element.15), channel_id=1, source_target_pairs={{0,5},{1,4},{2,7},{3,6},{4,1},{5,0},{6,3},{7,2},{8,13},{9,12},{10,... | collective-permute-start | bytes 786440 | tf_op jit(solution)/shard_map/ppermute | solution.py:427
  116.5 18.6 %all-to-all-start.1 = ((bf16[8,192,128]{2,1,0:T(8,128)(2,1)}), bf16[8,192,128]{2,1,0:T(8,128)(2,1)S(1)}, u32[]{:S(2)}, u32[]{:S(2)}) async-start(bf16[8,192,128]{2,1,0:T(8,128)(2,1)} %shrink.1), calls=%async_computation.1 | async-start | bytes 786432 | tf_op jit(solution)/shard_map/all_to_all | solution.py:445
  121.1 14.0 %collective-permute-start.7 = (bf16[2,2,64,512]{3,2,1,0:T(8,128)(2,1)}, bf16[2,2,64,512]{3,2,1,0:T(8,128)(2,1)S(1)}, u32[]{:S(2)}, u32[]{:S(2)}) collective-permute-start(bf16[2,2,64,512]{3,2,1,0:T(8,128)(2,1)} %get-tuple-element.16), channel_id=1, source_target_pairs={{0,6},{1,7},{2,4},{3,5},{4,2},{5,3},{6,0},{7,1},{8,14},{9,15},{10,... | collective-permute-start | bytes 786440 | tf_op jit(solution)/shard_map/ppermute | solution.py:427
  123.3 37.5 %collective-permute-start.8 = (bf16[2,2,64,512]{3,2,1,0:T(8,128)(2,1)}, bf16[2,2,64,512]{3,2,1,0:T(8,128)(2,1)}, u32[]{:S(2)}, u32[]{:S(2)}) collective-permute-start(bf16[2,2,64,512]{3,2,1,0:T(8,128)(2,1)} %get-tuple-element.9), channel_id=1, source_target_pairs={{0,7},{1,6},{2,5},{3,4},{4,3},{5,2},{6,1},{7,0},{8,15},{9,14},{10,... | collective-permute-start | bytes 786440 | tf_op jit(solution)/shard_map/ppermute | solution.py:427
  125.3 25.9 %collective-permute-start.22 = (bf16[128,2048]{1,0:T(8,128)(2,1)}, bf16[128,2048]{1,0:T(8,128)(2,1)}, u32[]{:S(2)}, u32[]{:S(2)}) collective-permute-start(bf16[128,2048]{1,0:T(8,128)(2,1)} %collective-permute-done.18.rest_4_), channel_id=1, source_target_pairs={{0,4},{1,5},{2,6},{3,7},{4,8},{5,9},{6,10},{7,11},{8,12},{9,13},{1... | collective-permute-start | bytes 1572872 | tf_op jit(solution)/shard_map/ppermute | solution.py:438
  136.6 15.8 %collective-permute-start.9 = (bf16[128,128]{1,0:T(8,128)(2,1)S(1)}, bf16[128,128]{1,0:T(8,128)(2,1)S(1)}, u32[]{:S(2)}, u32[]{:S(2)}) collective-permute-start(bf16[128,128]{1,0:T(8,128)(2,1)S(1)} %slice.63), channel_id=1, source_target_pairs={{0,2},{1,3},{2,0},{3,1},{4,6},{5,7},{6,4},{7,5},{8,10},{9,11},{10,... | collective-permute-start | bytes 98312 | tf_op jit(solution)/shard_map/ppermute | solution.py:458
  137.7 26.5 %collective-permute-start.20 = (bf16[128,2048]{1,0:T(8,128)(2,1)}, bf16[128,2048]{1,0:T(8,128)(2,1)S(1)}, u32[]{:S(2)}, u32[]{:S(2)}) collective-permute-start(bf16[128,2048]{1,0:T(8,128)(2,1)} %collective-permute-done.18.rest_4_), channel_id=1, source_target_pairs={{0,2},{1,3},{2,0},{3,1},{4,6},{5,7},{6,4},{7,5},{8,10},{9,11},{10,... | collective-permute-start | bytes 1572872 | tf_op jit(solution)/shard_map/ppermute | solution.py:439
  151.2 16.3 %collective-permute-start.24 = (bf16[128,2048]{1,0:T(8,128)(2,1)}, bf16[128,2048]{1,0:T(8,128)(2,1)S(1)}, u32[]{:S(2)}, u32[]{:S(2)}) collective-permute-start(bf16[128,2048]{1,0:T(8,128)(2,1)} %collective-permute-done.22.rest_8_), channel_id=1, source_target_pairs={{0,2},{1,3},{2,0},{3,1},{4,6},{5,7},{6,4},{7,5},{8,10},{9,11},{10,... | collective-permute-start | bytes 1572872 | tf_op jit(solution)/shard_map/ppermute | solution.py:439
  152.3 4.9 %collective-permute-start.10 = (bf16[128,128]{1,0:T(8,128)(2,1)S(1)}, bf16[128,128]{1,0:T(8,128)(2,1)S(1)}, u32[]{:S(2)}, u32[]{:S(2)}) collective-permute-start(bf16[128,128]{1,0:T(8,128)(2,1)S(1)} %slice.63), channel_id=1, source_target_pairs={{0,4},{1,5},{2,6},{3,7},{4,8},{5,9},{6,10},{7,11},{8,12},{9,13},{1... | collective-permute-start | bytes 98312 | tf_op jit(solution)/shard_map/ppermute | solution.py:458
  157.3 5.7 %collective-permute-start.11 = (bf16[128,128]{1,0:T(8,128)(2,1)S(1)}, bf16[128,128]{1,0:T(8,128)(2,1)S(1)}, u32[]{:S(2)}, u32[]{:S(2)}) collective-permute-start(bf16[128,128]{1,0:T(8,128)(2,1)S(1)} %slice.63), channel_id=1, source_target_pairs={{0,6},{1,7},{2,4},{3,5},{4,10},{5,11},{6,8},{7,9},{8,14},{9,15},{1... | collective-permute-start | bytes 98312 | tf_op jit(solution)/shard_map/ppermute | solution.py:458
  158.6 15.2 %collective-permute-start.19 = (bf16[128,2048]{1,0:T(8,128)(2,1)}, bf16[128,2048]{1,0:T(8,128)(2,1)S(1)}, u32[]{:S(2)}, u32[]{:S(2)}) collective-permute-start(bf16[128,2048]{1,0:T(8,128)(2,1)} %collective-permute-done.18.rest_4_), channel_id=1, source_target_pairs={{0,1},{1,0},{2,3},{3,2},{4,5},{5,4},{6,7},{7,6},{8,9},{9,8},{10,11... | collective-permute-start | bytes 1572872 | tf_op jit(solution)/shard_map/ppermute | solution.py:440
  160.8 6.9 %collective-permute-start.12 = (bf16[128,128]{1,0:T(8,128)(2,1)S(1)}, bf16[128,128]{1,0:T(8,128)(2,1)S(1)}, u32[]{:S(2)}, u32[]{:S(2)}) collective-permute-start(bf16[128,128]{1,0:T(8,128)(2,1)S(1)} %slice.63), channel_id=1, source_target_pairs={{0,8},{1,9},{2,10},{3,11},{4,12},{5,13},{6,14},{7,15},{16,24},{17,... | collective-permute-start | bytes 98312 | tf_op jit(solution)/shard_map/ppermute | solution.py:458
  162.9 7.1 %collective-permute-start.13 = (bf16[128,128]{1,0:T(8,128)(2,1)S(1)}, bf16[128,128]{1,0:T(8,128)(2,1)S(1)}, u32[]{:S(2)}, u32[]{:S(2)}) collective-permute-start(bf16[128,128]{1,0:T(8,128)(2,1)S(1)} %slice.63), channel_id=1, source_target_pairs={{0,10},{1,11},{2,8},{3,9},{4,14},{5,15},{6,12},{7,13},{16,26},{17,... | collective-permute-start | bytes 98312 | tf_op jit(solution)/shard_map/ppermute | solution.py:458
  164.2 10.8 %copy-start.3 = (bf16[128,2048]{1,0:T(8,128)(2,1)}, bf16[128,2048]{1,0:T(8,128)(2,1)S(1)}, u32[]{:S(2)}) copy-start(bf16[128,2048]{1,0:T(8,128)(2,1)S(1)} %collective-permute-done.20.rest_6_) | copy-start | bytes 1572868
  164.2 12.2 %collective-permute-start.17 = (bf16[128,2048]{1,0:T(8,128)(2,1)}, bf16[128,2048]{1,0:T(8,128)(2,1)S(1)}, u32[]{:S(2)}, u32[]{:S(2)}) collective-permute-start(bf16[128,2048]{1,0:T(8,128)(2,1)} %collective-permute-done.16.rest_2_), channel_id=1, source_target_pairs={{0,1},{1,0},{2,3},{3,2},{4,5},{5,4},{6,7},{7,6},{8,9},{9,8},{10,11... | collective-permute-start | bytes 1572872 | tf_op jit(solution)/shard_map/ppermute | solution.py:441
  167.6 8.9 %copy-start.4 = (bf16[128,2048]{1,0:T(8,128)(2,1)}, bf16[128,2048]{1,0:T(8,128)(2,1)S(1)}, u32[]{:S(2)}) copy-start(bf16[128,2048]{1,0:T(8,128)(2,1)S(1)} %collective-permute-done.24.rest_10_) | copy-start | bytes 1572868
  167.6 8.9 %collective-permute-start.23 = (bf16[128,2048]{1,0:T(8,128)(2,1)}, bf16[128,2048]{1,0:T(8,128)(2,1)S(1)}, u32[]{:S(2)}, u32[]{:S(2)}) collective-permute-start(bf16[128,2048]{1,0:T(8,128)(2,1)} %collective-permute-done.22.rest_8_), channel_id=1, source_target_pairs={{0,1},{1,0},{2,3},{3,2},{4,5},{5,4},{6,7},{7,6},{8,9},{9,8},{10,11... | collective-permute-start | bytes 1572872 | tf_op jit(solution)/shard_map/ppermute | solution.py:440
  167.7 8.8 %collective-permute-start.21 = (bf16[128,2048]{1,0:T(8,128)(2,1)S(1)}, bf16[128,2048]{1,0:T(8,128)(2,1)S(1)}, u32[]{:S(2)}, u32[]{:S(2)}) collective-permute-start(bf16[128,2048]{1,0:T(8,128)(2,1)S(1)} %collective-permute-done.20.rest_6_), channel_id=1, source_target_pairs={{0,1},{1,0},{2,3},{3,2},{4,5},{5,4},{6,7},{7,6},{8,9},{9,8},{10,11... | collective-permute-start | bytes 1572872 | tf_op jit(solution)/shard_map/ppermute | solution.py:441
  170.0 6.5 %collective-permute-start.25 = (bf16[128,2048]{1,0:T(8,128)(2,1)S(1)}, bf16[128,2048]{1,0:T(8,128)(2,1)S(1)}, u32[]{:S(2)}, u32[]{:S(2)}) collective-permute-start(bf16[128,2048]{1,0:T(8,128)(2,1)S(1)} %collective-permute-done.24.rest_10_), channel_id=1, source_target_pairs={{0,1},{1,0},{2,3},{3,2},{4,5},{5,4},{6,7},{7,6},{8,9},{9,8},{10,11... | collective-permute-start | bytes 1572872 | tf_op jit(solution)/shard_map/ppermute | solution.py:441
  173.8 4.7 %copy-start.10 = (bf16[6,128,128]{2,1,0:T(8,128)(2,1)}, bf16[6,128,128]{2,1,0:T(8,128)(2,1)S(1)}, u32[]{:S(2)}) copy-start(bf16[6,128,128]{2,1,0:T(8,128)(2,1)S(1)} %bitcast_dynamic-update-slice_fusion.7.near_ref) | copy-start | bytes 589828
  173.8 2.7 %copy-start.5 = (bf16[128,2048]{1,0:T(8,128)(2,1)}, bf16[128,2048]{1,0:T(8,128)(2,1)S(1)}, u32[]{:S(2)}) copy-start(bf16[128,2048]{1,0:T(8,128)(2,1)S(1)} %collective-permute-done.19.rest_5_) | copy-start | bytes 1572868
  173.8 4.6 %collective-permute-start.14 = (bf16[6,128,128]{2,1,0:T(8,128)(2,1)S(1)}, bf16[6,128,128]{2,1,0:T(8,128)(2,1)S(1)}, u32[]{:S(2)}, u32[]{:S(2)}) collective-permute-start(bf16[6,128,128]{2,1,0:T(8,128)(2,1)S(1)} %bitcast_dynamic-update-slice_fusion.7.near_ref), channel_id=1, source_target_pairs={{0,1},{1,0},{2,3},{3,2},{4,5},{5,4},{6,7},{7,6},{8,9},{9,8},{10,11... | collective-permute-start | bytes 589832 | tf_op jit(solution)/shard_map/ppermute | solution.py:460
  175.1 13.2 %copy-start.2 = (bf16[8,2,2,64,512]{4,3,2,1,0:T(8,128)(2,1)}, bf16[8,2,2,64,512]{4,3,2,1,0:T(8,128)(2,1)S(1)}, u32[]{:S(2)}) copy-start(bf16[8,2,2,64,512]{4,3,2,1,0:T(8,128)(2,1)S(1)} %bitcast_dynamic-update-slice_fusion.rest_0_.rest_1_) | copy-start | bytes 6291460
  176.5 0.8 copy-start.6
  176.5 1.0 copy-start.7
  176.5 1.1 copy-start.8
  177.7 0.8 copy-start.9
  178.5 0.7 copy-start.11

commit v2 on v1

--- a/solution.py
+++ b/solution.py
@@ -78,15 +78,27 @@
     first = pl.program_id(0) * sources
     for source in range(sources):
         device = (first + source) * CORES + core
-        for part in range(per_device):
-            adapter = adapter_ref[request_ref[device * per_device + part]]
-            span = pl.ds(part * block_len, block_len)
+        picks = [adapter_ref[request_ref[device * per_device + part]] for part in range(per_device)]
+        shared = picks[0] == picks[-1]
+        for pick in picks[1:-1]:
+            shared = shared & (pick == picks[0])
+
+        def put(adapter, span):
             total = lax.dot_general(
                 own_ref[adapter], rows_ref[source, span, own_columns], NT, preferred_element_type=jnp.float32
             ) + lax.dot_general(
                 other_ref[adapter], rows_ref[source, span, other_columns], NT, preferred_element_type=jnp.float32
             )
             out_ref[source, :, span] = total.astype(out_ref.dtype)
+
+        @pl.when(shared)
+        def _():
+            put(picks[0], pl.ds(0, tokens))
+
+        @pl.when(jnp.logical_not(shared))
+        def _():
+            for part in range(per_device):
+                put(picks[part], pl.ds(part * block_len, block_len))
 
 
 def shrink(rows, own, other, place, block_request, request_adapter, block_len):
@@ -116,6 +128,19 @@
     )(place, block_request, request_adapter, rows, own, other)
 
 
+def join_kernel(*refs):
+    for index, ref in enumerate(refs[:-1]):
+        refs[-1][index] = ref[...]
+
+
+def join(parts):
+    return pl.pallas_call(
+        join_kernel,
+        out_shape=jax.ShapeDtypeStruct((len(parts), *parts[0].shape), parts[0].dtype),
+        name="join",
+    )(*parts)
+
+
 def finish_kernel(block_len, planes, place_ref, request_ref, adapter_ref, near_ref, flipped_ref, up_ref, *rest):
     pieces = planes * PLANE
     piece_refs = rest[:pieces]
@@ -133,11 +158,11 @@
         low_ref = flipped_ref if flip % CORES else near_ref
         low_index = back * (PLANE // CORES) + flip // CORES
         place = within ^ flip
-        device = me - within - back * PLANE + place
         pltpu.make_async_copy(piece_refs[index], base_ref.at[index], in_sems.at[index]).wait()
-        for part in range(per_device):
-            adapter = adapter_ref[request_ref[jnp.maximum(device * per_device + part, 0)]]
-            span = pl.ds(part * block_len, block_len)
+        spans = [(0, tokens)] if index else [(part * block_len, block_len) for part in range(per_device)]
+        for part, (at, length) in enumerate(spans):
+            adapter = adapter_ref[request_ref[me * per_device + part]]
+            span = pl.ds(at, length)
             for which in range(2):
                 columns = pl.ds(which * width, width)
                 delta = lax.dot_general(
@@ -191,14 +216,24 @@
     block_len, most_blocks, planes,
     place_ref, request_ref, q_ref, low_ref, *rest,
 ):
-    up_refs = rest[:-8]
-    key_ref, value_ref, out_ref, query_ref, total_ref, score_ref, top_ref, sum_ref = rest[-8:]
+    key_ref, value_ref = rest[:2]
+    out_ref, up_ref, query_ref, total_ref, score_ref, top_ref, sum_ref, sems = rest[-8:]
+    spread_refs = rest[2:-8]
+    head = pl.program_id(0)
+    half, _, _, _, span = up_ref.shape
+
+    @pl.when(head == 0)
+    def _():
+        for step, ref in enumerate(spread_refs):
+            pltpu.make_async_copy(ref, up_ref.at[step], sems.at[step]).start()
+        for step, ref in enumerate(spread_refs):
+            pltpu.make_async_copy(ref, up_ref.at[step], sems.at[step]).wait()
+
     tokens = q_ref.shape[0]
     per_device = tokens // block_len
     me = place_ref[0]
     within = lax.rem(me, PLANE)
-    sources = len(up_refs)
-    span = up_refs[0].shape[4]
+    sources = q_ref.shape[1] // span
     heads = span // HEAD_SIZE
     group = sources * heads
     rows = group * block_len
@@ -207,8 +242,11 @@
         own_rows = pl.ds(part * block_len, block_len)
         for source in range(sources):
             columns = pl.ds(offsets[source], span)
+            owner = head * sources + source
+            far = lax.div(owner, half) ^ lax.div(me, half)
+            step = lax.rem(owner, half) ^ lax.rem(me, half)
             delta = lax.dot_general(
-                low_ref[:, own_rows], up_refs[source][0, 0, part], TN, preferred_element_type=jnp.float32
+                low_ref[:, own_rows], up_ref[step, far, part], TN, preferred_element_type=jnp.float32
             )
             query = (q_ref[own_rows, columns].astype(jnp.float32) + delta).astype(jnp.bfloat16)
             for at in range(heads):
@@ -341,22 +379,12 @@
                 ]
 
 
-def attend(q_base, low, up_rows, kv, place, block_request, block_len, most_blocks, planes, devices):
+def attend(q_base, low, spread, kv, place, block_request, block_len, most_blocks, planes):
     tokens, width = q_base.shape
-    half, _, per_device, rank, span = up_rows.shape
+    _, _, rank, _ = spread[0].shape
     window = kv.shape[0]
     head_span = width // KEY_VALUE_HEADS
-    sources = devices // KEY_VALUE_HEADS
     lanes = tokens * head_span // HEAD_SIZE
-
-    def up_spec(source):
-        def index(m, me, br):
-            owner = m * sources + source
-            far = lax.div(owner, half) ^ lax.div(me[0], half)
-            return lax.rem(owner, half) ^ lax.rem(me[0], half), far, 0, 0, 0
-
-        return pl.BlockSpec((1, 1, per_device, rank, span), index)
-
     return pl.pallas_call(
         functools.partial(attend_kernel, block_len, most_blocks, planes),
         out_shape=jax.ShapeDtypeStruct((tokens, width), jnp.bfloat16),
@@ -367,25 +395,27 @@
                 pl.BlockSpec((tokens, head_span), lambda m, me, br: (0, m)),
                 pl.BlockSpec((rank, tokens), lambda m, me, br: (0, 0)),
             ]
-            + [up_spec(source) for source in range(sources)]
             + [
                 pl.BlockSpec((window, HEAD_SIZE), lambda m, me, br: (0, m)),
                 pl.BlockSpec((window, HEAD_SIZE), lambda m, me, br: (0, KEY_VALUE_HEADS + m)),
-            ],
+            ]
+            + [pl.BlockSpec(memory_space=pl.ANY)] * len(spread),
             out_specs=pl.BlockSpec((tokens, head_span), lambda m, me, br: (0, m)),
             scratch_shapes=[
+                pltpu.VMEM((len(spread), *spread[0].shape), jnp.bfloat16),
                 pltpu.VMEM((lanes, HEAD_SIZE), jnp.bfloat16),
                 pltpu.VMEM((HEAD_SIZE, lanes), jnp.float32),
                 pltpu.VMEM((2, KEY_CHUNK, lanes), jnp.float32),
                 pltpu.VMEM((2, 1, lanes), jnp.float32),
                 pltpu.VMEM((1, lanes), jnp.float32),
+                pltpu.SemaphoreType.DMA((len(spread),)),
             ],
         ),
         cost_estimate=pl.CostEstimate(
             flops=2 * tokens * width * window, bytes_accessed=16 << 20, transcendentals=8 << 20
         ),
         name="attend",
-    )(place, block_request, q_base, low, *[up_rows] * sources, kv, kv)
+    )(place, block_request, q_base, low, kv, kv, *spread)
 
 
 def body(
@@ -456,15 +486,15 @@
                 continue
             pairs = [(i, (i ^ flip) + back * PLANE) for i in range(devices - back * PLANE)]
             near.append(lax.ppermute(low_kv, "seq", pairs))
-    near = jnp.stack(near)
+    near = join(near)
     flipped = lax.ppermute(near, "seq", swap_core)
 
     window = finish(
         pieces, near, flipped, key_value_up_weight, place, block_request, request_adapter, block_len, planes
     )
     return attend(
-        q_base, low[:ADAPTER_RANK], jnp.stack(spread), window, place, block_request,
-        block_len, most_blocks, planes, devices,
+        q_base, low[:ADAPTER_RANK], spread, window, place, block_request,
+        block_len, most_blocks, planes,
     )
 
 

time: 210 us -> 196 us (0.933)
  the two profiles are of different devices: /device:TPU:25 before, /device:TPU:19 now
where the time goes in v2:
time: 196 us; the launch traced here: 195 us
  waiting for transfers between devices  97.4 us (50%)
  starting transfers between devices  45 us (23%)
  Pallas kernels  42.6 us (22%)
  local copies, waits for them, and re-layouts  8.29 us (4%)
    ppermute x2, waiting for transfers between devices, body(): own = lax.ppermute(own, 'seq', forward)  71.4 us
    ppermute x7, waiting for transfers between devices, body(): lax.ppermute(picked[step], 'seq', [(i, i ^ step) for i in range(devices)])  25.9 us
    pallas_call x1, Pallas kernels, attend(): pl.pallas_call(functools.partial(attend_kernel, block_len, most_blocks, p...  22.5 us
    pallas_call x1, Pallas kernels, finish(): pl.pallas_call(functools.partial(finish_kernel, block_len, planes), out_s...  8.91 us
    ppermute x5, starting transfers between devices, body(): near.append(lax.ppermute(low_kv, 'seq', pairs))  7.98 us
    pallas_call x1, Pallas kernels, shrink(): pl.pallas_call(functools.partial(shrink_kernel, block_len), out_shape=jax...  6.93 us
    ppermute x7, starting transfers between devices, body(): lax.ppermute(picked[step], 'seq', [(i, i ^ step) for i in range(devices)])  6.82 us
    all_to_all x1, starting transfers between devices, body(): lax.all_to_all(sent, 'seq', split_axis=0, concat_axis=0, axis_index_group...  5.62 us
  transfers between devices with their start and end apart: 28, of which 6 were waited for; matrix products, arithmetic and copies ran while one was open for 4% of the time, Pallas kernels for 9%

profile of v2, /device:TPU:19, one launch (start us, length us, event | category | flops | bytes accessed | tf_op | source)
XLA Modules:
  0.0 195.1 jit_solution(9939544211009946738)
XLA Ops:
  0.0 2.8 %split.1 = (bf16[8,128,1024]{2,1,0:T(8,128)(2,1)}, bf16[128,2048]{1,0:T(8,128)(2,1)}) custom-call(bf16[128,8192]{1,0:T(8,128)(2,1)} %hidden_ref.1, bf16[128,1024]{1,0:T(8,128)(2,1)} %key_ref.1, bf16[128,1024]{1,0:T(8,128)(2,1)} %value_ref.1), custom_call_target="tpu_custom_call" | custom-call | tf_op jit(solution)/shard_map/split/pallas_call | solution.py:53
  2.8 0.0 copy-start.17
  2.8 0.0 copy-start.1
  2.8 5.6 %all-to-all-start = ((bf16[8,128,1024]{2,1,0:T(8,128)(2,1)}), bf16[8,128,1024]{2,1,0:T(8,128)(2,1)S(1)}, u32[]{:S(2)}, u32[]{:S(2)}) async-start(bf16[8,128,1024]{2,1,0:T(8,128)(2,1)} %get-tuple-element.7), calls=%async_computation | async-start | bytes 4194304 | tf_op jit(solution)/shard_map/all_to_all | solution.py:458
  8.4 1.2 collective-permute-start
  9.6 3.1 %collective-permute-start.10 = (bf16[128,2048]{1,0:T(8,128)(2,1)}, bf16[128,2048]{1,0:T(8,128)(2,1)}, u32[]{:S(2)}, u32[]{:S(2)}) collective-permute-start(bf16[128,2048]{1,0:T(8,128)(2,1)} %get-tuple-element.8.rest_0_), channel_id=1, source_target_pairs={{0,4},{1,5},{2,6},{3,7},{4,8},{5,9},{6,10},{7,11},{8,12},{9,13},{1... | collective-permute-start | bytes 1572872 | tf_op jit(solution)/shard_map/ppermute | solution.py:468
  12.7 0.3 collective-permute-start.7
  13.1 1.2 collective-permute-start.8
  14.3 1.4 gather_fusion
  15.7 1.0 collective-permute-start.18
  16.7 61.7 %collective-permute-done.10.rest_4_ = bf16[128,2048]{1,0:T(8,128)(2,1)} collective-permute-done((bf16[128,2048]{1,0:T(8,128)(2,1)}, bf16[128,2048]{1,0:T(8,128)(2,1)}, u32[]{:S(2)}, u32[]{:S(2)}) %collective-permute-start.10) | collective-permute-done | bytes 524320 | tf_op jit(solution)/shard_map/ppermute | solution.py:468
  78.4 1.9 collective-permute-start.14
  80.3 0.1 compare_select_fusion.1
  80.4 0.1 reshape.72
  80.5 0.7 gather_fusion.1
  81.2 0.1 gather.16
  81.3 0.0 collective-permute-done.other_ref
  81.3 0.0 all-to-all-done.rows_ref
  81.3 0.0 copy-start.2
  81.3 1.3 copy-done.2
  82.6 6.9 %shrink.1 = bf16[8,192,128]{2,1,0:T(8,128)(2,1)} custom-call(s32[1]{0:T(128)} %bitcast.place_ref, s32[32]{0:T(128)} %request_ref.5, s32[8]{0:T(128)} %adapter_ref.3, bf16[8,128,1024]{2,1,0:T(8,128)(2,1)} %copy-done.2, bf16[16,192,512]{2,1,0:T(8,128)(2,1)} %bitcast.27, bf16[16,192,512]{2,1,0:T(8,128)(2,1)} %collective-permute-done.other_ref), custom_call_target="tpu_custom_call" | custom-call | flops 402653184 | bytes 8388608 | tf_op jit(solution)/shard_map/shrink/pallas_call | solution.py:109
  89.5 4.6 %all-to-all-start.1 = ((bf16[8,192,128]{2,1,0:T(8,128)(2,1)}), bf16[8,192,128]{2,1,0:T(8,128)(2,1)S(1)}, u32[]{:S(2)}, u32[]{:S(2)}) async-start(bf16[8,192,128]{2,1,0:T(8,128)(2,1)} %shrink.1), calls=%async_computation.1 | async-start | bytes 786432 | tf_op jit(solution)/shard_map/all_to_all | solution.py:475
  94.1 0.1 reshape.80
  94.2 1.2 collective-permute-start.12
  95.4 9.7 %collective-permute-done.14.rest_8_ = bf16[128,2048]{1,0:T(8,128)(2,1)} collective-permute-done((bf16[128,2048]{1,0:T(8,128)(2,1)}, bf16[128,2048]{1,0:T(8,128)(2,1)}, u32[]{:S(2)}, u32[]{:S(2)}) %collective-permute-start.14) | collective-permute-done | bytes 524320 | tf_op jit(solution)/shard_map/ppermute | solution.py:468
  105.2 0.4 collective-permute-start.16
  105.6 1.7 gather_fusion.2
  107.2 0.0 collective-permute-done.18
  107.2 1.7 gather_fusion.3
  108.9 1.3 fusion.7
  110.2 0.9 collective-permute-start.19
  111.1 0.0 collective-permute-done.7.rest_1_
  111.1 1.0 collective-permute-start.20
  112.1 0.0 collective-permute-done.8.rest_2_
  112.2 0.4 collective-permute-start.9
  112.5 0.1 reduce_sum.12
  112.6 0.9 collective-permute-start.1
  113.5 14.7 %collective-permute-done.20.rest_4_ = bf16[2,2,64,512]{3,2,1,0:T(8,128)(2,1)S(1)} collective-permute-done((bf16[2,2,64,512]{3,2,1,0:T(8,128)(2,1)}, bf16[2,2,64,512]{3,2,1,0:T(8,128)(2,1)S(1)}, u32[]{:S(2)}, u32[]{:S(2)}) %collective-permute-start.20) | collective-permute-done | bytes 262176 | tf_op jit(solution)/shard_map/ppermute | solution.py:457
  128.3 2.6 %collective-permute-start.2 = (bf16[128,128]{1,0:T(8,128)(2,1)S(1)}, bf16[128,128]{1,0:T(8,128)(2,1)S(1)}, u32[]{:S(2)}, u32[]{:S(2)}) collective-permute-start(bf16[128,128]{1,0:T(8,128)(2,1)S(1)} %slice.49.refs_0_), channel_id=1, source_target_pairs={{0,4},{1,5},{2,6},{3,7},{4,8},{5,9},{6,10},{7,11},{8,12},{9,13},{1... | collective-permute-start | bytes 98312 | tf_op jit(solution)/shard_map/ppermute | solution.py:488
  130.9 1.9 collective-permute-start.3
  132.8 0.0 collective-permute-done.16.rest_10_
  132.8 1.3 collective-permute-start.4
  134.1 0.0 collective-permute-done.1.refs_1_
  134.1 0.0 copy-start.12
  134.1 1.3 collective-permute-start.5
  135.5 2.4 %collective-permute-start.11 = (bf16[128,2048]{1,0:T(8,128)(2,1)}, bf16[128,2048]{1,0:T(8,128)(2,1)S(1)}, u32[]{:S(2)}, u32[]{:S(2)}) collective-permute-start(bf16[128,2048]{1,0:T(8,128)(2,1)} %collective-permute-done.10.rest_4_), channel_id=1, source_target_pairs={{0,1},{1,0},{2,3},{3,2},{4,5},{5,4},{6,7},{7,6},{8,9},{9,8},{10,11... | collective-permute-start | bytes 1572872 | tf_op jit(solution)/shard_map/ppermute | solution.py:470
  137.9 0.0 collective-permute-done.3.refs_3_
  137.9 2.4 %collective-permute-start.13 = (bf16[128,2048]{1,0:T(8,128)(2,1)}, bf16[128,2048]{1,0:T(8,128)(2,1)S(1)}, u32[]{:S(2)}, u32[]{:S(2)}) collective-permute-start(bf16[128,2048]{1,0:T(8,128)(2,1)} %collective-permute-done.12.rest_6_), channel_id=1, source_target_pairs={{0,1},{1,0},{2,3},{3,2},{4,5},{5,4},{6,7},{7,6},{8,9},{9,8},{10,11... | collective-permute-start | bytes 1572872 | tf_op jit(solution)/shard_map/ppermute | solution.py:471
  140.3 0.0 collective-permute-done.4.refs_4_
  140.3 1.7 collective-permute-start.15
  142.0 0.0 collective-permute-done.5.refs_5_
  142.0 2.1 %collective-permute-start.17 = (bf16[128,2048]{1,0:T(8,128)(2,1)}, bf16[128,2048]{1,0:T(8,128)(2,1)}, u32[]{:S(2)}, u32[]{:S(2)}) collective-permute-start(bf16[128,2048]{1,0:T(8,128)(2,1)} %collective-permute-done.16.rest_10_), channel_id=1, source_target_pairs={{0,1},{1,0},{2,3},{3,2},{4,5},{5,4},{6,7},{7,6},{8,9},{9,8},{10,11... | collective-permute-start | bytes 1572872 | tf_op jit(solution)/shard_map/ppermute | solution.py:471
  144.1 1.5 join.1.near_ref
  145.7 0.6 collective-permute-start.6
  146.2 0.5 collective-permute-start.21
  146.8 2.0 %collective-permute-start.23 = (bf16[2,2,64,512]{3,2,1,0:T(8,128)(2,1)}, bf16[2,2,64,512]{3,2,1,0:T(8,128)(2,1)}, u32[]{:S(2)}, u32[]{:S(2)}) collective-permute-start(bf16[2,2,64,512]{3,2,1,0:T(8,128)(2,1)} %get-tuple-element.15), channel_id=1, source_target_pairs={{0,5},{1,4},{2,7},{3,6},{4,1},{5,0},{6,3},{7,2},{8,13},{9,12},{10,... | collective-permute-start | bytes 786440 | tf_op jit(solution)/shard_map/ppermute | solution.py:457
  148.8 0.4 collective-permute-start.24
  149.3 1.9 collective-permute-start.25
  151.2 1.3 slice.48.low_ref
  152.5 8.9 %finish.1.rest_0_.rest_1_ = bf16[1536,2048]{1,0:T(8,128)(2,1)} custom-call(s32[1]{0:T(128)} %bitcast.place_ref, s32[32]{0:T(128)} %request_ref.5, s32[8]{0:T(128)} %adapter_ref.3, bf16[6,128,128]{2,1,0:T(8,128)(2,1)} %join.1.near_ref, bf16[6,128,128]{2,1,0:T(8,128)(2,1)} %collective-permute-done.6.flipped_ref, bf16[16,64,2048]{2,1,0:T(8,128)(2,1)} %up_ref.1, ...), custom_call_target="tpu_custom_call" | custom-call | flops 402653184 | bytes 12582912 | tf_op jit(solution)/shard_map/finish/pallas_call | solution.py:188
  161.5 0.2 collective-permute-done.23.rest_7_
  161.6 4.8 %collective-permute-done.24.rest_8_ = bf16[2,2,64,512]{3,2,1,0:T(8,128)(2,1)} collective-permute-done((bf16[2,2,64,512]{3,2,1,0:T(8,128)(2,1)}, bf16[2,2,64,512]{3,2,1,0:T(8,128)(2,1)}, u32[]{:S(2)}, u32[]{:S(2)}) %collective-permute-start.24) | collective-permute-done | bytes 262176 | tf_op jit(solution)/shard_map/ppermute | solution.py:457
  166.4 6.2 %collective-permute-done.25.rest_9_ = bf16[2,2,64,512]{3,2,1,0:T(8,128)(2,1)} collective-permute-done((bf16[2,2,64,512]{3,2,1,0:T(8,128)(2,1)}, bf16[2,2,64,512]{3,2,1,0:T(8,128)(2,1)}, u32[]{:S(2)}, u32[]{:S(2)}) %collective-permute-start.25) | collective-permute-done | bytes 262176 | tf_op jit(solution)/shard_map/ppermute | solution.py:457
  172.6 22.5 %attend.1 = bf16[128,8192]{1,0:T(8,128)(2,1)} custom-call(s32[1]{0:T(128)} %bitcast.place_ref, s32[32]{0:T(128)} %request_ref.5, bf16[128,8192]{1,0:T(8,128)(2,1)} %q_ref.1, bf16[64,128]{1,0:T(8,128)(2,1)} %slice.48.low_ref, bf16[1536,2048]{1,0:T(8,128)(2,1)} %finish.1.rest_0_.rest_1_, bf16[1536,2048]{1,0:T(8,128)(2,1)} %finish.1.rest_0_.rest_1_, ...), custom_call_target="tpu_custom_call" | custom-call | flops 3221225472 | bytes 16777216 | tf_op jit(solution)/shard_map/attend/pallas_call | solution.py:388
  (51 shorter events, 0.1 us)
Async XLA Ops:
  0.0 14.3 %copy-start = (bf16[16,64,512]{2,1,0:T(8,128)(2,1)S(1)}, bf16[16,64,512]{2,1,0:T(8,128)(2,1)}, u32[]{:S(2)}) copy-start(bf16[16,64,512]{2,1,0:T(8,128)(2,1)} %param.14) | copy-start | bytes 3145732
  2.8 11.5 %copy-start.17 = (s32[8]{0:T(128)S(1)}, s32[8]{0:T(128)}, u32[]{:S(2)}) copy-start(s32[8]{0:T(128)} %adapter_ref.3) | copy-start | bytes 100
  2.8 77.7 %copy-start.1 = (s32[32]{0:T(128)S(1)}, s32[32]{0:T(128)}, u32[]{:S(2)}) copy-start(s32[32]{0:T(128)} %request_ref.5) | copy-start | bytes 388
  2.8 78.5 %all-to-all-start = ((bf16[8,128,1024]{2,1,0:T(8,128)(2,1)}), bf16[8,128,1024]{2,1,0:T(8,128)(2,1)S(1)}, u32[]{:S(2)}, u32[]{:S(2)}) async-start(bf16[8,128,1024]{2,1,0:T(8,128)(2,1)} %get-tuple-element.7), calls=%async_computation | async-start | bytes 4194304 | tf_op jit(solution)/shard_map/all_to_all | solution.py:458
  8.4 72.8 %collective-permute-start = (bf16[16,192,512]{2,1,0:T(8,128)(2,1)}, bf16[16,192,512]{2,1,0:T(8,128)(2,1)}, u32[]{:S(2)}, u32[]{:S(2)}) collective-permute-start(bf16[16,192,512]{2,1,0:T(8,128)(2,1)} %bitcast.26), channel_id=1, source_target_pairs={{0,1},{1,0},{2,3},{3,2},{4,5},{5,4},{6,7},{7,6},{8,9},{9,8},{10,11... | collective-permute-start | bytes 9437192 | tf_op jit(solution)/shard_map/ppermute | solution.py:462
  9.6 68.8 %collective-permute-start.10 = (bf16[128,2048]{1,0:T(8,128)(2,1)}, bf16[128,2048]{1,0:T(8,128)(2,1)}, u32[]{:S(2)}, u32[]{:S(2)}) collective-permute-start(bf16[128,2048]{1,0:T(8,128)(2,1)} %get-tuple-element.8.rest_0_), channel_id=1, source_target_pairs={{0,4},{1,5},{2,6},{3,7},{4,8},{5,9},{6,10},{7,11},{8,12},{9,13},{1... | collective-permute-start | bytes 1572872 | tf_op jit(solution)/shard_map/ppermute | solution.py:468
  12.7 98.4 %collective-permute-start.7 = (bf16[128,2048]{1,0:T(8,128)(2,1)}, bf16[128,2048]{1,0:T(8,128)(2,1)}, u32[]{:S(2)}, u32[]{:S(2)}) collective-permute-start(bf16[128,2048]{1,0:T(8,128)(2,1)} %get-tuple-element.8.rest_0_), channel_id=1, source_target_pairs={{0,1},{1,0},{2,3},{3,2},{4,5},{5,4},{6,7},{7,6},{8,9},{9,8},{10,11... | collective-permute-start | bytes 1572872 | tf_op jit(solution)/shard_map/ppermute | solution.py:470
  13.1 99.1 %collective-permute-start.8 = (bf16[128,2048]{1,0:T(8,128)(2,1)}, bf16[128,2048]{1,0:T(8,128)(2,1)}, u32[]{:S(2)}, u32[]{:S(2)}) collective-permute-start(bf16[128,2048]{1,0:T(8,128)(2,1)} %get-tuple-element.8.rest_0_), channel_id=1, source_target_pairs={{0,2},{1,3},{2,0},{3,1},{4,6},{5,7},{6,4},{7,5},{8,10},{9,11},{10,... | collective-permute-start | bytes 1572872 | tf_op jit(solution)/shard_map/ppermute | solution.py:469
  15.7 91.6 %collective-permute-start.18 = (bf16[8,64,512]{2,1,0:T(8,128)(2,1)}, bf16[8,64,512]{2,1,0:T(8,128)(2,1)}, u32[]{:S(2)}, u32[]{:S(2)}) collective-permute-start(bf16[8,64,512]{2,1,0:T(8,128)(2,1)} %gather_fusion), channel_id=1, source_target_pairs={{0,8},{1,9},{2,10},{3,11},{4,12},{5,13},{6,14},{7,15},{8,0},{9,1},... | collective-permute-start | bytes 1572872 | tf_op jit(solution)/shard_map/ppermute | solution.py:451
  78.4 26.7 %collective-permute-start.14 = (bf16[128,2048]{1,0:T(8,128)(2,1)}, bf16[128,2048]{1,0:T(8,128)(2,1)}, u32[]{:S(2)}, u32[]{:S(2)}) collective-permute-start(bf16[128,2048]{1,0:T(8,128)(2,1)} %collective-permute-done.10.rest_4_), channel_id=1, source_target_pairs={{0,4},{1,5},{2,6},{3,7},{4,8},{5,9},{6,10},{7,11},{8,12},{9,13},{1... | collective-permute-start | bytes 1572872 | tf_op jit(solution)/shard_map/ppermute | solution.py:468
  81.3 1.3 copy-start.2
  89.5 23.0 %all-to-all-start.1 = ((bf16[8,192,128]{2,1,0:T(8,128)(2,1)}), bf16[8,192,128]{2,1,0:T(8,128)(2,1)S(1)}, u32[]{:S(2)}, u32[]{:S(2)}) async-start(bf16[8,192,128]{2,1,0:T(8,128)(2,1)} %shrink.1), calls=%async_computation.1 | async-start | bytes 786432 | tf_op jit(solution)/shard_map/all_to_all | solution.py:475
  94.2 36.6 %collective-permute-start.12 = (bf16[128,2048]{1,0:T(8,128)(2,1)}, bf16[128,2048]{1,0:T(8,128)(2,1)}, u32[]{:S(2)}, u32[]{:S(2)}) collective-permute-start(bf16[128,2048]{1,0:T(8,128)(2,1)} %collective-permute-done.10.rest_4_), channel_id=1, source_target_pairs={{0,2},{1,3},{2,0},{3,1},{4,6},{5,7},{6,4},{7,5},{8,10},{9,11},{10,... | collective-permute-start | bytes 1572872 | tf_op jit(solution)/shard_map/ppermute | solution.py:469
  105.2 27.6 %collective-permute-start.16 = (bf16[128,2048]{1,0:T(8,128)(2,1)}, bf16[128,2048]{1,0:T(8,128)(2,1)}, u32[]{:S(2)}, u32[]{:S(2)}) collective-permute-start(bf16[128,2048]{1,0:T(8,128)(2,1)} %collective-permute-done.14.rest_8_), channel_id=1, source_target_pairs={{0,2},{1,3},{2,0},{3,1},{4,6},{5,7},{6,4},{7,5},{8,10},{9,11},{10,... | collective-permute-start | bytes 1572872 | tf_op jit(solution)/shard_map/ppermute | solution.py:469
  110.2 2.4 %collective-permute-start.19 = (bf16[2,2,64,512]{3,2,1,0:T(8,128)(2,1)}, bf16[2,2,64,512]{3,2,1,0:T(8,128)(2,1)S(1)}, u32[]{:S(2)}, u32[]{:S(2)}) collective-permute-start(bf16[2,2,64,512]{3,2,1,0:T(8,128)(2,1)} %get-tuple-element.11), channel_id=1, source_target_pairs={{0,1},{1,0},{2,3},{3,2},{4,5},{5,4},{6,7},{7,6},{8,9},{9,8},{10,11... | collective-permute-start | bytes 786440 | tf_op jit(solution)/shard_map/ppermute | solution.py:457
  111.1 17.2 %collective-permute-start.20 = (bf16[2,2,64,512]{3,2,1,0:T(8,128)(2,1)}, bf16[2,2,64,512]{3,2,1,0:T(8,128)(2,1)S(1)}, u32[]{:S(2)}, u32[]{:S(2)}) collective-permute-start(bf16[2,2,64,512]{3,2,1,0:T(8,128)(2,1)} %get-tuple-element.12), channel_id=1, source_target_pairs={{0,2},{1,3},{2,0},{3,1},{4,6},{5,7},{6,4},{7,5},{8,10},{9,11},{10,... | collective-permute-start | bytes 786440 | tf_op jit(solution)/shard_map/ppermute | solution.py:457
  112.2 33.5 %collective-permute-start.9 = (bf16[128,2048]{1,0:T(8,128)(2,1)}, bf16[128,2048]{1,0:T(8,128)(2,1)S(1)}, u32[]{:S(2)}, u32[]{:S(2)}) collective-permute-start(bf16[128,2048]{1,0:T(8,128)(2,1)} %collective-permute-done.8.rest_2_), channel_id=1, source_target_pairs={{0,1},{1,0},{2,3},{3,2},{4,5},{5,4},{6,7},{7,6},{8,9},{9,8},{10,11... | collective-permute-start | bytes 1572872 | tf_op jit(solution)/shard_map/ppermute | solution.py:471
  112.6 25.3 %copy-start.10 = (bf16[192,128]{1,0:T(8,128)(2,1)}, bf16[192,128]{1,0:T(8,128)(2,1)S(1)}, u32[]{:S(2)}) copy-start(bf16[192,128]{1,0:T(8,128)(2,1)S(1)} %reduce_sum.12) | copy-start | bytes 147460
  112.6 31.5 %copy-start.11 = (bf16[128,128]{1,0:T(8,128)(2,1)}, bf16[128,128]{1,0:T(8,128)(2,1)S(1)}, u32[]{:S(2)}) copy-start(bf16[128,128]{1,0:T(8,128)(2,1)S(1)} %slice.49.refs_0_) | copy-start | bytes 98308
  112.6 22.8 %copy-start.7 = (bf16[2,2,64,512]{3,2,1,0:T(8,128)(2,1)}, bf16[2,2,64,512]{3,2,1,0:T(8,128)(2,1)S(1)}, u32[]{:S(2)}) copy-start(bf16[2,2,64,512]{3,2,1,0:T(8,128)(2,1)S(1)} %collective-permute-done.19.rest_3_) | copy-start | bytes 786436
  112.6 21.5 %collective-permute-start.1 = (bf16[128,128]{1,0:T(8,128)(2,1)S(1)}, bf16[128,128]{1,0:T(8,128)(2,1)S(1)}, u32[]{:S(2)}, u32[]{:S(2)}) collective-permute-start(bf16[128,128]{1,0:T(8,128)(2,1)S(1)} %slice.49.refs_0_), channel_id=1, source_target_pairs={{0,2},{1,3},{2,0},{3,1},{4,6},{5,7},{6,4},{7,5},{8,10},{9,11},{10,... | collective-permute-start | bytes 98312 | tf_op jit(solution)/shard_map/ppermute | solution.py:488
  128.3 7.2 %copy-start.8 = (bf16[2,2,64,512]{3,2,1,0:T(8,128)(2,1)}, bf16[2,2,64,512]{3,2,1,0:T(8,128)(2,1)S(1)}, u32[]{:S(2)}) copy-start(bf16[2,2,64,512]{3,2,1,0:T(8,128)(2,1)S(1)} %collective-permute-done.20.rest_4_) | copy-start | bytes 786436
  128.3 7.2 %collective-permute-start.2 = (bf16[128,128]{1,0:T(8,128)(2,1)S(1)}, bf16[128,128]{1,0:T(8,128)(2,1)S(1)}, u32[]{:S(2)}, u32[]{:S(2)}) collective-permute-start(bf16[128,128]{1,0:T(8,128)(2,1)S(1)} %slice.49.refs_0_), channel_id=1, source_target_pairs={{0,4},{1,5},{2,6},{3,7},{4,8},{5,9},{6,10},{7,11},{8,12},{9,13},{1... | collective-permute-start | bytes 98312 | tf_op jit(solution)/shard_map/ppermute | solution.py:488
  130.9 7.0 %collective-permute-start.3 = (bf16[128,128]{1,0:T(8,128)(2,1)S(1)}, bf16[128,128]{1,0:T(8,128)(2,1)S(1)}, u32[]{:S(2)}, u32[]{:S(2)}) collective-permute-start(bf16[128,128]{1,0:T(8,128)(2,1)S(1)} %slice.49.refs_0_), channel_id=1, source_target_pairs={{0,6},{1,7},{2,4},{3,5},{4,10},{5,11},{6,8},{7,9},{8,14},{9,15},{1... | collective-permute-start | bytes 98312 | tf_op jit(solution)/shard_map/ppermute | solution.py:488
  132.8 7.5 %collective-permute-start.4 = (bf16[128,128]{1,0:T(8,128)(2,1)S(1)}, bf16[128,128]{1,0:T(8,128)(2,1)S(1)}, u32[]{:S(2)}, u32[]{:S(2)}) collective-permute-start(bf16[128,128]{1,0:T(8,128)(2,1)S(1)} %slice.49.refs_0_), channel_id=1, source_target_pairs={{0,8},{1,9},{2,10},{3,11},{4,12},{5,13},{6,14},{7,15},{16,24},{17,... | collective-permute-start | bytes 98312 | tf_op jit(solution)/shard_map/ppermute | solution.py:488
  134.1 10.0 %copy-start.12 = (bf16[128,128]{1,0:T(8,128)(2,1)}, bf16[128,128]{1,0:T(8,128)(2,1)S(1)}, u32[]{:S(2)}) copy-start(bf16[128,128]{1,0:T(8,128)(2,1)S(1)} %collective-permute-done.1.refs_1_) | copy-start | bytes 98308
  134.1 7.9 %collective-permute-start.5 = (bf16[128,128]{1,0:T(8,128)(2,1)S(1)}, bf16[128,128]{1,0:T(8,128)(2,1)S(1)}, u32[]{:S(2)}, u32[]{:S(2)}) collective-permute-start(bf16[128,128]{1,0:T(8,128)(2,1)S(1)} %slice.49.refs_0_), channel_id=1, source_target_pairs={{0,10},{1,11},{2,8},{3,9},{4,14},{5,15},{6,12},{7,13},{16,26},{17,... | collective-permute-start | bytes 98312 | tf_op jit(solution)/shard_map/ppermute | solution.py:488
  135.5 8.7 %copy-start.13 = (bf16[128,128]{1,0:T(8,128)(2,1)}, bf16[128,128]{1,0:T(8,128)(2,1)S(1)}, u32[]{:S(2)}) copy-start(bf16[128,128]{1,0:T(8,128)(2,1)S(1)} %collective-permute-done.2.refs_2_) | copy-start | bytes 98308
  135.5 10.8 %collective-permute-start.11 = (bf16[128,2048]{1,0:T(8,128)(2,1)}, bf16[128,2048]{1,0:T(8,128)(2,1)S(1)}, u32[]{:S(2)}, u32[]{:S(2)}) collective-permute-start(bf16[128,2048]{1,0:T(8,128)(2,1)} %collective-permute-done.10.rest_4_), channel_id=1, source_target_pairs={{0,1},{1,0},{2,3},{3,2},{4,5},{5,4},{6,7},{7,6},{8,9},{9,8},{10,11... | collective-permute-start | bytes 1572872 | tf_op jit(solution)/shard_map/ppermute | solution.py:470
  137.9 6.2 %copy-start.14 = (bf16[128,128]{1,0:T(8,128)(2,1)}, bf16[128,128]{1,0:T(8,128)(2,1)S(1)}, u32[]{:S(2)}) copy-start(bf16[128,128]{1,0:T(8,128)(2,1)S(1)} %collective-permute-done.3.refs_3_) | copy-start | bytes 98308
  137.9 8.9 %collective-permute-start.13 = (bf16[128,2048]{1,0:T(8,128)(2,1)}, bf16[128,2048]{1,0:T(8,128)(2,1)S(1)}, u32[]{:S(2)}, u32[]{:S(2)}) collective-permute-start(bf16[128,2048]{1,0:T(8,128)(2,1)} %collective-permute-done.12.rest_6_), channel_id=1, source_target_pairs={{0,1},{1,0},{2,3},{3,2},{4,5},{5,4},{6,7},{7,6},{8,9},{9,8},{10,11... | collective-permute-start | bytes 1572872 | tf_op jit(solution)/shard_map/ppermute | solution.py:471
  140.3 3.8 %copy-start.15 = (bf16[128,128]{1,0:T(8,128)(2,1)}, bf16[128,128]{1,0:T(8,128)(2,1)S(1)}, u32[]{:S(2)}) copy-start(bf16[128,128]{1,0:T(8,128)(2,1)S(1)} %collective-permute-done.4.refs_4_) | copy-start | bytes 98308
  140.3 6.5 %collective-permute-start.15 = (bf16[128,2048]{1,0:T(8,128)(2,1)}, bf16[128,2048]{1,0:T(8,128)(2,1)S(1)}, u32[]{:S(2)}, u32[]{:S(2)}) collective-permute-start(bf16[128,2048]{1,0:T(8,128)(2,1)} %collective-permute-done.14.rest_8_), channel_id=1, source_target_pairs={{0,1},{1,0},{2,3},{3,2},{4,5},{5,4},{6,7},{7,6},{8,9},{9,8},{10,11... | collective-permute-start | bytes 1572872 | tf_op jit(solution)/shard_map/ppermute | solution.py:470
  142.0 2.1 %copy-start.16 = (bf16[128,128]{1,0:T(8,128)(2,1)}, bf16[128,128]{1,0:T(8,128)(2,1)S(1)}, u32[]{:S(2)}) copy-start(bf16[128,128]{1,0:T(8,128)(2,1)S(1)} %collective-permute-done.5.refs_5_) | copy-start | bytes 98308
  142.0 6.9 %collective-permute-start.17 = (bf16[128,2048]{1,0:T(8,128)(2,1)}, bf16[128,2048]{1,0:T(8,128)(2,1)}, u32[]{:S(2)}, u32[]{:S(2)}) collective-permute-start(bf16[128,2048]{1,0:T(8,128)(2,1)} %collective-permute-done.16.rest_10_), channel_id=1, source_target_pairs={{0,1},{1,0},{2,3},{3,2},{4,5},{5,4},{6,7},{7,6},{8,9},{9,8},{10,11... | collective-permute-start | bytes 1572872 | tf_op jit(solution)/shard_map/ppermute | solution.py:471
  145.7 6.8 %copy-start.3 = (bf16[128,2048]{1,0:T(8,128)(2,1)}, bf16[128,2048]{1,0:T(8,128)(2,1)S(1)}, u32[]{:S(2)}) copy-start(bf16[128,2048]{1,0:T(8,128)(2,1)S(1)} %collective-permute-done.9.rest_3_) | copy-start | bytes 1572868
  145.7 3.6 %collective-permute-start.6 = (bf16[6,128,128]{2,1,0:T(8,128)(2,1)}, bf16[6,128,128]{2,1,0:T(8,128)(2,1)}, u32[]{:S(2)}, u32[]{:S(2)}) collective-permute-start(bf16[6,128,128]{2,1,0:T(8,128)(2,1)} %join.1.near_ref), channel_id=1, source_target_pairs={{0,1},{1,0},{2,3},{3,2},{4,5},{5,4},{6,7},{7,6},{8,9},{9,8},{10,11... | collective-permute-start | bytes 589832 | tf_op jit(solution)/shard_map/ppermute | solution.py:490
  146.2 6.3 %copy-start.4 = (bf16[128,2048]{1,0:T(8,128)(2,1)}, bf16[128,2048]{1,0:T(8,128)(2,1)S(1)}, u32[]{:S(2)}) copy-start(bf16[128,2048]{1,0:T(8,128)(2,1)S(1)} %collective-permute-done.11.rest_5_) | copy-start | bytes 1572868
  146.2 15.2 %collective-permute-start.21 = (bf16[2,2,64,512]{3,2,1,0:T(8,128)(2,1)}, bf16[2,2,64,512]{3,2,1,0:T(8,128)(2,1)S(1)}, u32[]{:S(2)}, u32[]{:S(2)}) collective-permute-start(bf16[2,2,64,512]{3,2,1,0:T(8,128)(2,1)} %get-tuple-element.13), channel_id=1, source_target_pairs={{0,3},{1,2},{2,1},{3,0},{4,7},{5,6},{6,5},{7,4},{8,11},{9,10},{10,... | collective-permute-start | bytes 786440 | tf_op jit(solution)/shard_map/ppermute | solution.py:457
  146.8 5.7 %copy-start.5 = (bf16[128,2048]{1,0:T(8,128)(2,1)}, bf16[128,2048]{1,0:T(8,128)(2,1)S(1)}, u32[]{:S(2)}) copy-start(bf16[128,2048]{1,0:T(8,128)(2,1)S(1)} %collective-permute-done.13.rest_7_) | copy-start | bytes 1572868
  146.8 14.7 %collective-permute-start.22 = (bf16[2,2,64,512]{3,2,1,0:T(8,128)(2,1)}, bf16[2,2,64,512]{3,2,1,0:T(8,128)(2,1)}, u32[]{:S(2)}, u32[]{:S(2)}) collective-permute-start(bf16[2,2,64,512]{3,2,1,0:T(8,128)(2,1)} %get-tuple-element.14), channel_id=1, source_target_pairs={{0,4},{1,5},{2,6},{3,7},{4,0},{5,1},{6,2},{7,3},{8,12},{9,13},{10,... | collective-permute-start | bytes 786440 | tf_op jit(solution)/shard_map/ppermute | solution.py:457
  146.8 5.7 %copy-start.6 = (bf16[128,2048]{1,0:T(8,128)(2,1)}, bf16[128,2048]{1,0:T(8,128)(2,1)S(1)}, u32[]{:S(2)}) copy-start(bf16[128,2048]{1,0:T(8,128)(2,1)S(1)} %collective-permute-done.15.rest_9_) | copy-start | bytes 1572868
  146.8 14.8 %collective-permute-start.23 = (bf16[2,2,64,512]{3,2,1,0:T(8,128)(2,1)}, bf16[2,2,64,512]{3,2,1,0:T(8,128)(2,1)}, u32[]{:S(2)}, u32[]{:S(2)}) collective-permute-start(bf16[2,2,64,512]{3,2,1,0:T(8,128)(2,1)} %get-tuple-element.15), channel_id=1, source_target_pairs={{0,5},{1,4},{2,7},{3,6},{4,1},{5,0},{6,3},{7,2},{8,13},{9,12},{10,... | collective-permute-start | bytes 786440 | tf_op jit(solution)/shard_map/ppermute | solution.py:457
  148.8 17.6 %collective-permute-start.24 = (bf16[2,2,64,512]{3,2,1,0:T(8,128)(2,1)}, bf16[2,2,64,512]{3,2,1,0:T(8,128)(2,1)}, u32[]{:S(2)}, u32[]{:S(2)}) collective-permute-start(bf16[2,2,64,512]{3,2,1,0:T(8,128)(2,1)} %get-tuple-element.16), channel_id=1, source_target_pairs={{0,6},{1,7},{2,4},{3,5},{4,2},{5,3},{6,0},{7,1},{8,14},{9,15},{10,... | collective-permute-start | bytes 786440 | tf_op jit(solution)/shard_map/ppermute | solution.py:457
  149.3 23.3 %collective-permute-start.25 = (bf16[2,2,64,512]{3,2,1,0:T(8,128)(2,1)}, bf16[2,2,64,512]{3,2,1,0:T(8,128)(2,1)}, u32[]{:S(2)}, u32[]{:S(2)}) collective-permute-start(bf16[2,2,64,512]{3,2,1,0:T(8,128)(2,1)} %get-tuple-element.9), channel_id=1, source_target_pairs={{0,7},{1,6},{2,5},{3,4},{4,3},{5,2},{6,1},{7,0},{8,15},{9,14},{10,... | collective-permute-start | bytes 786440 | tf_op jit(solution)/shard_map/ppermute | solution.py:457
  161.5 11.2 %copy-start.9 = (bf16[2,2,64,512]{3,2,1,0:T(8,128)(2,1)}, bf16[2,2,64,512]{3,2,1,0:T(8,128)(2,1)S(1)}, u32[]{:S(2)}) copy-start(bf16[2,2,64,512]{3,2,1,0:T(8,128)(2,1)S(1)} %collective-permute-done.21.rest_5_) | copy-start | bytes 786436

commit v3 on v0

--- a/solution.py
+++ b/solution.py
@@ -68,44 +68,81 @@
     )(hidden, base_key, base_value)
 
 
-def shrink_kernel(block_len, place_ref, request_ref, adapter_ref, rows_ref, own_ref, other_ref, out_ref):
-    sources, tokens, features = rows_ref.shape
+def shrink_kernel(
+    block_len, place_ref, request_ref, adapter_ref, rows_hbm, own_hbm, other_hbm, out_ref,
+    rows_ref, down_ref, row_sems, down_sems,
+):
+    chips, tokens, features = rows_ref.shape
+    requests = down_ref.shape[1]
     per_device = tokens // block_len
     half = features // CORES
     core = lax.rem(place_ref[0], CORES)
-    own_columns = pl.ds(pl.multiple_of(core * half, half), half)
-    other_columns = pl.ds(pl.multiple_of((1 - core) * half, half), half)
-    first = pl.program_id(0) * sources
-    for source in range(sources):
-        device = (first + source) * CORES + core
-        for part in range(per_device):
-            adapter = adapter_ref[request_ref[device * per_device + part]]
-            span = pl.ds(part * block_len, block_len)
-            total = lax.dot_general(
-                own_ref[adapter], rows_ref[source, span, own_columns], NT, preferred_element_type=jnp.float32
-            ) + lax.dot_general(
-                other_ref[adapter], rows_ref[source, span, other_columns], NT, preferred_element_type=jnp.float32
+    downs = []
+    for request in range(requests):
+        adapter = adapter_ref[request]
+        for which, source in enumerate((own_hbm, other_hbm)):
+            downs.append(
+                pltpu.make_async_copy(
+                    source.at[adapter], down_ref.at[which, request], down_sems.at[which, request]
+                )
             )
-            out_ref[source, :, span] = total.astype(out_ref.dtype)
+    loads = [pltpu.make_async_copy(rows_hbm.at[i], rows_ref.at[i], row_sems.at[i]) for i in range(chips)]
+    loads[0].start()
+    for copy in downs:
+        copy.start()
+    for copy in loads[1:]:
+        copy.start()
+    for copy in downs:
+        copy.wait()
+    columns = [
+        pl.ds(pl.multiple_of(core * half, half), half),
+        pl.ds(pl.multiple_of((1 - core) * half, half), half),
+    ]
+    for chip in range(chips):
+        loads[chip].wait()
+        device = chip * CORES + core
+        picks = [request_ref[device * per_device + part] for part in range(per_device)]
+
+        def put(request, span):
+            total = None
+            for which in range(CORES):
+                term = lax.dot_general(
+                    down_ref[which, request], rows_ref[chip, span, columns[which]], NT,
+                    preferred_element_type=jnp.float32,
+                )
+                total = term if total is None else total + term
+            out_ref[chip, :, span] = total.astype(out_ref.dtype)
+
+        shared = picks[0] == picks[-1]
+
+        @pl.when(shared)
+        def _():
+            put(picks[0], pl.ds(0, tokens))
+
+        @pl.when(jnp.logical_not(shared))
+        def _():
+            for part in range(per_device):
+                put(picks[part], pl.ds(part * block_len, block_len))
 
 
 def shrink(rows, own, other, place, block_request, request_adapter, block_len):
     chips, tokens, features = rows.shape
-    adapters, width, half = own.shape
-    steps = min(2, chips)
-    sources = chips // steps
+    _, width, half = own.shape
+    requests = request_adapter.shape[0]
     return pl.pallas_call(
         functools.partial(shrink_kernel, block_len),
         out_shape=jax.ShapeDtypeStruct((chips, width, tokens), jnp.bfloat16),
         grid_spec=pltpu.PrefetchScalarGridSpec(
             num_scalar_prefetch=3,
-            grid=(steps,),
-            in_specs=[
-                pl.BlockSpec((sources, tokens, features), lambda i, me, br, ra: (i, 0, 0)),
-                pl.BlockSpec((adapters, width, half), lambda i, me, br, ra: (0, 0, 0)),
-                pl.BlockSpec((adapters, width, half), lambda i, me, br, ra: (0, 0, 0)),
+            grid=(1,),
+            in_specs=[pl.BlockSpec(memory_space=pl.ANY)] * 3,
+            out_specs=pl.BlockSpec((chips, width, tokens), lambda i, me, br, ra: (0, 0, 0)),
+            scratch_shapes=[
+                pltpu.VMEM((chips, tokens, features), jnp.bfloat16),
+                pltpu.VMEM((CORES, requests, width, half), jnp.bfloat16),
+                pltpu.SemaphoreType.DMA((chips,)),
+                pltpu.SemaphoreType.DMA((CORES, requests)),
             ],
-            out_specs=pl.BlockSpec((sources, width, tokens), lambda i, me, br, ra: (i, 0, 0)),
         ),
         cost_estimate=pl.CostEstimate(
             flops=2 * chips * tokens * features * width,
@@ -116,8 +153,22 @@
     )(place, block_request, request_adapter, rows, own, other)
 
 
-def finish_kernel(block_len, planes, place_ref, request_ref, adapter_ref, near_ref, flipped_ref, up_ref, *rest):
+def join_kernel(*refs):
+    for index, ref in enumerate(refs[:-1]):
+        refs[-1][index] = ref[...]
+
+
+def join(parts):
+    return pl.pallas_call(
+        join_kernel,
+        out_shape=jax.ShapeDtypeStruct((len(parts), *parts[0].shape), parts[0].dtype),
+        name="join",
+    )(*parts)
+
+
+def finish_kernel(block_len, planes, place_ref, request_ref, adapter_ref, up_ref, *rest):
     pieces = planes * PLANE
+    low_refs, rest = rest[:PLANE], rest[PLANE:]
     piece_refs = rest[:pieces]
     out_ref, base_ref, done_ref, in_sems, out_sems = rest[pieces:]
     tokens = piece_refs[0].shape[0]
@@ -130,18 +181,17 @@
         pltpu.make_async_copy(piece_refs[index], base_ref.at[index], in_sems.at[index]).start()
     for index in range(pieces):
         back, flip = index // PLANE, index % PLANE
-        low_ref = flipped_ref if flip % CORES else near_ref
-        low_index = back * (PLANE // CORES) + flip // CORES
+        low_ref = low_refs[flip]
         place = within ^ flip
-        device = me - within - back * PLANE + place
         pltpu.make_async_copy(piece_refs[index], base_ref.at[index], in_sems.at[index]).wait()
-        for part in range(per_device):
-            adapter = adapter_ref[request_ref[jnp.maximum(device * per_device + part, 0)]]
-            span = pl.ds(part * block_len, block_len)
+        spans = [(0, tokens)] if index else [(part * block_len, block_len) for part in range(per_device)]
+        for part, (at, length) in enumerate(spans):
+            adapter = adapter_ref[request_ref[me * per_device + part]]
+            span = pl.ds(at, length)
             for which in range(2):
                 columns = pl.ds(which * width, width)
                 delta = lax.dot_general(
-                    low_ref[low_index, pl.ds(which * rank, rank), span],
+                    low_ref[back, pl.ds(which * rank, rank), span],
                     up_ref[adapter, :, columns],
                     TN,
                     preferred_element_type=jnp.float32,
@@ -157,7 +207,7 @@
         pltpu.make_async_copy(done_ref.at[index], out_ref.at[pl.ds(0, tokens), :], out_sems.at[index]).wait()
 
 
-def finish(pieces, near, flipped, up_weight, place, block_request, request_adapter, block_len, planes):
+def finish(pieces, lows, up_weight, place, block_request, request_adapter, block_len, planes):
     tokens, width = pieces[0].shape
     count = len(pieces)
     return pl.pallas_call(
@@ -167,10 +217,9 @@
             num_scalar_prefetch=3,
             grid=(1,),
             in_specs=[
-                pl.BlockSpec(near.shape, lambda i, me, br, ra: (0, 0, 0)),
-                pl.BlockSpec(near.shape, lambda i, me, br, ra: (0, 0, 0)),
                 pl.BlockSpec(up_weight.shape, lambda i, me, br, ra: (0, 0, 0)),
             ]
+            + [pl.BlockSpec(lows[0].shape, lambda i, me, br, ra: (0, 0, 0))] * PLANE
             + [pl.BlockSpec(memory_space=pl.ANY)] * count,
             out_specs=pl.BlockSpec(memory_space=pl.ANY),
             scratch_shapes=[
@@ -184,7 +233,7 @@
             flops=2 * count * tokens * width * ADAPTER_RANK, bytes_accessed=4 * count * tokens * width, transcendentals=0
         ),
         name="finish",
-    )(place, block_request, request_adapter, near, flipped, up_weight, *pieces)
+    )(place, block_request, request_adapter, up_weight, *lows, *pieces)
 
 
 def attend_kernel(
@@ -192,7 +241,7 @@
     place_ref, request_ref, q_ref, low_ref, up_ref, key_ref, value_ref, *rest,
 ):
     done_ref = rest[0] if piece > 0 else None
-    out_ref, query_ref, total_ref, score_ref, top_ref, sum_ref = rest[-6:]
+    out_ref, query_ref, total_ref, score_ref, bias_ref, top_ref, sum_ref = rest[-7:]
     tokens = q_ref.shape[0]
     per_device = tokens // block_len
     me = place_ref[0]
@@ -231,29 +280,35 @@
     chunks = lax.div(end - starts[0] + (KEY_CHUNK - 1), KEY_CHUNK)
     factor = math.log2(math.e) / math.sqrt(HEAD_SIZE)
 
+    @pl.when(pl.program_id(0) == 0)
+    def _():
+        key_at = lax.broadcasted_iota(jnp.int32, (tokens, rows), 0)
+        offset = lax.rem(lax.broadcasted_iota(jnp.int32, (tokens, rows), 1), block_len)
+        for part in range(per_device):
+            bound = starts[part] - (end - tokens)
+            allowed = (key_at >= bound) & (key_at <= offset + part * block_len)
+            bias_ref[:, pl.ds(part * rows, rows)] = jnp.where(allowed, 0.0, -1e30)
+
     def score(step, slot, parts, first, masked):
         stop = end - step * KEY_CHUNK
         start = stop - KEY_CHUNK
         if masked:
             start = jnp.maximum(start, 0)
         start = pl.multiple_of(start, block_len)
+        sections = [(0, KEY_CHUNK - tokens), (KEY_CHUNK - tokens, tokens)] if first else [(0, KEY_CHUNK)]
         for part in parts:
             columns = pl.ds(part * rows, rows)
             top = None
-            for at in range(0, KEY_CHUNK, KEY_STEP):
-                keys = key_ref[pl.ds(start + at, KEY_STEP), :]
+            for at, length in sections:
+                keys = key_ref[pl.ds(start + at, length), :]
                 scores = lax.dot_general(keys, query_ref[columns, :], NT, preferred_element_type=jnp.float32)
-                if masked:
-                    key_at = start + at + lax.broadcasted_iota(jnp.int32, (KEY_STEP, 1), 0)
+                if first and at > 0:
+                    scores = scores + bias_ref[:, columns]
+                elif masked:
+                    key_at = start + at + lax.broadcasted_iota(jnp.int32, (length, 1), 0)
                     allowed = (key_at >= starts[part]) & (key_at < stop)
-                    if first and at >= KEY_CHUNK - tokens - KEY_STEP + 1:
-                        key_at = start + at + lax.broadcasted_iota(jnp.int32, scores.shape, 0)
-                        query_at = (window_first + part) * block_len + lax.rem(
-                            lax.broadcasted_iota(jnp.int32, scores.shape, 1), block_len
-                        )
-                        allowed = allowed & (key_at <= query_at)
                     scores = jnp.where(allowed, scores, -1e30)
-                score_ref[slot, pl.ds(at, KEY_STEP), columns] = scores
+                score_ref[slot, pl.ds(at, length), columns] = scores
                 high = jnp.max(scores, axis=0, keepdims=True)
                 top = high if top is None else jnp.maximum(top, high)
             if first:
@@ -372,6 +427,7 @@
                 pltpu.VMEM((lanes, HEAD_SIZE), jnp.bfloat16),
                 pltpu.VMEM((HEAD_SIZE, lanes), jnp.float32),
                 pltpu.VMEM((2, KEY_CHUNK, lanes), jnp.float32),
+                pltpu.VMEM((tokens, lanes), jnp.float32),
                 pltpu.VMEM((2, 1, lanes), jnp.float32),
                 pltpu.VMEM((1, lanes), jnp.float32),
             ],
@@ -452,20 +508,18 @@
         up_pieces.append(lax.all_to_all(picked, "seq", split_axis=0, concat_axis=0, tiled=True))
 
     low = jnp.sum(received.astype(jnp.float32), axis=0).astype(jnp.bfloat16)
-    low_kv = low[ADAPTER_RANK:]
-    near = []
-    for back in range(planes):
-        for flip in (0, CORES):
-            if back == 0 and flip == 0:
-                near.append(low_kv)
-                continue
-            pairs = [(i, (i ^ flip) + back * PLANE) for i in range(devices - back * PLANE)]
-            near.append(lax.ppermute(low_kv, "seq", pairs))
-    near = jnp.stack(near)
-    flipped = lax.ppermute(near, "seq", swap_core)
+    column = [low[ADAPTER_RANK:]]
+    for back in range(1, planes):
+        pairs = [(i, i + back * PLANE) for i in range(devices - back * PLANE)]
+        column.append(lax.ppermute(column[0], "seq", pairs))
+    column = join(column)
+    across = lax.ppermute(column, "seq", swap_row)
+    column_flipped = lax.ppermute(column, "seq", swap_core)
+    across_flipped = lax.ppermute(across, "seq", swap_core)
+    lows = [column, column_flipped, across, across_flipped]
 
     window = finish(
-        pieces, near, flipped, key_value_up_weight, place, block_request, request_adapter, block_len, planes
+        pieces, lows, key_value_up_weight, place, block_request, request_adapter, block_len, planes
     )
     out = None
     for piece in range(piece_count):

time: 237 us -> 224 us (0.945)
  the two profiles are of different devices: /device:TPU:19 before, /device:TPU:15 now
where the time goes in v3:
time: 224 us
  waiting for transfers between devices  129 us (58%)
  starting transfers between devices  44.7 us (20%)
  Pallas kernels  40.3 us (18%)
  local copies, waits for them, and re-layouts  8.22 us (4%)
    ppermute x2, waiting for transfers between devices, body(): own = lax.ppermute(own, 'seq', forward)  61 us
    all_to_all x1, waiting for transfers between devices, body(): lax.all_to_all(sent, 'seq', split_axis=0, concat_axis=0, axis_index_group...  38.8 us
    pallas_call x1, Pallas kernels, attend(): pl.pallas_call(functools.partial(attend_kernel, block_len, most_blocks, p...  20.6 us
    ppermute x3, waiting for transfers between devices, body(): across = lax.ppermute(own, 'seq', swap_row)  13.8 us
    pallas_call x1, Pallas kernels, finish(): pl.pallas_call(functools.partial(finish_kernel, block_len, planes), out_s...  8.94 us
    ppermute x2, starting transfers between devices, body(): own = lax.ppermute(own, 'seq', forward)  7.18 us
    all_to_all x1, starting transfers between devices, body(): lax.all_to_all(picked, 'seq', split_axis=0, concat_axis=0, tiled=True)  7.11 us
    all_to_all x1, waiting for transfers between devices, body(): lax.all_to_all(partials, 'seq', split_axis=0, concat_axis=0, axis_index_g...  6.95 us
  transfers between devices with their start and end apart: 20, of which 8 were waited for; matrix products, arithmetic and copies ran while one was open for 2% of the time, Pallas kernels for 5%

profile of v3, /device:TPU:15, one launch (start us, length us, event | category | flops | bytes accessed | tf_op | source)
XLA Modules:
  0.0 223.6 jit_solution(5765889220585925302)
XLA Ops:
  0.0 0.0 copy-start
  0.0 2.8 %split.1 = (bf16[8,128,1024]{2,1,0:T(8,128)(2,1)}, bf16[128,2048]{1,0:T(8,128)(2,1)}) custom-call(bf16[128,8192]{1,0:T(8,128)(2,1)} %hidden_ref.1, bf16[128,1024]{1,0:T(8,128)(2,1)} %key_ref.1, bf16[128,1024]{1,0:T(8,128)(2,1)} %value_ref.1), custom_call_target="tpu_custom_call" | custom-call | tf_op jit(solution)/shard_map/split/pallas_call | solution.py:53
  2.8 5.7 %all-to-all-start = ((bf16[8,128,1024]{2,1,0:T(8,128)(2,1)}), bf16[8,128,1024]{2,1,0:T(8,128)(2,1)S(1)}, u32[]{:S(2)}, u32[]{:S(2)}) async-start(bf16[8,128,1024]{2,1,0:T(8,128)(2,1)} %get-tuple-element.7), calls=%async_computation | async-start | bytes 4194304 | tf_op jit(solution)/shard_map/all_to_all | solution.py:473
  8.4 1.2 collective-permute-start
  9.7 5.6 %collective-permute-done.other_hbm = bf16[16,192,512]{2,1,0:T(8,128)(2,1)} collective-permute-done((bf16[16,192,512]{2,1,0:T(8,128)(2,1)}, bf16[16,192,512]{2,1,0:T(8,128)(2,1)}, u32[]{:S(2)}, u32[]{:S(2)}) %collective-permute-start) | collective-permute-done | bytes 3145760 | tf_op jit(solution)/shard_map/ppermute | solution.py:477
  15.3 38.8 %all-to-all-done.rows_hbm = bf16[8,128,1024]{2,1,0:T(8,128)(2,1)S(1)} async-done(((bf16[8,128,1024]{2,1,0:T(8,128)(2,1)}), bf16[8,128,1024]{2,1,0:T(8,128)(2,1)S(1)}, u32[]{:S(2)}, u32[]{:S(2)}) %all-to-all-start) | async-done | bytes 2097184 | tf_op jit(solution)/shard_map/all_to_all | solution.py:473
  54.2 1.3 copy-done.1
  55.5 6.6 %shrink.1 = bf16[8,192,128]{2,1,0:T(8,128)(2,1)} custom-call(s32[1]{0:T(128)} %bitcast.place_ref, s32[32]{0:T(128)} %request_ref.5, s32[8]{0:T(128)} %adapter_ref.3, bf16[8,128,1024]{2,1,0:T(8,128)(2,1)} %copy-done.1, bf16[16,192,512]{2,1,0:T(8,128)(2,1)} %bitcast.8, bf16[16,192,512]{2,1,0:T(8,128)(2,1)} %collective-permute-done.other_hbm), custom_call_target="tpu_custom_call" | custom-call | flops 402653184 | bytes 8388608 | tf_op jit(solution)/shard_map/shrink/pallas_call | solution.py:132
  62.0 6.4 %all-to-all-start.1 = ((bf16[8,192,128]{2,1,0:T(8,128)(2,1)}), bf16[8,192,128]{2,1,0:T(8,128)(2,1)S(1)}, u32[]{:S(2)}, u32[]{:S(2)}) async-start(bf16[8,192,128]{2,1,0:T(8,128)(2,1)} %shrink.1), calls=%async_computation.1 | async-start | bytes 786432 | tf_op jit(solution)/shard_map/all_to_all | solution.py:490
  68.4 0.0 copy-done.9
  68.4 0.0 copy-done.10
  68.4 0.1 select_reduce_fusion
  68.5 0.0 copy-done
  68.5 2.0 gather_fusion
  70.5 6.9 %all-to-all-done.1 = bf16[8,192,128]{2,1,0:T(8,128)(2,1)S(1)} async-done(((bf16[8,192,128]{2,1,0:T(8,128)(2,1)}), bf16[8,192,128]{2,1,0:T(8,128)(2,1)S(1)}, u32[]{:S(2)}, u32[]{:S(2)}) %all-to-all-start.1) | async-done | bytes 393248 | tf_op jit(solution)/shard_map/all_to_all | solution.py:490
  77.5 7.1 %all-to-all-start.2 = ((bf16[16,2,64,512]{3,2,1,0:T(8,128)(2,1)}), bf16[16,2,64,512]{3,2,1,0:T(8,128)(2,1)S(1)}, u32[]{:S(2)}, u32[]{:S(2)}) async-start(bf16[16,2,64,512]{3,2,1,0:T(8,128)(2,1)} %bitcast.4), calls=%async_computation.2 | async-start | bytes 4194304 | tf_op jit(solution)/shard_map/all_to_all | solution.py:508
  84.6 3.1 %collective-permute-start.9 = (bf16[128,2048]{1,0:T(8,128)(2,1)}, bf16[128,2048]{1,0:T(8,128)(2,1)}, u32[]{:S(2)}, u32[]{:S(2)}) collective-permute-start(bf16[128,2048]{1,0:T(8,128)(2,1)} %get-tuple-element.8.rest_4_), channel_id=1, source_target_pairs={{0,4},{1,5},{2,6},{3,7},{4,8},{5,9},{6,10},{7,11},{8,12},{9,13},{1... | collective-permute-start | bytes 1572872 | tf_op jit(solution)/shard_map/ppermute | solution.py:483
  87.7 53.5 %collective-permute-done.9.rest_8_ = bf16[128,2048]{1,0:T(8,128)(2,1)} collective-permute-done((bf16[128,2048]{1,0:T(8,128)(2,1)}, bf16[128,2048]{1,0:T(8,128)(2,1)}, u32[]{:S(2)}, u32[]{:S(2)}) %collective-permute-start.9) | collective-permute-done | bytes 524320 | tf_op jit(solution)/shard_map/ppermute | solution.py:483
  141.1 4.1 %collective-permute-start.13 = (bf16[128,2048]{1,0:T(8,128)(2,1)}, bf16[128,2048]{1,0:T(8,128)(2,1)}, u32[]{:S(2)}, u32[]{:S(2)}) collective-permute-start(bf16[128,2048]{1,0:T(8,128)(2,1)} %collective-permute-done.9.rest_8_), channel_id=1, source_target_pairs={{0,4},{1,5},{2,6},{3,7},{4,8},{5,9},{6,10},{7,11},{8,12},{9,13},{1... | collective-permute-start | bytes 1572872 | tf_op jit(solution)/shard_map/ppermute | solution.py:483
  145.2 0.3 collective-permute-start.7
  145.6 1.5 collective-permute-start.6
  147.1 1.2 collective-permute-start.11
  148.3 7.5 %collective-permute-done.13.rest_12_ = bf16[128,2048]{1,0:T(8,128)(2,1)} collective-permute-done((bf16[128,2048]{1,0:T(8,128)(2,1)}, bf16[128,2048]{1,0:T(8,128)(2,1)}, u32[]{:S(2)}, u32[]{:S(2)}) %collective-permute-start.13) | collective-permute-done | bytes 524320 | tf_op jit(solution)/shard_map/ppermute | solution.py:483
  155.8 0.3 collective-permute-start.15
  156.1 2.1 collective-permute-start.10
  158.2 0.0 collective-permute-done.7.rest_6_
  158.2 3.4 %collective-permute-start.8 = (bf16[128,2048]{1,0:T(8,128)(2,1)}, bf16[128,2048]{1,0:T(8,128)(2,1)}, u32[]{:S(2)}, u32[]{:S(2)}) collective-permute-start(bf16[128,2048]{1,0:T(8,128)(2,1)} %collective-permute-done.7.rest_6_), channel_id=1, source_target_pairs={{0,1},{1,0},{2,3},{3,2},{4,5},{5,4},{6,7},{7,6},{8,9},{9,8},{10,11... | collective-permute-start | bytes 1572872 | tf_op jit(solution)/shard_map/ppermute | solution.py:486
  161.7 0.7 reduce_sum.23
  162.3 0.8 slice.11.refs_0_
  163.1 0.0 collective-permute-done.6.rest_5_
  163.1 1.9 collective-permute-start.1
  165.0 4.1 %collective-permute-done.11.rest_10_ = bf16[128,2048]{1,0:T(8,128)(2,1)} collective-permute-done((bf16[128,2048]{1,0:T(8,128)(2,1)}, bf16[128,2048]{1,0:T(8,128)(2,1)}, u32[]{:S(2)}, u32[]{:S(2)}) %collective-permute-start.11) | collective-permute-done | bytes 524320 | tf_op jit(solution)/shard_map/ppermute | solution.py:484
  169.1 1.5 collective-permute-start.2
  170.6 9.8 %collective-permute-done.15.rest_14_ = bf16[128,2048]{1,0:T(8,128)(2,1)} collective-permute-done((bf16[128,2048]{1,0:T(8,128)(2,1)}, bf16[128,2048]{1,0:T(8,128)(2,1)}, u32[]{:S(2)}, u32[]{:S(2)}) %collective-permute-start.15) | collective-permute-done | bytes 524320 | tf_op jit(solution)/shard_map/ppermute | solution.py:484
  180.3 2.1 collective-permute-start.14
  182.4 0.0 collective-permute-done.1.refs_1_
  182.4 0.1 collective-permute-start.12
  182.5 0.0 collective-permute-done.2.refs_2_
  182.5 0.4 collective-permute-start.16
  183.0 0.0 copy-done.3
  183.0 0.1 copy-done.7
  183.1 0.1 copy-done.8
  183.1 1.4 join.1.rest_0_
  184.6 0.0 collective-permute-done.10.rest_9_
  184.6 0.3 collective-permute-start.4
  184.8 0.0 collective-permute-done.8.rest_7_
  184.8 0.7 collective-permute-start.3
  185.6 3.1 %collective-permute-done.4.rest_2_ = bf16[3,128,128]{2,1,0:T(8,128)(2,1)S(1)} collective-permute-done((bf16[3,128,128]{2,1,0:T(8,128)(2,1)}, bf16[3,128,128]{2,1,0:T(8,128)(2,1)S(1)}, u32[]{:S(2)}, u32[]{:S(2)}) %collective-permute-start.4) | collective-permute-done | bytes 98336 | tf_op jit(solution)/shard_map/ppermute | solution.py:516
  188.7 1.3 collective-permute-start.5
  190.0 1.3 slice.10.low_ref
  191.3 0.0 collective-permute-done.14.rest_13_
  191.3 0.0 collective-permute-done.12.rest_11_
  191.3 0.0 collective-permute-done.16.rest_15_
  191.3 0.0 collective-permute-done.3.rest_1_
  191.3 0.0 copy-start.5
  191.3 0.0 collective-permute-done.5.rest_3_
  191.4 0.0 copy-done.4
  191.4 0.6 copy-done.5
  192.0 0.6 copy-done.6
  192.6 8.9 %finish.1.key_ref.value_ref = bf16[1536,2048]{1,0:T(8,128)(2,1)} custom-call(s32[1]{0:T(128)} %bitcast.place_ref, s32[32]{0:T(128)} %request_ref.5, s32[8]{0:T(128)} %adapter_ref.3, bf16[16,64,2048]{2,1,0:T(8,128)(2,1)} %up_ref.1, bf16[3,128,128]{2,1,0:T(8,128)(2,1)} %join.1.rest_0_, bf16[3,128,128]{2,1,0:T(8,128)(2,1)} %copy-done.5, ...), custom_call_target="tpu_custom_call" | custom-call | flops 402653184 | bytes 12582912 | tf_op jit(solution)/shard_map/finish/pallas_call | solution.py:213
  201.6 0.0 all-to-all-done.2.up_ref
  201.6 0.0 copy-start.2
  201.6 1.4 copy-done.2
  203.0 20.6 %attend.1 = bf16[128,8192]{1,0:T(8,128)(2,1)} custom-call(s32[1]{0:T(128)} %bitcast.place_ref, s32[32]{0:T(128)} %request_ref.5, bf16[128,8192]{1,0:T(8,128)(2,1)} %q_ref.1, bf16[64,128]{1,0:T(8,128)(2,1)} %slice.10.low_ref, bf16[16,2,64,512]{3,2,1,0:T(8,128)(2,1)} %copy-done.2, bf16[1536,2048]{1,0:T(8,128)(2,1)} %finish.1.key_ref.value_ref, ...), custom_call_target="tpu_custom_call" | custom-call | flops 3221225472 | bytes 16777216 | tf_op jit(solution)/shard_map/attend/pallas_call | solution.py:411
  (10 shorter events, 0.0 us)
Async XLA Ops:
  0.0 68.5 %copy-start = (bf16[16,64,512]{2,1,0:T(8,128)(2,1)S(1)}, bf16[16,64,512]{2,1,0:T(8,128)(2,1)}, u32[]{:S(2)}) copy-start(bf16[16,64,512]{2,1,0:T(8,128)(2,1)} %param.14) | copy-start | bytes 3145732
  2.8 51.4 %all-to-all-start = ((bf16[8,128,1024]{2,1,0:T(8,128)(2,1)}), bf16[8,128,1024]{2,1,0:T(8,128)(2,1)S(1)}, u32[]{:S(2)}, u32[]{:S(2)}) async-start(bf16[8,128,1024]{2,1,0:T(8,128)(2,1)} %get-tuple-element.7), calls=%async_computation | async-start | bytes 4194304 | tf_op jit(solution)/shard_map/all_to_all | solution.py:473
  8.4 6.9 %collective-permute-start = (bf16[16,192,512]{2,1,0:T(8,128)(2,1)}, bf16[16,192,512]{2,1,0:T(8,128)(2,1)}, u32[]{:S(2)}, u32[]{:S(2)}) collective-permute-start(bf16[16,192,512]{2,1,0:T(8,128)(2,1)} %bitcast.7), channel_id=1, source_target_pairs={{0,1},{1,0},{2,3},{3,2},{4,5},{5,4},{6,7},{7,6},{8,9},{9,8},{10,11... | collective-permute-start | bytes 9437192 | tf_op jit(solution)/shard_map/ppermute | solution.py:477
  54.2 1.3 copy-start.1
  55.5 12.9 %copy-start.9 = (s32[32]{0:T(128)S(1)}, s32[32]{0:T(128)}, u32[]{:S(2)}) copy-start(s32[32]{0:T(128)} %request_ref.5) | copy-start | bytes 388
  55.5 12.9 %copy-start.10 = (s32[8]{0:T(128)S(1)}, s32[8]{0:T(128)}, u32[]{:S(2)}) copy-start(s32[8]{0:T(128)} %adapter_ref.3) | copy-start | bytes 100
  62.0 15.4 %all-to-all-start.1 = ((bf16[8,192,128]{2,1,0:T(8,128)(2,1)}), bf16[8,192,128]{2,1,0:T(8,128)(2,1)S(1)}, u32[]{:S(2)}, u32[]{:S(2)}) async-start(bf16[8,192,128]{2,1,0:T(8,128)(2,1)} %shrink.1), calls=%async_computation.1 | async-start | bytes 786432 | tf_op jit(solution)/shard_map/all_to_all | solution.py:490
  77.5 124.1 %all-to-all-start.2 = ((bf16[16,2,64,512]{3,2,1,0:T(8,128)(2,1)}), bf16[16,2,64,512]{3,2,1,0:T(8,128)(2,1)S(1)}, u32[]{:S(2)}, u32[]{:S(2)}) async-start(bf16[16,2,64,512]{3,2,1,0:T(8,128)(2,1)} %bitcast.4), calls=%async_computation.2 | async-start | bytes 4194304 | tf_op jit(solution)/shard_map/all_to_all | solution.py:508
  84.6 56.6 %collective-permute-start.9 = (bf16[128,2048]{1,0:T(8,128)(2,1)}, bf16[128,2048]{1,0:T(8,128)(2,1)}, u32[]{:S(2)}, u32[]{:S(2)}) collective-permute-start(bf16[128,2048]{1,0:T(8,128)(2,1)} %get-tuple-element.8.rest_4_), channel_id=1, source_target_pairs={{0,4},{1,5},{2,6},{3,7},{4,8},{5,9},{6,10},{7,11},{8,12},{9,13},{1... | collective-permute-start | bytes 1572872 | tf_op jit(solution)/shard_map/ppermute | solution.py:483
  141.1 14.7 %collective-permute-start.13 = (bf16[128,2048]{1,0:T(8,128)(2,1)}, bf16[128,2048]{1,0:T(8,128)(2,1)}, u32[]{:S(2)}, u32[]{:S(2)}) collective-permute-start(bf16[128,2048]{1,0:T(8,128)(2,1)} %collective-permute-done.9.rest_8_), channel_id=1, source_target_pairs={{0,4},{1,5},{2,6},{3,7},{4,8},{5,9},{6,10},{7,11},{8,12},{9,13},{1... | collective-permute-start | bytes 1572872 | tf_op jit(solution)/shard_map/ppermute | solution.py:483
  145.2 13.0 %collective-permute-start.7 = (bf16[128,2048]{1,0:T(8,128)(2,1)}, bf16[128,2048]{1,0:T(8,128)(2,1)}, u32[]{:S(2)}, u32[]{:S(2)}) collective-permute-start(bf16[128,2048]{1,0:T(8,128)(2,1)} %get-tuple-element.8.rest_4_), channel_id=1, source_target_pairs={{0,2},{1,3},{2,0},{3,1},{4,6},{5,7},{6,4},{7,5},{8,10},{9,11},{10,... | collective-permute-start | bytes 1572872 | tf_op jit(solution)/shard_map/ppermute | solution.py:484
  145.6 17.5 %collective-permute-start.6 = (bf16[128,2048]{1,0:T(8,128)(2,1)}, bf16[128,2048]{1,0:T(8,128)(2,1)}, u32[]{:S(2)}, u32[]{:S(2)}) collective-permute-start(bf16[128,2048]{1,0:T(8,128)(2,1)} %get-tuple-element.8.rest_4_), channel_id=1, source_target_pairs={{0,1},{1,0},{2,3},{3,2},{4,5},{5,4},{6,7},{7,6},{8,9},{9,8},{10,11... | collective-permute-start | bytes 1572872 | tf_op jit(solution)/shard_map/ppermute | solution.py:485
  147.1 22.0 %collective-permute-start.11 = (bf16[128,2048]{1,0:T(8,128)(2,1)}, bf16[128,2048]{1,0:T(8,128)(2,1)}, u32[]{:S(2)}, u32[]{:S(2)}) collective-permute-start(bf16[128,2048]{1,0:T(8,128)(2,1)} %collective-permute-done.9.rest_8_), channel_id=1, source_target_pairs={{0,2},{1,3},{2,0},{3,1},{4,6},{5,7},{6,4},{7,5},{8,10},{9,11},{10,... | collective-permute-start | bytes 1572872 | tf_op jit(solution)/shard_map/ppermute | solution.py:484
  155.8 24.5 %collective-permute-start.15 = (bf16[128,2048]{1,0:T(8,128)(2,1)}, bf16[128,2048]{1,0:T(8,128)(2,1)}, u32[]{:S(2)}, u32[]{:S(2)}) collective-permute-start(bf16[128,2048]{1,0:T(8,128)(2,1)} %collective-permute-done.13.rest_12_), channel_id=1, source_target_pairs={{0,2},{1,3},{2,0},{3,1},{4,6},{5,7},{6,4},{7,5},{8,10},{9,11},{10,... | collective-permute-start | bytes 1572872 | tf_op jit(solution)/shard_map/ppermute | solution.py:484
  156.1 28.4 %collective-permute-start.10 = (bf16[128,2048]{1,0:T(8,128)(2,1)}, bf16[128,2048]{1,0:T(8,128)(2,1)}, u32[]{:S(2)}, u32[]{:S(2)}) collective-permute-start(bf16[128,2048]{1,0:T(8,128)(2,1)} %collective-permute-done.9.rest_8_), channel_id=1, source_target_pairs={{0,1},{1,0},{2,3},{3,2},{4,5},{5,4},{6,7},{7,6},{8,9},{9,8},{10,11... | collective-permute-start | bytes 1572872 | tf_op jit(solution)/shard_map/ppermute | solution.py:485
  158.2 26.6 %collective-permute-start.8 = (bf16[128,2048]{1,0:T(8,128)(2,1)}, bf16[128,2048]{1,0:T(8,128)(2,1)}, u32[]{:S(2)}, u32[]{:S(2)}) collective-permute-start(bf16[128,2048]{1,0:T(8,128)(2,1)} %collective-permute-done.7.rest_6_), channel_id=1, source_target_pairs={{0,1},{1,0},{2,3},{3,2},{4,5},{5,4},{6,7},{7,6},{8,9},{9,8},{10,11... | collective-permute-start | bytes 1572872 | tf_op jit(solution)/shard_map/ppermute | solution.py:486
  163.1 19.9 %copy-start.3 = (bf16[128,128]{1,0:T(8,128)(2,1)}, bf16[128,128]{1,0:T(8,128)(2,1)S(1)}, u32[]{:S(2)}) copy-start(bf16[128,128]{1,0:T(8,128)(2,1)S(1)} %slice.11.refs_0_) | copy-start | bytes 98308
  163.1 19.3 %collective-permute-start.1 = (bf16[128,128]{1,0:T(8,128)(2,1)S(1)}, bf16[128,128]{1,0:T(8,128)(2,1)S(1)}, u32[]{:S(2)}, u32[]{:S(2)}) collective-permute-start(bf16[128,128]{1,0:T(8,128)(2,1)S(1)} %slice.11.refs_0_), channel_id=1, source_target_pairs={{0,4},{1,5},{2,6},{3,7},{4,8},{5,9},{6,10},{7,11},{8,12},{9,13},{1... | collective-permute-start | bytes 98312 | tf_op jit(solution)/shard_map/ppermute | solution.py:514
  169.1 13.4 %collective-permute-start.2 = (bf16[128,128]{1,0:T(8,128)(2,1)S(1)}, bf16[128,128]{1,0:T(8,128)(2,1)S(1)}, u32[]{:S(2)}, u32[]{:S(2)}) collective-permute-start(bf16[128,128]{1,0:T(8,128)(2,1)S(1)} %slice.11.refs_0_), channel_id=1, source_target_pairs={{0,8},{1,9},{2,10},{3,11},{4,12},{5,13},{6,14},{7,15},{16,24},{17,... | collective-permute-start | bytes 98312 | tf_op jit(solution)/shard_map/ppermute | solution.py:514
  180.3 11.0 %collective-permute-start.14 = (bf16[128,2048]{1,0:T(8,128)(2,1)}, bf16[128,2048]{1,0:T(8,128)(2,1)}, u32[]{:S(2)}, u32[]{:S(2)}) collective-permute-start(bf16[128,2048]{1,0:T(8,128)(2,1)} %collective-permute-done.13.rest_12_), channel_id=1, source_target_pairs={{0,1},{1,0},{2,3},{3,2},{4,5},{5,4},{6,7},{7,6},{8,9},{9,8},{10,11... | collective-permute-start | bytes 1572872 | tf_op jit(solution)/shard_map/ppermute | solution.py:485
  182.4 0.6 copy-start.7
  182.4 8.9 %collective-permute-start.12 = (bf16[128,2048]{1,0:T(8,128)(2,1)}, bf16[128,2048]{1,0:T(8,128)(2,1)}, u32[]{:S(2)}, u32[]{:S(2)}) collective-permute-start(bf16[128,2048]{1,0:T(8,128)(2,1)} %collective-permute-done.11.rest_10_), channel_id=1, source_target_pairs={{0,1},{1,0},{2,3},{3,2},{4,5},{5,4},{6,7},{7,6},{8,9},{9,8},{10,11... | collective-permute-start | bytes 1572872 | tf_op jit(solution)/shard_map/ppermute | solution.py:486
  182.5 0.6 copy-start.8
  182.5 8.8 %collective-permute-start.16 = (bf16[128,2048]{1,0:T(8,128)(2,1)}, bf16[128,2048]{1,0:T(8,128)(2,1)}, u32[]{:S(2)}, u32[]{:S(2)}) collective-permute-start(bf16[128,2048]{1,0:T(8,128)(2,1)} %collective-permute-done.15.rest_14_), channel_id=1, source_target_pairs={{0,1},{1,0},{2,3},{3,2},{4,5},{5,4},{6,7},{7,6},{8,9},{9,8},{10,11... | collective-permute-start | bytes 1572872 | tf_op jit(solution)/shard_map/ppermute | solution.py:486
  184.6 4.1 %collective-permute-start.4 = (bf16[3,128,128]{2,1,0:T(8,128)(2,1)}, bf16[3,128,128]{2,1,0:T(8,128)(2,1)S(1)}, u32[]{:S(2)}, u32[]{:S(2)}) collective-permute-start(bf16[3,128,128]{2,1,0:T(8,128)(2,1)} %join.1.rest_0_), channel_id=1, source_target_pairs={{0,2},{1,3},{2,0},{3,1},{4,6},{5,7},{6,4},{7,5},{8,10},{9,11},{10,... | collective-permute-start | bytes 294920 | tf_op jit(solution)/shard_map/ppermute | solution.py:516
  184.8 6.5 %collective-permute-start.3 = (bf16[3,128,128]{2,1,0:T(8,128)(2,1)}, bf16[3,128,128]{2,1,0:T(8,128)(2,1)S(1)}, u32[]{:S(2)}, u32[]{:S(2)}) collective-permute-start(bf16[3,128,128]{2,1,0:T(8,128)(2,1)} %join.1.rest_0_), channel_id=1, source_target_pairs={{0,1},{1,0},{2,3},{3,2},{4,5},{5,4},{6,7},{7,6},{8,9},{9,8},{10,11... | collective-permute-start | bytes 294920 | tf_op jit(solution)/shard_map/ppermute | solution.py:517
  188.7 2.7 %copy-start.4 = (bf16[3,128,128]{2,1,0:T(8,128)(2,1)}, bf16[3,128,128]{2,1,0:T(8,128)(2,1)S(1)}, u32[]{:S(2)}) copy-start(bf16[3,128,128]{2,1,0:T(8,128)(2,1)S(1)} %collective-permute-done.4.rest_2_) | copy-start | bytes 294916
  188.7 2.7 %collective-permute-start.5 = (bf16[3,128,128]{2,1,0:T(8,128)(2,1)S(1)}, bf16[3,128,128]{2,1,0:T(8,128)(2,1)S(1)}, u32[]{:S(2)}, u32[]{:S(2)}) collective-permute-start(bf16[3,128,128]{2,1,0:T(8,128)(2,1)S(1)} %collective-permute-done.4.rest_2_), channel_id=1, source_target_pairs={{0,1},{1,0},{2,3},{3,2},{4,5},{5,4},{6,7},{7,6},{8,9},{9,8},{10,11... | collective-permute-start | bytes 294920 | tf_op jit(solution)/shard_map/ppermute | solution.py:518
  191.3 0.6 copy-start.5
  192.0 0.6 copy-start.6
  201.6 1.4 copy-start.2

commit v4 on v3

--- a/solution.py
+++ b/solution.py
@@ -241,7 +241,7 @@
     place_ref, request_ref, q_ref, low_ref, up_ref, key_ref, value_ref, *rest,
 ):
     done_ref = rest[0] if piece > 0 else None
-    out_ref, query_ref, total_ref, score_ref, bias_ref, top_ref, sum_ref = rest[-7:]
+    out_ref, query_ref, total_ref, score_ref, bias_ref, top_ref, fade_ref, sum_ref = rest[-8:]
     tokens = q_ref.shape[0]
     per_device = tokens // block_len
     me = place_ref[0]
@@ -314,7 +314,10 @@
             if first:
                 top_ref[slot, :, columns] = top
             else:
-                top_ref[slot, :, columns] = jnp.maximum(top, top_ref[1 - slot, :, columns])
+                before = top_ref[1 - slot, :, columns]
+                top = jnp.maximum(top, before)
+                top_ref[slot, :, columns] = top
+                fade_ref[slot, :, columns] = jnp.exp2((before - top) * factor)
 
     def gather(step, slot, parts, first, masked):
         stop = end - step * KEY_CHUNK
@@ -337,7 +340,7 @@
                 sums = more if sums is None else sums + more
                 product = extra if product is None else product + extra
             if not first:
-                fade = jnp.exp2((top_ref[1 - slot, :, columns] - top) * factor)
+                fade = fade_ref[slot, :, columns]
                 sums = sums + sum_ref[:, columns] * fade
                 product = product + total_ref[:, columns] * fade
             sum_ref[:, columns] = sums
@@ -376,13 +379,16 @@
 
     @pl.when((chunks > 1) & jnp.logical_not(all_same))
     def _():
+        score(1, 1, leading, False, True)
         gather(0, 0, every, True, True)
 
-        @pl.loop(1, chunks)
+        @pl.loop(2, chunks)
         def _(step):
             slot = lax.rem(step, 2)
             score(step, slot, leading, False, True)
-            gather(step, slot, leading, False, True)
+            gather(step - 1, 1 - slot, leading, False, True)
+
+        gather(chunks - 1, lax.rem(chunks - 1, 2), leading, False, True)
 
     for part in every:
         columns = pl.ds(part * rows, rows)
@@ -429,6 +435,7 @@
                 pltpu.VMEM((2, KEY_CHUNK, lanes), jnp.float32),
                 pltpu.VMEM((tokens, lanes), jnp.float32),
                 pltpu.VMEM((2, 1, lanes), jnp.float32),
+                pltpu.VMEM((2, 1, lanes), jnp.float32),
                 pltpu.VMEM((1, lanes), jnp.float32),
             ],
         ),

time: 224 us -> 224 us (level)
  no operation moved by 1% of the time
where the time goes in v4:
time: 224 us; the launch traced here: 223 us
  waiting for transfers between devices  129 us (58%)
  starting transfers between devices  44.7 us (20%)
  Pallas kernels  40.2 us (18%)
  local copies, waits for them, and re-layouts  8.22 us (4%)
    ppermute x2, waiting for transfers between devices, body(): own = lax.ppermute(own, 'seq', forward)  61 us
    all_to_all x1, waiting for transfers between devices, body(): lax.all_to_all(sent, 'seq', split_axis=0, concat_axis=0, axis_index_group...  38.8 us
    pallas_call x1, Pallas kernels, attend(): pl.pallas_call(functools.partial(attend_kernel, block_len, most_blocks, p...  20.5 us
    ppermute x3, waiting for transfers between devices, body(): across = lax.ppermute(own, 'seq', swap_row)  13.8 us
    pallas_call x1, Pallas kernels, finish(): pl.pallas_call(functools.partial(finish_kernel, block_len, planes), out_s...  8.94 us
    ppermute x2, starting transfers between devices, body(): own = lax.ppermute(own, 'seq', forward)  7.18 us
    all_to_all x1, starting transfers between devices, body(): lax.all_to_all(picked, 'seq', split_axis=0, concat_axis=0, tiled=True)  7.11 us
    all_to_all x1, waiting for transfers between devices, body(): lax.all_to_all(partials, 'seq', split_axis=0, concat_axis=0, axis_index_g...  6.95 us
  transfers between devices with their start and end apart: 20, of which 8 were waited for; matrix products, arithmetic and copies ran while one was open for 2% of the time, Pallas kernels for 5%

profile of v4, /device:TPU:15, one launch (start us, length us, event | category | flops | bytes accessed | tf_op | source)
XLA Modules:
  0.0 223.4 jit_solution(10662910025903051508)
XLA Ops:
  0.0 0.0 copy-start
  0.0 2.8 %split.1 = (bf16[8,128,1024]{2,1,0:T(8,128)(2,1)}, bf16[128,2048]{1,0:T(8,128)(2,1)}) custom-call(bf16[128,8192]{1,0:T(8,128)(2,1)} %hidden_ref.1, bf16[128,1024]{1,0:T(8,128)(2,1)} %key_ref.1, bf16[128,1024]{1,0:T(8,128)(2,1)} %value_ref.1), custom_call_target="tpu_custom_call" | custom-call | tf_op jit(solution)/shard_map/split/pallas_call | solution.py:53
  2.8 5.7 %all-to-all-start = ((bf16[8,128,1024]{2,1,0:T(8,128)(2,1)}), bf16[8,128,1024]{2,1,0:T(8,128)(2,1)S(1)}, u32[]{:S(2)}, u32[]{:S(2)}) async-start(bf16[8,128,1024]{2,1,0:T(8,128)(2,1)} %get-tuple-element.7), calls=%async_computation | async-start | bytes 4194304 | tf_op jit(solution)/shard_map/all_to_all | solution.py:480
  8.4 1.2 collective-permute-start
  9.7 5.6 %collective-permute-done.other_hbm = bf16[16,192,512]{2,1,0:T(8,128)(2,1)} collective-permute-done((bf16[16,192,512]{2,1,0:T(8,128)(2,1)}, bf16[16,192,512]{2,1,0:T(8,128)(2,1)}, u32[]{:S(2)}, u32[]{:S(2)}) %collective-permute-start) | collective-permute-done | bytes 3145760 | tf_op jit(solution)/shard_map/ppermute | solution.py:484
  15.3 38.8 %all-to-all-done.rows_hbm = bf16[8,128,1024]{2,1,0:T(8,128)(2,1)S(1)} async-done(((bf16[8,128,1024]{2,1,0:T(8,128)(2,1)}), bf16[8,128,1024]{2,1,0:T(8,128)(2,1)S(1)}, u32[]{:S(2)}, u32[]{:S(2)}) %all-to-all-start) | async-done | bytes 2097184 | tf_op jit(solution)/shard_map/all_to_all | solution.py:480
  54.2 1.3 copy-done.1
  55.5 6.6 %shrink.1 = bf16[8,192,128]{2,1,0:T(8,128)(2,1)} custom-call(s32[1]{0:T(128)} %bitcast.place_ref, s32[32]{0:T(128)} %request_ref.5, s32[8]{0:T(128)} %adapter_ref.3, bf16[8,128,1024]{2,1,0:T(8,128)(2,1)} %copy-done.1, bf16[16,192,512]{2,1,0:T(8,128)(2,1)} %bitcast.8, bf16[16,192,512]{2,1,0:T(8,128)(2,1)} %collective-permute-done.other_hbm), custom_call_target="tpu_custom_call" | custom-call | flops 402653184 | bytes 8388608 | tf_op jit(solution)/shard_map/shrink/pallas_call | solution.py:132
  62.0 6.4 %all-to-all-start.1 = ((bf16[8,192,128]{2,1,0:T(8,128)(2,1)}), bf16[8,192,128]{2,1,0:T(8,128)(2,1)S(1)}, u32[]{:S(2)}, u32[]{:S(2)}) async-start(bf16[8,192,128]{2,1,0:T(8,128)(2,1)} %shrink.1), calls=%async_computation.1 | async-start | bytes 786432 | tf_op jit(solution)/shard_map/all_to_all | solution.py:497
  68.4 0.0 copy-done.9
  68.4 0.0 copy-done.10
  68.4 0.1 select_reduce_fusion
  68.5 0.0 copy-done
  68.5 2.0 gather_fusion
  70.5 6.9 %all-to-all-done.1 = bf16[8,192,128]{2,1,0:T(8,128)(2,1)S(1)} async-done(((bf16[8,192,128]{2,1,0:T(8,128)(2,1)}), bf16[8,192,128]{2,1,0:T(8,128)(2,1)S(1)}, u32[]{:S(2)}, u32[]{:S(2)}) %all-to-all-start.1) | async-done | bytes 393248 | tf_op jit(solution)/shard_map/all_to_all | solution.py:497
  77.5 7.1 %all-to-all-start.2 = ((bf16[16,2,64,512]{3,2,1,0:T(8,128)(2,1)}), bf16[16,2,64,512]{3,2,1,0:T(8,128)(2,1)S(1)}, u32[]{:S(2)}, u32[]{:S(2)}) async-start(bf16[16,2,64,512]{3,2,1,0:T(8,128)(2,1)} %bitcast.4), calls=%async_computation.2 | async-start | bytes 4194304 | tf_op jit(solution)/shard_map/all_to_all | solution.py:515
  84.6 3.1 %collective-permute-start.9 = (bf16[128,2048]{1,0:T(8,128)(2,1)}, bf16[128,2048]{1,0:T(8,128)(2,1)}, u32[]{:S(2)}, u32[]{:S(2)}) collective-permute-start(bf16[128,2048]{1,0:T(8,128)(2,1)} %get-tuple-element.8.rest_4_), channel_id=1, source_target_pairs={{0,4},{1,5},{2,6},{3,7},{4,8},{5,9},{6,10},{7,11},{8,12},{9,13},{1... | collective-permute-start | bytes 1572872 | tf_op jit(solution)/shard_map/ppermute | solution.py:490
  87.7 53.5 %collective-permute-done.9.rest_8_ = bf16[128,2048]{1,0:T(8,128)(2,1)} collective-permute-done((bf16[128,2048]{1,0:T(8,128)(2,1)}, bf16[128,2048]{1,0:T(8,128)(2,1)}, u32[]{:S(2)}, u32[]{:S(2)}) %collective-permute-start.9) | collective-permute-done | bytes 524320 | tf_op jit(solution)/shard_map/ppermute | solution.py:490
  141.1 4.1 %collective-permute-start.13 = (bf16[128,2048]{1,0:T(8,128)(2,1)}, bf16[128,2048]{1,0:T(8,128)(2,1)}, u32[]{:S(2)}, u32[]{:S(2)}) collective-permute-start(bf16[128,2048]{1,0:T(8,128)(2,1)} %collective-permute-done.9.rest_8_), channel_id=1, source_target_pairs={{0,4},{1,5},{2,6},{3,7},{4,8},{5,9},{6,10},{7,11},{8,12},{9,13},{1... | collective-permute-start | bytes 1572872 | tf_op jit(solution)/shard_map/ppermute | solution.py:490
  145.2 0.3 collective-permute-start.7
  145.6 1.5 collective-permute-start.6
  147.1 1.2 collective-permute-start.11
  148.3 7.5 %collective-permute-done.13.rest_12_ = bf16[128,2048]{1,0:T(8,128)(2,1)} collective-permute-done((bf16[128,2048]{1,0:T(8,128)(2,1)}, bf16[128,2048]{1,0:T(8,128)(2,1)}, u32[]{:S(2)}, u32[]{:S(2)}) %collective-permute-start.13) | collective-permute-done | bytes 524320 | tf_op jit(solution)/shard_map/ppermute | solution.py:490
  155.8 0.3 collective-permute-start.15
  156.1 2.1 collective-permute-start.10
  158.2 0.0 collective-permute-done.7.rest_6_
  158.2 3.4 %collective-permute-start.8 = (bf16[128,2048]{1,0:T(8,128)(2,1)}, bf16[128,2048]{1,0:T(8,128)(2,1)}, u32[]{:S(2)}, u32[]{:S(2)}) collective-permute-start(bf16[128,2048]{1,0:T(8,128)(2,1)} %collective-permute-done.7.rest_6_), channel_id=1, source_target_pairs={{0,1},{1,0},{2,3},{3,2},{4,5},{5,4},{6,7},{7,6},{8,9},{9,8},{10,11... | collective-permute-start | bytes 1572872 | tf_op jit(solution)/shard_map/ppermute | solution.py:493
  161.7 0.7 reduce_sum.23
  162.3 0.8 slice.11.refs_0_
  163.1 0.0 collective-permute-done.6.rest_5_
  163.1 1.9 collective-permute-start.1
  165.0 4.1 %collective-permute-done.11.rest_10_ = bf16[128,2048]{1,0:T(8,128)(2,1)} collective-permute-done((bf16[128,2048]{1,0:T(8,128)(2,1)}, bf16[128,2048]{1,0:T(8,128)(2,1)}, u32[]{:S(2)}, u32[]{:S(2)}) %collective-permute-start.11) | collective-permute-done | bytes 524320 | tf_op jit(solution)/shard_map/ppermute | solution.py:491
  169.1 1.5 collective-permute-start.2
  170.6 9.8 %collective-permute-done.15.rest_14_ = bf16[128,2048]{1,0:T(8,128)(2,1)} collective-permute-done((bf16[128,2048]{1,0:T(8,128)(2,1)}, bf16[128,2048]{1,0:T(8,128)(2,1)}, u32[]{:S(2)}, u32[]{:S(2)}) %collective-permute-start.15) | collective-permute-done | bytes 524320 | tf_op jit(solution)/shard_map/ppermute | solution.py:491
  180.3 2.1 collective-permute-start.14
  182.4 0.0 collective-permute-done.1.refs_1_
  182.4 0.1 collective-permute-start.12
  182.5 0.0 collective-permute-done.2.refs_2_
  182.5 0.4 collective-permute-start.16
  183.0 0.0 copy-done.3
  183.0 0.1 copy-done.7
  183.1 0.1 copy-done.8
  183.1 1.4 join.1.rest_0_
  184.6 0.0 collective-permute-done.10.rest_9_
  184.6 0.3 collective-permute-start.4
  184.8 0.0 collective-permute-done.8.rest_7_
  184.8 0.7 collective-permute-start.3
  185.6 3.1 %collective-permute-done.4.rest_2_ = bf16[3,128,128]{2,1,0:T(8,128)(2,1)S(1)} collective-permute-done((bf16[3,128,128]{2,1,0:T(8,128)(2,1)}, bf16[3,128,128]{2,1,0:T(8,128)(2,1)S(1)}, u32[]{:S(2)}, u32[]{:S(2)}) %collective-permute-start.4) | collective-permute-done | bytes 98336 | tf_op jit(solution)/shard_map/ppermute | solution.py:523
  188.7 1.3 collective-permute-start.5
  190.0 1.3 slice.10.low_ref
  191.3 0.0 collective-permute-done.14.rest_13_
  191.3 0.0 collective-permute-done.12.rest_11_
  191.3 0.0 collective-permute-done.16.rest_15_
  191.3 0.0 collective-permute-done.3.rest_1_
  191.3 0.0 copy-start.5
  191.3 0.0 collective-permute-done.5.rest_3_
  191.4 0.0 copy-done.4
  191.4 0.6 copy-done.5
  192.0 0.6 copy-done.6
  192.6 8.9 %finish.1.key_ref.value_ref = bf16[1536,2048]{1,0:T(8,128)(2,1)} custom-call(s32[1]{0:T(128)} %bitcast.place_ref, s32[32]{0:T(128)} %request_ref.5, s32[8]{0:T(128)} %adapter_ref.3, bf16[16,64,2048]{2,1,0:T(8,128)(2,1)} %up_ref.1, bf16[3,128,128]{2,1,0:T(8,128)(2,1)} %join.1.rest_0_, bf16[3,128,128]{2,1,0:T(8,128)(2,1)} %copy-done.5, ...), custom_call_target="tpu_custom_call" | custom-call | flops 402653184 | bytes 12582912 | tf_op jit(solution)/shard_map/finish/pallas_call | solution.py:213
  201.6 0.0 all-to-all-done.2.up_ref
  201.6 0.0 copy-start.2
  201.6 1.4 copy-done.2
  203.0 20.5 %attend.1 = bf16[128,8192]{1,0:T(8,128)(2,1)} custom-call(s32[1]{0:T(128)} %bitcast.place_ref, s32[32]{0:T(128)} %request_ref.5, bf16[128,8192]{1,0:T(8,128)(2,1)} %q_ref.1, bf16[64,128]{1,0:T(8,128)(2,1)} %slice.10.low_ref, bf16[16,2,64,512]{3,2,1,0:T(8,128)(2,1)} %copy-done.2, bf16[1536,2048]{1,0:T(8,128)(2,1)} %finish.1.key_ref.value_ref, ...), custom_call_target="tpu_custom_call" | custom-call | flops 3221225472 | bytes 16777216 | tf_op jit(solution)/shard_map/attend/pallas_call | solution.py:417
  (10 shorter events, 0.0 us)
Async XLA Ops:
  0.0 68.5 %copy-start = (bf16[16,64,512]{2,1,0:T(8,128)(2,1)S(1)}, bf16[16,64,512]{2,1,0:T(8,128)(2,1)}, u32[]{:S(2)}) copy-start(bf16[16,64,512]{2,1,0:T(8,128)(2,1)} %param.14) | copy-start | bytes 3145732
  2.8 51.4 %all-to-all-start = ((bf16[8,128,1024]{2,1,0:T(8,128)(2,1)}), bf16[8,128,1024]{2,1,0:T(8,128)(2,1)S(1)}, u32[]{:S(2)}, u32[]{:S(2)}) async-start(bf16[8,128,1024]{2,1,0:T(8,128)(2,1)} %get-tuple-element.7), calls=%async_computation | async-start | bytes 4194304 | tf_op jit(solution)/shard_map/all_to_all | solution.py:480
  8.4 6.9 %collective-permute-start = (bf16[16,192,512]{2,1,0:T(8,128)(2,1)}, bf16[16,192,512]{2,1,0:T(8,128)(2,1)}, u32[]{:S(2)}, u32[]{:S(2)}) collective-permute-start(bf16[16,192,512]{2,1,0:T(8,128)(2,1)} %bitcast.7), channel_id=1, source_target_pairs={{0,1},{1,0},{2,3},{3,2},{4,5},{5,4},{6,7},{7,6},{8,9},{9,8},{10,11... | collective-permute-start | bytes 9437192 | tf_op jit(solution)/shard_map/ppermute | solution.py:484
  54.2 1.3 copy-start.1
  55.5 12.9 %copy-start.9 = (s32[32]{0:T(128)S(1)}, s32[32]{0:T(128)}, u32[]{:S(2)}) copy-start(s32[32]{0:T(128)} %request_ref.5) | copy-start | bytes 388
  55.5 12.9 %copy-start.10 = (s32[8]{0:T(128)S(1)}, s32[8]{0:T(128)}, u32[]{:S(2)}) copy-start(s32[8]{0:T(128)} %adapter_ref.3) | copy-start | bytes 100
  62.0 15.4 %all-to-all-start.1 = ((bf16[8,192,128]{2,1,0:T(8,128)(2,1)}), bf16[8,192,128]{2,1,0:T(8,128)(2,1)S(1)}, u32[]{:S(2)}, u32[]{:S(2)}) async-start(bf16[8,192,128]{2,1,0:T(8,128)(2,1)} %shrink.1), calls=%async_computation.1 | async-start | bytes 786432 | tf_op jit(solution)/shard_map/all_to_all | solution.py:497
  77.5 124.1 %all-to-all-start.2 = ((bf16[16,2,64,512]{3,2,1,0:T(8,128)(2,1)}), bf16[16,2,64,512]{3,2,1,0:T(8,128)(2,1)S(1)}, u32[]{:S(2)}, u32[]{:S(2)}) async-start(bf16[16,2,64,512]{3,2,1,0:T(8,128)(2,1)} %bitcast.4), calls=%async_computation.2 | async-start | bytes 4194304 | tf_op jit(solution)/shard_map/all_to_all | solution.py:515
  84.6 56.6 %collective-permute-start.9 = (bf16[128,2048]{1,0:T(8,128)(2,1)}, bf16[128,2048]{1,0:T(8,128)(2,1)}, u32[]{:S(2)}, u32[]{:S(2)}) collective-permute-start(bf16[128,2048]{1,0:T(8,128)(2,1)} %get-tuple-element.8.rest_4_), channel_id=1, source_target_pairs={{0,4},{1,5},{2,6},{3,7},{4,8},{5,9},{6,10},{7,11},{8,12},{9,13},{1... | collective-permute-start | bytes 1572872 | tf_op jit(solution)/shard_map/ppermute | solution.py:490
  141.1 14.7 %collective-permute-start.13 = (bf16[128,2048]{1,0:T(8,128)(2,1)}, bf16[128,2048]{1,0:T(8,128)(2,1)}, u32[]{:S(2)}, u32[]{:S(2)}) collective-permute-start(bf16[128,2048]{1,0:T(8,128)(2,1)} %collective-permute-done.9.rest_8_), channel_id=1, source_target_pairs={{0,4},{1,5},{2,6},{3,7},{4,8},{5,9},{6,10},{7,11},{8,12},{9,13},{1... | collective-permute-start | bytes 1572872 | tf_op jit(solution)/shard_map/ppermute | solution.py:490
  145.2 13.0 %collective-permute-start.7 = (bf16[128,2048]{1,0:T(8,128)(2,1)}, bf16[128,2048]{1,0:T(8,128)(2,1)}, u32[]{:S(2)}, u32[]{:S(2)}) collective-permute-start(bf16[128,2048]{1,0:T(8,128)(2,1)} %get-tuple-element.8.rest_4_), channel_id=1, source_target_pairs={{0,2},{1,3},{2,0},{3,1},{4,6},{5,7},{6,4},{7,5},{8,10},{9,11},{10,... | collective-permute-start | bytes 1572872 | tf_op jit(solution)/shard_map/ppermute | solution.py:491
  145.6 17.5 %collective-permute-start.6 = (bf16[128,2048]{1,0:T(8,128)(2,1)}, bf16[128,2048]{1,0:T(8,128)(2,1)}, u32[]{:S(2)}, u32[]{:S(2)}) collective-permute-start(bf16[128,2048]{1,0:T(8,128)(2,1)} %get-tuple-element.8.rest_4_), channel_id=1, source_target_pairs={{0,1},{1,0},{2,3},{3,2},{4,5},{5,4},{6,7},{7,6},{8,9},{9,8},{10,11... | collective-permute-start | bytes 1572872 | tf_op jit(solution)/shard_map/ppermute | solution.py:492
  147.1 22.0 %collective-permute-start.11 = (bf16[128,2048]{1,0:T(8,128)(2,1)}, bf16[128,2048]{1,0:T(8,128)(2,1)}, u32[]{:S(2)}, u32[]{:S(2)}) collective-permute-start(bf16[128,2048]{1,0:T(8,128)(2,1)} %collective-permute-done.9.rest_8_), channel_id=1, source_target_pairs={{0,2},{1,3},{2,0},{3,1},{4,6},{5,7},{6,4},{7,5},{8,10},{9,11},{10,... | collective-permute-start | bytes 1572872 | tf_op jit(solution)/shard_map/ppermute | solution.py:491
  155.8 24.5 %collective-permute-start.15 = (bf16[128,2048]{1,0:T(8,128)(2,1)}, bf16[128,2048]{1,0:T(8,128)(2,1)}, u32[]{:S(2)}, u32[]{:S(2)}) collective-permute-start(bf16[128,2048]{1,0:T(8,128)(2,1)} %collective-permute-done.13.rest_12_), channel_id=1, source_target_pairs={{0,2},{1,3},{2,0},{3,1},{4,6},{5,7},{6,4},{7,5},{8,10},{9,11},{10,... | collective-permute-start | bytes 1572872 | tf_op jit(solution)/shard_map/ppermute | solution.py:491
  156.1 28.4 %collective-permute-start.10 = (bf16[128,2048]{1,0:T(8,128)(2,1)}, bf16[128,2048]{1,0:T(8,128)(2,1)}, u32[]{:S(2)}, u32[]{:S(2)}) collective-permute-start(bf16[128,2048]{1,0:T(8,128)(2,1)} %collective-permute-done.9.rest_8_), channel_id=1, source_target_pairs={{0,1},{1,0},{2,3},{3,2},{4,5},{5,4},{6,7},{7,6},{8,9},{9,8},{10,11... | collective-permute-start | bytes 1572872 | tf_op jit(solution)/shard_map/ppermute | solution.py:492
  158.2 26.6 %collective-permute-start.8 = (bf16[128,2048]{1,0:T(8,128)(2,1)}, bf16[128,2048]{1,0:T(8,128)(2,1)}, u32[]{:S(2)}, u32[]{:S(2)}) collective-permute-start(bf16[128,2048]{1,0:T(8,128)(2,1)} %collective-permute-done.7.rest_6_), channel_id=1, source_target_pairs={{0,1},{1,0},{2,3},{3,2},{4,5},{5,4},{6,7},{7,6},{8,9},{9,8},{10,11... | collective-permute-start | bytes 1572872 | tf_op jit(solution)/shard_map/ppermute | solution.py:493
  163.1 19.9 %copy-start.3 = (bf16[128,128]{1,0:T(8,128)(2,1)}, bf16[128,128]{1,0:T(8,128)(2,1)S(1)}, u32[]{:S(2)}) copy-start(bf16[128,128]{1,0:T(8,128)(2,1)S(1)} %slice.11.refs_0_) | copy-start | bytes 98308
  163.1 19.3 %collective-permute-start.1 = (bf16[128,128]{1,0:T(8,128)(2,1)S(1)}, bf16[128,128]{1,0:T(8,128)(2,1)S(1)}, u32[]{:S(2)}, u32[]{:S(2)}) collective-permute-start(bf16[128,128]{1,0:T(8,128)(2,1)S(1)} %slice.11.refs_0_), channel_id=1, source_target_pairs={{0,4},{1,5},{2,6},{3,7},{4,8},{5,9},{6,10},{7,11},{8,12},{9,13},{1... | collective-permute-start | bytes 98312 | tf_op jit(solution)/shard_map/ppermute | solution.py:521
  169.1 13.4 %collective-permute-start.2 = (bf16[128,128]{1,0:T(8,128)(2,1)S(1)}, bf16[128,128]{1,0:T(8,128)(2,1)S(1)}, u32[]{:S(2)}, u32[]{:S(2)}) collective-permute-start(bf16[128,128]{1,0:T(8,128)(2,1)S(1)} %slice.11.refs_0_), channel_id=1, source_target_pairs={{0,8},{1,9},{2,10},{3,11},{4,12},{5,13},{6,14},{7,15},{16,24},{17,... | collective-permute-start | bytes 98312 | tf_op jit(solution)/shard_map/ppermute | solution.py:521
  180.3 11.0 %collective-permute-start.14 = (bf16[128,2048]{1,0:T(8,128)(2,1)}, bf16[128,2048]{1,0:T(8,128)(2,1)}, u32[]{:S(2)}, u32[]{:S(2)}) collective-permute-start(bf16[128,2048]{1,0:T(8,128)(2,1)} %collective-permute-done.13.rest_12_), channel_id=1, source_target_pairs={{0,1},{1,0},{2,3},{3,2},{4,5},{5,4},{6,7},{7,6},{8,9},{9,8},{10,11... | collective-permute-start | bytes 1572872 | tf_op jit(solution)/shard_map/ppermute | solution.py:492
  182.4 0.6 copy-start.7
  182.4 8.9 %collective-permute-start.12 = (bf16[128,2048]{1,0:T(8,128)(2,1)}, bf16[128,2048]{1,0:T(8,128)(2,1)}, u32[]{:S(2)}, u32[]{:S(2)}) collective-permute-start(bf16[128,2048]{1,0:T(8,128)(2,1)} %collective-permute-done.11.rest_10_), channel_id=1, source_target_pairs={{0,1},{1,0},{2,3},{3,2},{4,5},{5,4},{6,7},{7,6},{8,9},{9,8},{10,11... | collective-permute-start | bytes 1572872 | tf_op jit(solution)/shard_map/ppermute | solution.py:493
  182.5 0.6 copy-start.8
  182.5 8.8 %collective-permute-start.16 = (bf16[128,2048]{1,0:T(8,128)(2,1)}, bf16[128,2048]{1,0:T(8,128)(2,1)}, u32[]{:S(2)}, u32[]{:S(2)}) collective-permute-start(bf16[128,2048]{1,0:T(8,128)(2,1)} %collective-permute-done.15.rest_14_), channel_id=1, source_target_pairs={{0,1},{1,0},{2,3},{3,2},{4,5},{5,4},{6,7},{7,6},{8,9},{9,8},{10,11... | collective-permute-start | bytes 1572872 | tf_op jit(solution)/shard_map/ppermute | solution.py:493
  184.6 4.1 %collective-permute-start.4 = (bf16[3,128,128]{2,1,0:T(8,128)(2,1)}, bf16[3,128,128]{2,1,0:T(8,128)(2,1)S(1)}, u32[]{:S(2)}, u32[]{:S(2)}) collective-permute-start(bf16[3,128,128]{2,1,0:T(8,128)(2,1)} %join.1.rest_0_), channel_id=1, source_target_pairs={{0,2},{1,3},{2,0},{3,1},{4,6},{5,7},{6,4},{7,5},{8,10},{9,11},{10,... | collective-permute-start | bytes 294920 | tf_op jit(solution)/shard_map/ppermute | solution.py:523
  184.8 6.5 %collective-permute-start.3 = (bf16[3,128,128]{2,1,0:T(8,128)(2,1)}, bf16[3,128,128]{2,1,0:T(8,128)(2,1)S(1)}, u32[]{:S(2)}, u32[]{:S(2)}) collective-permute-start(bf16[3,128,128]{2,1,0:T(8,128)(2,1)} %join.1.rest_0_), channel_id=1, source_target_pairs={{0,1},{1,0},{2,3},{3,2},{4,5},{5,4},{6,7},{7,6},{8,9},{9,8},{10,11... | collective-permute-start | bytes 294920 | tf_op jit(solution)/shard_map/ppermute | solution.py:524
  188.7 2.7 %copy-start.4 = (bf16[3,128,128]{2,1,0:T(8,128)(2,1)}, bf16[3,128,128]{2,1,0:T(8,128)(2,1)S(1)}, u32[]{:S(2)}) copy-start(bf16[3,128,128]{2,1,0:T(8,128)(2,1)S(1)} %collective-permute-done.4.rest_2_) | copy-start | bytes 294916
  188.7 2.7 %collective-permute-start.5 = (bf16[3,128,128]{2,1,0:T(8,128)(2,1)S(1)}, bf16[3,128,128]{2,1,0:T(8,128)(2,1)S(1)}, u32[]{:S(2)}, u32[]{:S(2)}) collective-permute-start(bf16[3,128,128]{2,1,0:T(8,128)(2,1)S(1)} %collective-permute-done.4.rest_2_), channel_id=1, source_target_pairs={{0,1},{1,0},{2,3},{3,2},{4,5},{5,4},{6,7},{7,6},{8,9},{9,8},{10,11... | collective-permute-start | bytes 294920 | tf_op jit(solution)/shard_map/ppermute | solution.py:525
  191.3 0.6 copy-start.5
  192.0 0.6 copy-start.6
  201.6 1.4 copy-start.2

commit v5 on v4

--- a/solution.py
+++ b/solution.py
@@ -69,8 +69,8 @@
 
 
 def shrink_kernel(
-    block_len, place_ref, request_ref, adapter_ref, rows_hbm, own_hbm, other_hbm, out_ref,
-    rows_ref, down_ref, row_sems, down_sems,
+    block_len, place_ref, request_ref, adapter_ref, rows_ref, own_hbm, other_hbm, out_ref,
+    down_ref, down_sems,
 ):
     chips, tokens, features = rows_ref.shape
     requests = down_ref.shape[1]
@@ -86,11 +86,7 @@
                     source.at[adapter], down_ref.at[which, request], down_sems.at[which, request]
                 )
             )
-    loads = [pltpu.make_async_copy(rows_hbm.at[i], rows_ref.at[i], row_sems.at[i]) for i in range(chips)]
-    loads[0].start()
     for copy in downs:
-        copy.start()
-    for copy in loads[1:]:
         copy.start()
     for copy in downs:
         copy.wait()
@@ -99,7 +95,6 @@
         pl.ds(pl.multiple_of((1 - core) * half, half), half),
     ]
     for chip in range(chips):
-        loads[chip].wait()
         device = chip * CORES + core
         picks = [request_ref[device * per_device + part] for part in range(per_device)]
 
@@ -135,12 +130,10 @@
         grid_spec=pltpu.PrefetchScalarGridSpec(
             num_scalar_prefetch=3,
             grid=(1,),
-            in_specs=[pl.BlockSpec(memory_space=pl.ANY)] * 3,
+            in_specs=[pl.BlockSpec(memory_space=pltpu.VMEM)] + [pl.BlockSpec(memory_space=pl.ANY)] * 2,
             out_specs=pl.BlockSpec((chips, width, tokens), lambda i, me, br, ra: (0, 0, 0)),
             scratch_shapes=[
-                pltpu.VMEM((chips, tokens, features), jnp.bfloat16),
                 pltpu.VMEM((CORES, requests, width, half), jnp.bfloat16),
-                pltpu.SemaphoreType.DMA((chips,)),
                 pltpu.SemaphoreType.DMA((CORES, requests)),
             ],
         ),
@@ -246,8 +239,8 @@
     per_device = tokens // block_len
     me = place_ref[0]
     within = lax.rem(me, PLANE)
-    sources = up_ref.shape[0]
     span = up_ref.shape[3]
+    sources = up_ref.shape[0] // pl.num_programs(0)
     heads = span // HEAD_SIZE
     group = sources * heads
     rows = group * block_len
@@ -257,7 +250,7 @@
         for source in range(sources):
             columns = pl.ds(offsets[source], span)
             delta = lax.dot_general(
-                low_ref[:, own_rows], up_ref[source, part], TN, preferred_element_type=jnp.float32
+                low_ref[:, own_rows], up_ref[pl.program_id(0) * sources + source, part], TN, preferred_element_type=jnp.float32
             )
             query = (q_ref[own_rows, columns].astype(jnp.float32) + delta).astype(jnp.bfloat16)
             for at in range(heads):
@@ -408,7 +401,7 @@
 
 def attend(q_base, low, up_rows, kv, place, block_request, block_len, most_blocks, planes, piece, piece_count, done):
     tokens, width = q_base.shape
-    devices, per_device, rank, span = up_rows.shape
+    devices, _, rank, span = up_rows.shape
     window = kv.shape[0]
     head_span = width // KEY_VALUE_HEADS
     sources = devices // KEY_VALUE_HEADS
@@ -423,7 +416,7 @@
             in_specs=[
                 pl.BlockSpec((tokens, head_span), lambda m, me, br: (0, m)),
                 pl.BlockSpec((rank, tokens), lambda m, me, br: (0, 0)),
-                pl.BlockSpec((sources, per_device, rank, span), lambda m, me, br: (m, 0, 0, 0)),
+                pl.BlockSpec(memory_space=pltpu.VMEM),
                 pl.BlockSpec((window, HEAD_SIZE), lambda m, me, br: (0, m)),
                 pl.BlockSpec((window, HEAD_SIZE), lambda m, me, br: (0, KEY_VALUE_HEADS + m)),
             ]
@@ -480,6 +473,7 @@
     rows = lax.all_to_all(
         sent, "seq", split_axis=0, concat_axis=0, axis_index_groups=same_core, tiled=True
     )
+    rows = pltpu.with_memory_space_constraint(rows, pltpu.VMEM)
     down = jnp.swapaxes(shrink_a, 1, 2)
     other_down = lax.ppermute(down, "seq", swap_core)
 
@@ -512,7 +506,8 @@
     for piece in range(piece_count):
         picked = expand_q[:, :, piece * span : (piece + 1) * span][adapter_of]
         picked = picked.reshape(devices, per_device, ADAPTER_RANK, span)
-        up_pieces.append(lax.all_to_all(picked, "seq", split_axis=0, concat_axis=0, tiled=True))
+        received_up = lax.all_to_all(picked, "seq", split_axis=0, concat_axis=0, tiled=True)
+        up_pieces.append(pltpu.with_memory_space_constraint(received_up, pltpu.VMEM))
 
     low = jnp.sum(received.astype(jnp.float32), axis=0).astype(jnp.bfloat16)
     column = [low[ADAPTER_RANK:]]

time: 224 us -> 221 us (0.987)
  local copies, waits for them, and re-layouts: 8.22 us -> 5.5 us
    unnamed x22 -> x18, local copies, waits for them, and re-layouts: 4.15 us -> 1.43 us
where the time goes in v5:
time: 221 us; the launch traced here: 220 us
  waiting for transfers between devices  129 us (58%)
  starting transfers between devices  44.7 us (20%)
  Pallas kernels  39.4 us (18%)
  local copies, waits for them, and re-layouts  5.5 us (2%)
    ppermute x2, waiting for transfers between devices, body(): own = lax.ppermute(own, 'seq', forward)  61 us
    all_to_all x1, waiting for transfers between devices, body(): lax.all_to_all(sent, 'seq', split_axis=0, concat_axis=0, axis_index_group...  38.8 us
    pallas_call x1, Pallas kernels, attend(): pl.pallas_call(functools.partial(attend_kernel, block_len, most_blocks, p...  20.3 us
    ppermute x3, waiting for transfers between devices, body(): across = lax.ppermute(own, 'seq', swap_row)  13.8 us
    pallas_call x1, Pallas kernels, finish(): pl.pallas_call(functools.partial(finish_kernel, block_len, planes), out_s...  8.95 us
    ppermute x2, starting transfers between devices, body(): own = lax.ppermute(own, 'seq', forward)  7.18 us
    all_to_all x1, starting transfers between devices, body(): lax.all_to_all(picked, 'seq', split_axis=0, concat_axis=0, tiled=True)  7.12 us
    all_to_all x1, waiting for transfers between devices, body(): lax.all_to_all(partials, 'seq', split_axis=0, concat_axis=0, axis_index_g...  6.94 us
  transfers between devices with their start and end apart: 20, of which 8 were waited for; matrix products, arithmetic and copies ran while one was open for 2% of the time, Pallas kernels for 5%

profile of v5, /device:TPU:15, one launch (start us, length us, event | category | flops | bytes accessed | tf_op | source)
XLA Modules:
  0.0 219.9 jit_solution(1502128503189197635)
XLA Ops:
  0.0 0.0 copy-start
  0.0 2.8 %split.1 = (bf16[8,128,1024]{2,1,0:T(8,128)(2,1)}, bf16[128,2048]{1,0:T(8,128)(2,1)}) custom-call(bf16[128,8192]{1,0:T(8,128)(2,1)} %hidden_ref.1, bf16[128,1024]{1,0:T(8,128)(2,1)} %key_ref.1, bf16[128,1024]{1,0:T(8,128)(2,1)} %value_ref.1), custom_call_target="tpu_custom_call" | custom-call | tf_op jit(solution)/shard_map/split/pallas_call | solution.py:53
  2.8 5.7 %all-to-all-start = ((bf16[8,128,1024]{2,1,0:T(8,128)(2,1)}), bf16[8,128,1024]{2,1,0:T(8,128)(2,1)S(1)}, u32[]{:S(2)}, u32[]{:S(2)}) async-start(bf16[8,128,1024]{2,1,0:T(8,128)(2,1)} %get-tuple-element.7), calls=%async_computation | async-start | bytes 4194304 | tf_op jit(solution)/shard_map/all_to_all | solution.py:473
  8.4 1.2 collective-permute-start
  9.7 5.6 %collective-permute-done.other_hbm = bf16[16,192,512]{2,1,0:T(8,128)(2,1)} collective-permute-done((bf16[16,192,512]{2,1,0:T(8,128)(2,1)}, bf16[16,192,512]{2,1,0:T(8,128)(2,1)}, u32[]{:S(2)}, u32[]{:S(2)}) %collective-permute-start) | collective-permute-done | bytes 3145760 | tf_op jit(solution)/shard_map/ppermute | solution.py:478
  15.3 38.8 %all-to-all-done.rows_ref = bf16[8,128,1024]{2,1,0:T(8,128)(2,1)S(1)} async-done(((bf16[8,128,1024]{2,1,0:T(8,128)(2,1)}), bf16[8,128,1024]{2,1,0:T(8,128)(2,1)S(1)}, u32[]{:S(2)}, u32[]{:S(2)}) %all-to-all-start) | async-done | bytes 2097184 | tf_op jit(solution)/shard_map/all_to_all | solution.py:473
  54.2 0.0 copy-start.7
  54.2 0.0 copy-start.8
  54.2 5.9 %shrink.1 = bf16[8,192,128]{2,1,0:T(8,128)(2,1)} custom-call(s32[1]{0:T(128)} %bitcast.place_ref, s32[32]{0:T(128)} %request_ref.5, s32[8]{0:T(128)} %adapter_ref.3, bf16[8,128,1024]{2,1,0:T(8,128)(2,1)S(1)} %all-to-all-done.rows_ref, bf16[16,192,512]{2,1,0:T(8,128)(2,1)} %bitcast.9, bf16[16,192,512]{2,1,0:T(8,128)(2,1)} %collective-permute-done.other_hbm), custom_call_target="tpu_custom_call" | custom-call | flops 402653184 | bytes 8388608 | tf_op jit(solution)/shard_map/shrink/pallas_call | solution.py:127
  60.1 6.4 %all-to-all-start.1 = ((bf16[8,192,128]{2,1,0:T(8,128)(2,1)}), bf16[8,192,128]{2,1,0:T(8,128)(2,1)S(1)}, u32[]{:S(2)}, u32[]{:S(2)}) async-start(bf16[8,192,128]{2,1,0:T(8,128)(2,1)} %shrink.1), calls=%async_computation.1 | async-start | bytes 786432 | tf_op jit(solution)/shard_map/all_to_all | solution.py:491
  66.5 0.0 copy-done.7
  66.5 0.0 copy-done.8
  66.5 0.1 select_reduce_fusion
  66.6 0.0 copy-done
  66.6 2.0 gather_fusion
  68.6 6.9 %all-to-all-done.1 = bf16[8,192,128]{2,1,0:T(8,128)(2,1)S(1)} async-done(((bf16[8,192,128]{2,1,0:T(8,128)(2,1)}), bf16[8,192,128]{2,1,0:T(8,128)(2,1)S(1)}, u32[]{:S(2)}, u32[]{:S(2)}) %all-to-all-start.1) | async-done | bytes 393248 | tf_op jit(solution)/shard_map/all_to_all | solution.py:491
  75.5 7.1 %all-to-all-start.2 = ((bf16[16,2,64,512]{3,2,1,0:T(8,128)(2,1)}), bf16[16,2,64,512]{3,2,1,0:T(8,128)(2,1)S(1)}, u32[]{:S(2)}, u32[]{:S(2)}) async-start(bf16[16,2,64,512]{3,2,1,0:T(8,128)(2,1)} %bitcast.7), calls=%async_computation.2 | async-start | bytes 4194304 | tf_op jit(solution)/shard_map/all_to_all | solution.py:509
  82.6 3.1 %collective-permute-start.9 = (bf16[128,2048]{1,0:T(8,128)(2,1)}, bf16[128,2048]{1,0:T(8,128)(2,1)}, u32[]{:S(2)}, u32[]{:S(2)}) collective-permute-start(bf16[128,2048]{1,0:T(8,128)(2,1)} %get-tuple-element.8.rest_4_), channel_id=1, source_target_pairs={{0,4},{1,5},{2,6},{3,7},{4,8},{5,9},{6,10},{7,11},{8,12},{9,13},{1... | collective-permute-start | bytes 1572872 | tf_op jit(solution)/shard_map/ppermute | solution.py:484
  85.7 53.5 %collective-permute-done.9.rest_8_ = bf16[128,2048]{1,0:T(8,128)(2,1)} collective-permute-done((bf16[128,2048]{1,0:T(8,128)(2,1)}, bf16[128,2048]{1,0:T(8,128)(2,1)}, u32[]{:S(2)}, u32[]{:S(2)}) %collective-permute-start.9) | collective-permute-done | bytes 524320 | tf_op jit(solution)/shard_map/ppermute | solution.py:484
  139.2 4.1 %collective-permute-start.13 = (bf16[128,2048]{1,0:T(8,128)(2,1)}, bf16[128,2048]{1,0:T(8,128)(2,1)}, u32[]{:S(2)}, u32[]{:S(2)}) collective-permute-start(bf16[128,2048]{1,0:T(8,128)(2,1)} %collective-permute-done.9.rest_8_), channel_id=1, source_target_pairs={{0,4},{1,5},{2,6},{3,7},{4,8},{5,9},{6,10},{7,11},{8,12},{9,13},{1... | collective-permute-start | bytes 1572872 | tf_op jit(solution)/shard_map/ppermute | solution.py:484
  143.3 0.3 collective-permute-start.7
  143.6 1.5 collective-permute-start.6
  145.2 1.2 collective-permute-start.11
  146.4 7.5 %collective-permute-done.13.rest_12_ = bf16[128,2048]{1,0:T(8,128)(2,1)} collective-permute-done((bf16[128,2048]{1,0:T(8,128)(2,1)}, bf16[128,2048]{1,0:T(8,128)(2,1)}, u32[]{:S(2)}, u32[]{:S(2)}) %collective-permute-start.13) | collective-permute-done | bytes 524320 | tf_op jit(solution)/shard_map/ppermute | solution.py:484
  153.9 0.3 collective-permute-start.15
  154.2 2.1 collective-permute-start.10
  156.3 0.0 collective-permute-done.7.rest_6_
  156.3 3.4 %collective-permute-start.8 = (bf16[128,2048]{1,0:T(8,128)(2,1)}, bf16[128,2048]{1,0:T(8,128)(2,1)}, u32[]{:S(2)}, u32[]{:S(2)}) collective-permute-start(bf16[128,2048]{1,0:T(8,128)(2,1)} %collective-permute-done.7.rest_6_), channel_id=1, source_target_pairs={{0,1},{1,0},{2,3},{3,2},{4,5},{5,4},{6,7},{7,6},{8,9},{9,8},{10,11... | collective-permute-start | bytes 1572872 | tf_op jit(solution)/shard_map/ppermute | solution.py:487
  159.7 0.7 reduce_sum.23
  160.4 0.8 slice.11.refs_0_
  161.2 0.0 copy-start.1
  161.2 0.0 collective-permute-done.6.rest_5_
  161.2 1.9 collective-permute-start.1
  163.1 4.1 %collective-permute-done.11.rest_10_ = bf16[128,2048]{1,0:T(8,128)(2,1)} collective-permute-done((bf16[128,2048]{1,0:T(8,128)(2,1)}, bf16[128,2048]{1,0:T(8,128)(2,1)}, u32[]{:S(2)}, u32[]{:S(2)}) %collective-permute-start.11) | collective-permute-done | bytes 524320 | tf_op jit(solution)/shard_map/ppermute | solution.py:485
  167.1 1.5 collective-permute-start.2
  168.6 9.8 %collective-permute-done.15.rest_14_ = bf16[128,2048]{1,0:T(8,128)(2,1)} collective-permute-done((bf16[128,2048]{1,0:T(8,128)(2,1)}, bf16[128,2048]{1,0:T(8,128)(2,1)}, u32[]{:S(2)}, u32[]{:S(2)}) %collective-permute-start.15) | collective-permute-done | bytes 524320 | tf_op jit(solution)/shard_map/ppermute | solution.py:485
  178.4 2.1 collective-permute-start.14
  180.5 0.0 collective-permute-done.1.refs_1_
  180.5 0.1 collective-permute-start.12
  180.6 0.0 collective-permute-done.2.refs_2_
  180.6 0.4 collective-permute-start.16
  181.0 0.0 copy-done.1
  181.0 0.1 copy-done.5
  181.1 0.1 copy-done.6
  181.2 1.4 join.1.rest_0_
  182.6 0.0 collective-permute-done.10.rest_9_
  182.6 0.3 collective-permute-start.4
  182.9 0.0 collective-permute-done.8.rest_7_
  182.9 0.7 collective-permute-start.3
  183.6 3.1 %collective-permute-done.4.rest_2_ = bf16[3,128,128]{2,1,0:T(8,128)(2,1)S(1)} collective-permute-done((bf16[3,128,128]{2,1,0:T(8,128)(2,1)}, bf16[3,128,128]{2,1,0:T(8,128)(2,1)S(1)}, u32[]{:S(2)}, u32[]{:S(2)}) %collective-permute-start.4) | collective-permute-done | bytes 98336 | tf_op jit(solution)/shard_map/ppermute | solution.py:518
  186.7 1.3 collective-permute-start.5
  188.0 1.3 slice.10.low_ref
  189.4 0.0 collective-permute-done.14.rest_13_
  189.4 0.0 collective-permute-done.12.rest_11_
  189.4 0.0 collective-permute-done.16.rest_15_
  189.4 0.0 collective-permute-done.3.rest_1_
  189.4 0.0 copy-start.3
  189.4 0.0 collective-permute-done.5.rest_3_
  189.4 0.0 copy-done.2
  189.4 0.6 copy-done.3
  190.0 0.6 copy-done.4
  190.7 8.9 %finish.1.key_ref.value_ref = bf16[1536,2048]{1,0:T(8,128)(2,1)} custom-call(s32[1]{0:T(128)} %bitcast.place_ref, s32[32]{0:T(128)} %request_ref.5, s32[8]{0:T(128)} %adapter_ref.3, bf16[16,64,2048]{2,1,0:T(8,128)(2,1)} %up_ref.1, bf16[3,128,128]{2,1,0:T(8,128)(2,1)} %join.1.rest_0_, bf16[3,128,128]{2,1,0:T(8,128)(2,1)} %copy-done.3, ...), custom_call_target="tpu_custom_call" | custom-call | flops 402653184 | bytes 12582912 | tf_op jit(solution)/shard_map/finish/pallas_call | solution.py:206
  199.6 0.0 all-to-all-done.2.up_ref
  199.6 20.3 %attend.1 = bf16[128,8192]{1,0:T(8,128)(2,1)} custom-call(s32[1]{0:T(128)} %bitcast.place_ref, s32[32]{0:T(128)} %request_ref.5, bf16[128,8192]{1,0:T(8,128)(2,1)} %q_ref.1, bf16[64,128]{1,0:T(8,128)(2,1)} %slice.10.low_ref, bf16[16,2,64,512]{3,2,1,0:T(8,128)(2,1)S(1)} %all-to-all-done.2.up_ref, bf16[1536,2048]{1,0:T(8,128)(2,1)} %finish.1.key_ref.value_ref, ...), custom_call_target="tpu_custom_call" | custom-call | flops 3221225472 | bytes 16777216 | tf_op jit(solution)/shard_map/attend/pallas_call | solution.py:410
  (6 shorter events, 0.0 us)
Async XLA Ops:
  0.0 66.6 %copy-start = (bf16[16,64,512]{2,1,0:T(8,128)(2,1)S(1)}, bf16[16,64,512]{2,1,0:T(8,128)(2,1)}, u32[]{:S(2)}) copy-start(bf16[16,64,512]{2,1,0:T(8,128)(2,1)} %param.14) | copy-start | bytes 3145732
  2.8 51.4 %all-to-all-start = ((bf16[8,128,1024]{2,1,0:T(8,128)(2,1)}), bf16[8,128,1024]{2,1,0:T(8,128)(2,1)S(1)}, u32[]{:S(2)}, u32[]{:S(2)}) async-start(bf16[8,128,1024]{2,1,0:T(8,128)(2,1)} %get-tuple-element.7), calls=%async_computation | async-start | bytes 4194304 | tf_op jit(solution)/shard_map/all_to_all | solution.py:473
  8.4 6.9 %collective-permute-start = (bf16[16,192,512]{2,1,0:T(8,128)(2,1)}, bf16[16,192,512]{2,1,0:T(8,128)(2,1)}, u32[]{:S(2)}, u32[]{:S(2)}) collective-permute-start(bf16[16,192,512]{2,1,0:T(8,128)(2,1)} %bitcast.8), channel_id=1, source_target_pairs={{0,1},{1,0},{2,3},{3,2},{4,5},{5,4},{6,7},{7,6},{8,9},{9,8},{10,11... | collective-permute-start | bytes 9437192 | tf_op jit(solution)/shard_map/ppermute | solution.py:478
  54.2 12.3 %copy-start.7 = (s32[32]{0:T(128)S(1)}, s32[32]{0:T(128)}, u32[]{:S(2)}) copy-start(s32[32]{0:T(128)} %request_ref.5) | copy-start | bytes 388
  54.2 12.3 %copy-start.8 = (s32[8]{0:T(128)S(1)}, s32[8]{0:T(128)}, u32[]{:S(2)}) copy-start(s32[8]{0:T(128)} %adapter_ref.3) | copy-start | bytes 100
  60.1 15.4 %all-to-all-start.1 = ((bf16[8,192,128]{2,1,0:T(8,128)(2,1)}), bf16[8,192,128]{2,1,0:T(8,128)(2,1)S(1)}, u32[]{:S(2)}, u32[]{:S(2)}) async-start(bf16[8,192,128]{2,1,0:T(8,128)(2,1)} %shrink.1), calls=%async_computation.1 | async-start | bytes 786432 | tf_op jit(solution)/shard_map/all_to_all | solution.py:491
  75.5 124.1 %all-to-all-start.2 = ((bf16[16,2,64,512]{3,2,1,0:T(8,128)(2,1)}), bf16[16,2,64,512]{3,2,1,0:T(8,128)(2,1)S(1)}, u32[]{:S(2)}, u32[]{:S(2)}) async-start(bf16[16,2,64,512]{3,2,1,0:T(8,128)(2,1)} %bitcast.7), calls=%async_computation.2 | async-start | bytes 4194304 | tf_op jit(solution)/shard_map/all_to_all | solution.py:509
  82.6 56.6 %collective-permute-start.9 = (bf16[128,2048]{1,0:T(8,128)(2,1)}, bf16[128,2048]{1,0:T(8,128)(2,1)}, u32[]{:S(2)}, u32[]{:S(2)}) collective-permute-start(bf16[128,2048]{1,0:T(8,128)(2,1)} %get-tuple-element.8.rest_4_), channel_id=1, source_target_pairs={{0,4},{1,5},{2,6},{3,7},{4,8},{5,9},{6,10},{7,11},{8,12},{9,13},{1... | collective-permute-start | bytes 1572872 | tf_op jit(solution)/shard_map/ppermute | solution.py:484
  139.2 14.7 %collective-permute-start.13 = (bf16[128,2048]{1,0:T(8,128)(2,1)}, bf16[128,2048]{1,0:T(8,128)(2,1)}, u32[]{:S(2)}, u32[]{:S(2)}) collective-permute-start(bf16[128,2048]{1,0:T(8,128)(2,1)} %collective-permute-done.9.rest_8_), channel_id=1, source_target_pairs={{0,4},{1,5},{2,6},{3,7},{4,8},{5,9},{6,10},{7,11},{8,12},{9,13},{1... | collective-permute-start | bytes 1572872 | tf_op jit(solution)/shard_map/ppermute | solution.py:484
  143.3 13.0 %collective-permute-start.7 = (bf16[128,2048]{1,0:T(8,128)(2,1)}, bf16[128,2048]{1,0:T(8,128)(2,1)}, u32[]{:S(2)}, u32[]{:S(2)}) collective-permute-start(bf16[128,2048]{1,0:T(8,128)(2,1)} %get-tuple-element.8.rest_4_), channel_id=1, source_target_pairs={{0,2},{1,3},{2,0},{3,1},{4,6},{5,7},{6,4},{7,5},{8,10},{9,11},{10,... | collective-permute-start | bytes 1572872 | tf_op jit(solution)/shard_map/ppermute | solution.py:485
  143.6 17.5 %collective-permute-start.6 = (bf16[128,2048]{1,0:T(8,128)(2,1)}, bf16[128,2048]{1,0:T(8,128)(2,1)}, u32[]{:S(2)}, u32[]{:S(2)}) collective-permute-start(bf16[128,2048]{1,0:T(8,128)(2,1)} %get-tuple-element.8.rest_4_), channel_id=1, source_target_pairs={{0,1},{1,0},{2,3},{3,2},{4,5},{5,4},{6,7},{7,6},{8,9},{9,8},{10,11... | collective-permute-start | bytes 1572872 | tf_op jit(solution)/shard_map/ppermute | solution.py:486
  145.2 22.0 %collective-permute-start.11 = (bf16[128,2048]{1,0:T(8,128)(2,1)}, bf16[128,2048]{1,0:T(8,128)(2,1)}, u32[]{:S(2)}, u32[]{:S(2)}) collective-permute-start(bf16[128,2048]{1,0:T(8,128)(2,1)} %collective-permute-done.9.rest_8_), channel_id=1, source_target_pairs={{0,2},{1,3},{2,0},{3,1},{4,6},{5,7},{6,4},{7,5},{8,10},{9,11},{10,... | collective-permute-start | bytes 1572872 | tf_op jit(solution)/shard_map/ppermute | solution.py:485
  153.9 24.5 %collective-permute-start.15 = (bf16[128,2048]{1,0:T(8,128)(2,1)}, bf16[128,2048]{1,0:T(8,128)(2,1)}, u32[]{:S(2)}, u32[]{:S(2)}) collective-permute-start(bf16[128,2048]{1,0:T(8,128)(2,1)} %collective-permute-done.13.rest_12_), channel_id=1, source_target_pairs={{0,2},{1,3},{2,0},{3,1},{4,6},{5,7},{6,4},{7,5},{8,10},{9,11},{10,... | collective-permute-start | bytes 1572872 | tf_op jit(solution)/shard_map/ppermute | solution.py:485
  154.2 28.4 %collective-permute-start.10 = (bf16[128,2048]{1,0:T(8,128)(2,1)}, bf16[128,2048]{1,0:T(8,128)(2,1)}, u32[]{:S(2)}, u32[]{:S(2)}) collective-permute-start(bf16[128,2048]{1,0:T(8,128)(2,1)} %collective-permute-done.9.rest_8_), channel_id=1, source_target_pairs={{0,1},{1,0},{2,3},{3,2},{4,5},{5,4},{6,7},{7,6},{8,9},{9,8},{10,11... | collective-permute-start | bytes 1572872 | tf_op jit(solution)/shard_map/ppermute | solution.py:486
  156.3 26.6 %collective-permute-start.8 = (bf16[128,2048]{1,0:T(8,128)(2,1)}, bf16[128,2048]{1,0:T(8,128)(2,1)}, u32[]{:S(2)}, u32[]{:S(2)}) collective-permute-start(bf16[128,2048]{1,0:T(8,128)(2,1)} %collective-permute-done.7.rest_6_), channel_id=1, source_target_pairs={{0,1},{1,0},{2,3},{3,2},{4,5},{5,4},{6,7},{7,6},{8,9},{9,8},{10,11... | collective-permute-start | bytes 1572872 | tf_op jit(solution)/shard_map/ppermute | solution.py:487
  161.2 19.9 %copy-start.1 = (bf16[128,128]{1,0:T(8,128)(2,1)}, bf16[128,128]{1,0:T(8,128)(2,1)S(1)}, u32[]{:S(2)}) copy-start(bf16[128,128]{1,0:T(8,128)(2,1)S(1)} %slice.11.refs_0_) | copy-start | bytes 98308
  161.2 19.3 %collective-permute-start.1 = (bf16[128,128]{1,0:T(8,128)(2,1)S(1)}, bf16[128,128]{1,0:T(8,128)(2,1)S(1)}, u32[]{:S(2)}, u32[]{:S(2)}) collective-permute-start(bf16[128,128]{1,0:T(8,128)(2,1)S(1)} %slice.11.refs_0_), channel_id=1, source_target_pairs={{0,4},{1,5},{2,6},{3,7},{4,8},{5,9},{6,10},{7,11},{8,12},{9,13},{1... | collective-permute-start | bytes 98312 | tf_op jit(solution)/shard_map/ppermute | solution.py:516
  167.1 13.4 %collective-permute-start.2 = (bf16[128,128]{1,0:T(8,128)(2,1)S(1)}, bf16[128,128]{1,0:T(8,128)(2,1)S(1)}, u32[]{:S(2)}, u32[]{:S(2)}) collective-permute-start(bf16[128,128]{1,0:T(8,128)(2,1)S(1)} %slice.11.refs_0_), channel_id=1, source_target_pairs={{0,8},{1,9},{2,10},{3,11},{4,12},{5,13},{6,14},{7,15},{16,24},{17,... | collective-permute-start | bytes 98312 | tf_op jit(solution)/shard_map/ppermute | solution.py:516
  178.4 11.0 %collective-permute-start.14 = (bf16[128,2048]{1,0:T(8,128)(2,1)}, bf16[128,2048]{1,0:T(8,128)(2,1)}, u32[]{:S(2)}, u32[]{:S(2)}) collective-permute-start(bf16[128,2048]{1,0:T(8,128)(2,1)} %collective-permute-done.13.rest_12_), channel_id=1, source_target_pairs={{0,1},{1,0},{2,3},{3,2},{4,5},{5,4},{6,7},{7,6},{8,9},{9,8},{10,11... | collective-permute-start | bytes 1572872 | tf_op jit(solution)/shard_map/ppermute | solution.py:486
  180.5 0.6 copy-start.5
  180.5 8.9 %collective-permute-start.12 = (bf16[128,2048]{1,0:T(8,128)(2,1)}, bf16[128,2048]{1,0:T(8,128)(2,1)}, u32[]{:S(2)}, u32[]{:S(2)}) collective-permute-start(bf16[128,2048]{1,0:T(8,128)(2,1)} %collective-permute-done.11.rest_10_), channel_id=1, source_target_pairs={{0,1},{1,0},{2,3},{3,2},{4,5},{5,4},{6,7},{7,6},{8,9},{9,8},{10,11... | collective-permute-start | bytes 1572872 | tf_op jit(solution)/shard_map/ppermute | solution.py:487
  180.6 0.6 copy-start.6
  180.6 8.8 %collective-permute-start.16 = (bf16[128,2048]{1,0:T(8,128)(2,1)}, bf16[128,2048]{1,0:T(8,128)(2,1)}, u32[]{:S(2)}, u32[]{:S(2)}) collective-permute-start(bf16[128,2048]{1,0:T(8,128)(2,1)} %collective-permute-done.15.rest_14_), channel_id=1, source_target_pairs={{0,1},{1,0},{2,3},{3,2},{4,5},{5,4},{6,7},{7,6},{8,9},{9,8},{10,11... | collective-permute-start | bytes 1572872 | tf_op jit(solution)/shard_map/ppermute | solution.py:487
  182.6 4.1 %collective-permute-start.4 = (bf16[3,128,128]{2,1,0:T(8,128)(2,1)}, bf16[3,128,128]{2,1,0:T(8,128)(2,1)S(1)}, u32[]{:S(2)}, u32[]{:S(2)}) collective-permute-start(bf16[3,128,128]{2,1,0:T(8,128)(2,1)} %join.1.rest_0_), channel_id=1, source_target_pairs={{0,2},{1,3},{2,0},{3,1},{4,6},{5,7},{6,4},{7,5},{8,10},{9,11},{10,... | collective-permute-start | bytes 294920 | tf_op jit(solution)/shard_map/ppermute | solution.py:518
  182.9 6.5 %collective-permute-start.3 = (bf16[3,128,128]{2,1,0:T(8,128)(2,1)}, bf16[3,128,128]{2,1,0:T(8,128)(2,1)S(1)}, u32[]{:S(2)}, u32[]{:S(2)}) collective-permute-start(bf16[3,128,128]{2,1,0:T(8,128)(2,1)} %join.1.rest_0_), channel_id=1, source_target_pairs={{0,1},{1,0},{2,3},{3,2},{4,5},{5,4},{6,7},{7,6},{8,9},{9,8},{10,11... | collective-permute-start | bytes 294920 | tf_op jit(solution)/shard_map/ppermute | solution.py:519
  186.7 2.7 %copy-start.2 = (bf16[3,128,128]{2,1,0:T(8,128)(2,1)}, bf16[3,128,128]{2,1,0:T(8,128)(2,1)S(1)}, u32[]{:S(2)}) copy-start(bf16[3,128,128]{2,1,0:T(8,128)(2,1)S(1)} %collective-permute-done.4.rest_2_) | copy-start | bytes 294916
  186.7 2.6 %collective-permute-start.5 = (bf16[3,128,128]{2,1,0:T(8,128)(2,1)S(1)}, bf16[3,128,128]{2,1,0:T(8,128)(2,1)S(1)}, u32[]{:S(2)}, u32[]{:S(2)}) collective-permute-start(bf16[3,128,128]{2,1,0:T(8,128)(2,1)S(1)} %collective-permute-done.4.rest_2_), channel_id=1, source_target_pairs={{0,1},{1,0},{2,3},{3,2},{4,5},{5,4},{6,7},{7,6},{8,9},{9,8},{10,11... | collective-permute-start | bytes 294920 | tf_op jit(solution)/shard_map/ppermute | solution.py:520
  189.4 0.6 copy-start.3
  190.0 0.6 copy-start.4

commit v6 on v5

--- a/solution.py
+++ b/solution.py
@@ -159,13 +159,13 @@
     )(*parts)
 
 
-def finish_kernel(block_len, planes, place_ref, request_ref, adapter_ref, up_ref, *rest):
+def finish_kernel(block_len, planes, per_device, place_ref, request_ref, adapter_ref, *rest):
     pieces = planes * PLANE
+    up_refs, rest = rest[:per_device], rest[per_device:]
     low_refs, rest = rest[:PLANE], rest[PLANE:]
     piece_refs = rest[:pieces]
     out_ref, base_ref, done_ref, in_sems, out_sems = rest[pieces:]
     tokens = piece_refs[0].shape[0]
-    per_device = tokens // block_len
     rank = ADAPTER_RANK
     width = base_ref.shape[2] // 2
     me = place_ref[0]
@@ -179,13 +179,12 @@
         pltpu.make_async_copy(piece_refs[index], base_ref.at[index], in_sems.at[index]).wait()
         spans = [(0, tokens)] if index else [(part * block_len, block_len) for part in range(per_device)]
         for part, (at, length) in enumerate(spans):
-            adapter = adapter_ref[request_ref[me * per_device + part]]
             span = pl.ds(at, length)
             for which in range(2):
                 columns = pl.ds(which * width, width)
                 delta = lax.dot_general(
                     low_ref[back, pl.ds(which * rank, rank), span],
-                    up_ref[adapter, :, columns],
+                    up_refs[part][0, :, columns],
                     TN,
                     preferred_element_type=jnp.float32,
                 )
@@ -204,13 +203,17 @@
     tokens, width = pieces[0].shape
     count = len(pieces)
     return pl.pallas_call(
-        functools.partial(finish_kernel, block_len, planes),
+        functools.partial(finish_kernel, block_len, planes, tokens // block_len),
         out_shape=jax.ShapeDtypeStruct((count * tokens, width), jnp.bfloat16),
         grid_spec=pltpu.PrefetchScalarGridSpec(
             num_scalar_prefetch=3,
             grid=(1,),
             in_specs=[
-                pl.BlockSpec(up_weight.shape, lambda i, me, br, ra: (0, 0, 0)),
+                pl.BlockSpec(
+                    (1, ADAPTER_RANK, width),
+                    lambda i, me, br, ra, part=part: (ra[br[me[0] * (tokens // block_len) + part]], 0, 0),
+                )
+                for part in range(tokens // block_len)
             ]
             + [pl.BlockSpec(lows[0].shape, lambda i, me, br, ra: (0, 0, 0))] * PLANE
             + [pl.BlockSpec(memory_space=pl.ANY)] * count,
@@ -226,7 +229,7 @@
             flops=2 * count * tokens * width * ADAPTER_RANK, bytes_accessed=4 * count * tokens * width, transcendentals=0
         ),
         name="finish",
-    )(place, block_request, request_adapter, up_weight, *lows, *pieces)
+    )(place, block_request, request_adapter, *[up_weight] * (tokens // block_len), *lows, *pieces)
 
 
 def attend_kernel(

time: 221 us -> 219 us (level)
  transfers between devices with their start and end apart: 20 -> 20, of which waited for: 8 -> 8; matrix products, arithmetic and copies ran while one was open for 2% -> 2% of each run, Pallas kernels for 5% -> 4%
where the time goes in v6:
time: 219 us
  waiting for transfers between devices  129 us (59%)
  starting transfers between devices  44.7 us (20%)
  Pallas kernels  38.2 us (17%)
  local copies, waits for them, and re-layouts  5.5 us (3%)
    ppermute x2, waiting for transfers between devices, body(): own = lax.ppermute(own, 'seq', forward)  61 us
    all_to_all x1, waiting for transfers between devices, body(): lax.all_to_all(sent, 'seq', split_axis=0, concat_axis=0, axis_index_group...  38.8 us
    pallas_call x1, Pallas kernels, attend(): pl.pallas_call(functools.partial(attend_kernel, block_len, most_blocks, p...  20.3 us
    ppermute x3, waiting for transfers between devices, body(): across = lax.ppermute(own, 'seq', swap_row)  13.8 us
    pallas_call x1, Pallas kernels, finish(): pl.pallas_call(functools.partial(finish_kernel, block_len, planes, tokens...  7.78 us
    ppermute x2, starting transfers between devices, body(): own = lax.ppermute(own, 'seq', forward)  7.18 us
    all_to_all x1, starting transfers between devices, body(): lax.all_to_all(picked, 'seq', split_axis=0, concat_axis=0, tiled=True)  7.12 us
    all_to_all x1, waiting for transfers between devices, body(): lax.all_to_all(partials, 'seq', split_axis=0, concat_axis=0, axis_index_g...  6.94 us
  transfers between devices with their start and end apart: 20, of which 8 were waited for; matrix products, arithmetic and copies ran while one was open for 2% of the time, Pallas kernels for 4%

profile of v6, /device:TPU:15, one launch (start us, length us, event | category | flops | bytes accessed | tf_op | source)
XLA Modules:
  0.0 218.8 jit_solution(13713584606631612049)
XLA Ops:
  0.0 0.0 copy-start
  0.0 2.8 %split.1 = (bf16[8,128,1024]{2,1,0:T(8,128)(2,1)}, bf16[128,2048]{1,0:T(8,128)(2,1)}) custom-call(bf16[128,8192]{1,0:T(8,128)(2,1)} %hidden_ref.1, bf16[128,1024]{1,0:T(8,128)(2,1)} %key_ref.1, bf16[128,1024]{1,0:T(8,128)(2,1)} %value_ref.1), custom_call_target="tpu_custom_call" | custom-call | tf_op jit(solution)/shard_map/split/pallas_call | solution.py:53
  2.8 5.7 %all-to-all-start = ((bf16[8,128,1024]{2,1,0:T(8,128)(2,1)}), bf16[8,128,1024]{2,1,0:T(8,128)(2,1)S(1)}, u32[]{:S(2)}, u32[]{:S(2)}) async-start(bf16[8,128,1024]{2,1,0:T(8,128)(2,1)} %get-tuple-element.7), calls=%async_computation | async-start | bytes 4194304 | tf_op jit(solution)/shard_map/all_to_all | solution.py:476
  8.4 1.2 collective-permute-start
  9.7 5.6 %collective-permute-done.other_hbm = bf16[16,192,512]{2,1,0:T(8,128)(2,1)} collective-permute-done((bf16[16,192,512]{2,1,0:T(8,128)(2,1)}, bf16[16,192,512]{2,1,0:T(8,128)(2,1)}, u32[]{:S(2)}, u32[]{:S(2)}) %collective-permute-start) | collective-permute-done | bytes 3145760 | tf_op jit(solution)/shard_map/ppermute | solution.py:481
  15.3 38.8 %all-to-all-done.rows_ref = bf16[8,128,1024]{2,1,0:T(8,128)(2,1)S(1)} async-done(((bf16[8,128,1024]{2,1,0:T(8,128)(2,1)}), bf16[8,128,1024]{2,1,0:T(8,128)(2,1)S(1)}, u32[]{:S(2)}, u32[]{:S(2)}) %all-to-all-start) | async-done | bytes 2097184 | tf_op jit(solution)/shard_map/all_to_all | solution.py:476
  54.2 0.0 copy-start.7
  54.2 0.0 copy-start.8
  54.2 5.9 %shrink.1 = bf16[8,192,128]{2,1,0:T(8,128)(2,1)} custom-call(s32[1]{0:T(128)} %bitcast.place_ref, s32[32]{0:T(128)} %request_ref.5, s32[8]{0:T(128)} %adapter_ref.3, bf16[8,128,1024]{2,1,0:T(8,128)(2,1)S(1)} %all-to-all-done.rows_ref, bf16[16,192,512]{2,1,0:T(8,128)(2,1)} %bitcast.9, bf16[16,192,512]{2,1,0:T(8,128)(2,1)} %collective-permute-done.other_hbm), custom_call_target="tpu_custom_call" | custom-call | flops 402653184 | bytes 8388608 | tf_op jit(solution)/shard_map/shrink/pallas_call | solution.py:127
  60.1 6.4 %all-to-all-start.1 = ((bf16[8,192,128]{2,1,0:T(8,128)(2,1)}), bf16[8,192,128]{2,1,0:T(8,128)(2,1)S(1)}, u32[]{:S(2)}, u32[]{:S(2)}) async-start(bf16[8,192,128]{2,1,0:T(8,128)(2,1)} %shrink.1), calls=%async_computation.1 | async-start | bytes 786432 | tf_op jit(solution)/shard_map/all_to_all | solution.py:494
  66.5 0.0 copy-done.7
  66.5 0.0 copy-done.8
  66.5 0.1 select_reduce_fusion
  66.6 0.0 copy-done
  66.6 2.0 gather_fusion
  68.6 6.9 %all-to-all-done.1 = bf16[8,192,128]{2,1,0:T(8,128)(2,1)S(1)} async-done(((bf16[8,192,128]{2,1,0:T(8,128)(2,1)}), bf16[8,192,128]{2,1,0:T(8,128)(2,1)S(1)}, u32[]{:S(2)}, u32[]{:S(2)}) %all-to-all-start.1) | async-done | bytes 393248 | tf_op jit(solution)/shard_map/all_to_all | solution.py:494
  75.5 7.1 %all-to-all-start.2 = ((bf16[16,2,64,512]{3,2,1,0:T(8,128)(2,1)}), bf16[16,2,64,512]{3,2,1,0:T(8,128)(2,1)S(1)}, u32[]{:S(2)}, u32[]{:S(2)}) async-start(bf16[16,2,64,512]{3,2,1,0:T(8,128)(2,1)} %bitcast.7), calls=%async_computation.2 | async-start | bytes 4194304 | tf_op jit(solution)/shard_map/all_to_all | solution.py:512
  82.6 3.1 %collective-permute-start.9 = (bf16[128,2048]{1,0:T(8,128)(2,1)}, bf16[128,2048]{1,0:T(8,128)(2,1)}, u32[]{:S(2)}, u32[]{:S(2)}) collective-permute-start(bf16[128,2048]{1,0:T(8,128)(2,1)} %get-tuple-element.8.rest_6_), channel_id=1, source_target_pairs={{0,4},{1,5},{2,6},{3,7},{4,8},{5,9},{6,10},{7,11},{8,12},{9,13},{1... | collective-permute-start | bytes 1572872 | tf_op jit(solution)/shard_map/ppermute | solution.py:487
  85.7 53.5 %collective-permute-done.9.rest_10_ = bf16[128,2048]{1,0:T(8,128)(2,1)} collective-permute-done((bf16[128,2048]{1,0:T(8,128)(2,1)}, bf16[128,2048]{1,0:T(8,128)(2,1)}, u32[]{:S(2)}, u32[]{:S(2)}) %collective-permute-start.9) | collective-permute-done | bytes 524320 | tf_op jit(solution)/shard_map/ppermute | solution.py:487
  139.2 4.1 %collective-permute-start.13 = (bf16[128,2048]{1,0:T(8,128)(2,1)}, bf16[128,2048]{1,0:T(8,128)(2,1)}, u32[]{:S(2)}, u32[]{:S(2)}) collective-permute-start(bf16[128,2048]{1,0:T(8,128)(2,1)} %collective-permute-done.9.rest_10_), channel_id=1, source_target_pairs={{0,4},{1,5},{2,6},{3,7},{4,8},{5,9},{6,10},{7,11},{8,12},{9,13},{1... | collective-permute-start | bytes 1572872 | tf_op jit(solution)/shard_map/ppermute | solution.py:487
  143.3 0.3 collective-permute-start.7
  143.6 1.5 collective-permute-start.6
  145.2 1.2 collective-permute-start.11
  146.4 7.5 %collective-permute-done.13.rest_14_ = bf16[128,2048]{1,0:T(8,128)(2,1)} collective-permute-done((bf16[128,2048]{1,0:T(8,128)(2,1)}, bf16[128,2048]{1,0:T(8,128)(2,1)}, u32[]{:S(2)}, u32[]{:S(2)}) %collective-permute-start.13) | collective-permute-done | bytes 524320 | tf_op jit(solution)/shard_map/ppermute | solution.py:487
  153.9 0.3 collective-permute-start.15
  154.2 2.1 collective-permute-start.10
  156.3 0.0 collective-permute-done.7.rest_8_
  156.3 3.4 %collective-permute-start.8 = (bf16[128,2048]{1,0:T(8,128)(2,1)}, bf16[128,2048]{1,0:T(8,128)(2,1)}, u32[]{:S(2)}, u32[]{:S(2)}) collective-permute-start(bf16[128,2048]{1,0:T(8,128)(2,1)} %collective-permute-done.7.rest_8_), channel_id=1, source_target_pairs={{0,1},{1,0},{2,3},{3,2},{4,5},{5,4},{6,7},{7,6},{8,9},{9,8},{10,11... | collective-permute-start | bytes 1572872 | tf_op jit(solution)/shard_map/ppermute | solution.py:490
  159.7 0.7 reduce_sum.23
  160.4 0.8 slice.11.refs_0_
  161.2 0.0 copy-start.1
  161.2 0.0 collective-permute-done.6.rest_7_
  161.2 1.9 collective-permute-start.1
  163.1 4.1 %collective-permute-done.11.rest_12_ = bf16[128,2048]{1,0:T(8,128)(2,1)} collective-permute-done((bf16[128,2048]{1,0:T(8,128)(2,1)}, bf16[128,2048]{1,0:T(8,128)(2,1)}, u32[]{:S(2)}, u32[]{:S(2)}) %collective-permute-start.11) | collective-permute-done | bytes 524320 | tf_op jit(solution)/shard_map/ppermute | solution.py:488
  167.1 1.5 collective-permute-start.2
  168.6 9.8 %collective-permute-done.15.rest_16_ = bf16[128,2048]{1,0:T(8,128)(2,1)} collective-permute-done((bf16[128,2048]{1,0:T(8,128)(2,1)}, bf16[128,2048]{1,0:T(8,128)(2,1)}, u32[]{:S(2)}, u32[]{:S(2)}) %collective-permute-start.15) | collective-permute-done | bytes 524320 | tf_op jit(solution)/shard_map/ppermute | solution.py:488
  178.4 2.1 collective-permute-start.14
  180.5 0.0 collective-permute-done.1.refs_1_
  180.5 0.1 collective-permute-start.12
  180.6 0.0 collective-permute-done.2.refs_2_
  180.6 0.4 collective-permute-start.16
  181.0 0.0 copy-done.1
  181.0 0.1 copy-done.5
  181.1 0.1 copy-done.6
  181.2 1.4 join.1.rest_2_
  182.6 0.0 collective-permute-done.10.rest_11_
  182.6 0.3 collective-permute-start.4
  182.9 0.0 collective-permute-done.8.rest_9_
  182.9 0.7 collective-permute-start.3
  183.6 3.1 %collective-permute-done.4.rest_4_ = bf16[3,128,128]{2,1,0:T(8,128)(2,1)S(1)} collective-permute-done((bf16[3,128,128]{2,1,0:T(8,128)(2,1)}, bf16[3,128,128]{2,1,0:T(8,128)(2,1)S(1)}, u32[]{:S(2)}, u32[]{:S(2)}) %collective-permute-start.4) | collective-permute-done | bytes 98336 | tf_op jit(solution)/shard_map/ppermute | solution.py:521
  186.7 1.3 collective-permute-start.5
  188.0 1.3 slice.10.low_ref
  189.4 0.0 collective-permute-done.14.rest_15_
  189.4 0.0 collective-permute-done.12.rest_13_
  189.4 0.0 collective-permute-done.16.rest_17_
  189.4 0.0 collective-permute-done.3.rest_3_
  189.4 0.0 copy-start.3
  189.4 0.0 collective-permute-done.5.rest_5_
  189.4 0.0 copy-done.2
  189.4 0.6 copy-done.3
  190.0 0.6 copy-done.4
  190.7 7.8 %finish.1.key_ref.value_ref = bf16[1536,2048]{1,0:T(8,128)(2,1)} custom-call(s32[1]{0:T(128)} %bitcast.place_ref, s32[32]{0:T(128)} %request_ref.5, s32[8]{0:T(128)} %adapter_ref.3, bf16[16,64,2048]{2,1,0:T(8,128)(2,1)} %rest_1_.1, bf16[16,64,2048]{2,1,0:T(8,128)(2,1)} %rest_1_.1, bf16[3,128,128]{2,1,0:T(8,128)(2,1)} %join.1.rest_2_, ...), custom_call_target="tpu_custom_call" | custom-call | flops 402653184 | bytes 12582912 | tf_op jit(solution)/shard_map/finish/pallas_call | solution.py:205
  198.4 0.0 all-to-all-done.2.up_ref
  198.5 20.3 %attend.1 = bf16[128,8192]{1,0:T(8,128)(2,1)} custom-call(s32[1]{0:T(128)} %bitcast.place_ref, s32[32]{0:T(128)} %request_ref.5, bf16[128,8192]{1,0:T(8,128)(2,1)} %q_ref.1, bf16[64,128]{1,0:T(8,128)(2,1)} %slice.10.low_ref, bf16[16,2,64,512]{3,2,1,0:T(8,128)(2,1)S(1)} %all-to-all-done.2.up_ref, bf16[1536,2048]{1,0:T(8,128)(2,1)} %finish.1.key_ref.value_ref, ...), custom_call_target="tpu_custom_call" | custom-call | flops 3221225472 | bytes 16777216 | tf_op jit(solution)/shard_map/attend/pallas_call | solution.py:413
  (6 shorter events, 0.0 us)
Async XLA Ops:
  0.0 66.6 %copy-start = (bf16[16,64,512]{2,1,0:T(8,128)(2,1)S(1)}, bf16[16,64,512]{2,1,0:T(8,128)(2,1)}, u32[]{:S(2)}) copy-start(bf16[16,64,512]{2,1,0:T(8,128)(2,1)} %param.14) | copy-start | bytes 3145732
  2.8 51.4 %all-to-all-start = ((bf16[8,128,1024]{2,1,0:T(8,128)(2,1)}), bf16[8,128,1024]{2,1,0:T(8,128)(2,1)S(1)}, u32[]{:S(2)}, u32[]{:S(2)}) async-start(bf16[8,128,1024]{2,1,0:T(8,128)(2,1)} %get-tuple-element.7), calls=%async_computation | async-start | bytes 4194304 | tf_op jit(solution)/shard_map/all_to_all | solution.py:476
  8.4 6.9 %collective-permute-start = (bf16[16,192,512]{2,1,0:T(8,128)(2,1)}, bf16[16,192,512]{2,1,0:T(8,128)(2,1)}, u32[]{:S(2)}, u32[]{:S(2)}) collective-permute-start(bf16[16,192,512]{2,1,0:T(8,128)(2,1)} %bitcast.8), channel_id=1, source_target_pairs={{0,1},{1,0},{2,3},{3,2},{4,5},{5,4},{6,7},{7,6},{8,9},{9,8},{10,11... | collective-permute-start | bytes 9437192 | tf_op jit(solution)/shard_map/ppermute | solution.py:481
  54.2 12.3 %copy-start.7 = (s32[32]{0:T(128)S(1)}, s32[32]{0:T(128)}, u32[]{:S(2)}) copy-start(s32[32]{0:T(128)} %request_ref.5) | copy-start | bytes 388
  54.2 12.3 %copy-start.8 = (s32[8]{0:T(128)S(1)}, s32[8]{0:T(128)}, u32[]{:S(2)}) copy-start(s32[8]{0:T(128)} %adapter_ref.3) | copy-start | bytes 100
  60.1 15.4 %all-to-all-start.1 = ((bf16[8,192,128]{2,1,0:T(8,128)(2,1)}), bf16[8,192,128]{2,1,0:T(8,128)(2,1)S(1)}, u32[]{:S(2)}, u32[]{:S(2)}) async-start(bf16[8,192,128]{2,1,0:T(8,128)(2,1)} %shrink.1), calls=%async_computation.1 | async-start | bytes 786432 | tf_op jit(solution)/shard_map/all_to_all | solution.py:494
  75.5 122.9 %all-to-all-start.2 = ((bf16[16,2,64,512]{3,2,1,0:T(8,128)(2,1)}), bf16[16,2,64,512]{3,2,1,0:T(8,128)(2,1)S(1)}, u32[]{:S(2)}, u32[]{:S(2)}) async-start(bf16[16,2,64,512]{3,2,1,0:T(8,128)(2,1)} %bitcast.7), calls=%async_computation.2 | async-start | bytes 4194304 | tf_op jit(solution)/shard_map/all_to_all | solution.py:512
  82.6 56.6 %collective-permute-start.9 = (bf16[128,2048]{1,0:T(8,128)(2,1)}, bf16[128,2048]{1,0:T(8,128)(2,1)}, u32[]{:S(2)}, u32[]{:S(2)}) collective-permute-start(bf16[128,2048]{1,0:T(8,128)(2,1)} %get-tuple-element.8.rest_6_), channel_id=1, source_target_pairs={{0,4},{1,5},{2,6},{3,7},{4,8},{5,9},{6,10},{7,11},{8,12},{9,13},{1... | collective-permute-start | bytes 1572872 | tf_op jit(solution)/shard_map/ppermute | solution.py:487
  139.2 14.7 %collective-permute-start.13 = (bf16[128,2048]{1,0:T(8,128)(2,1)}, bf16[128,2048]{1,0:T(8,128)(2,1)}, u32[]{:S(2)}, u32[]{:S(2)}) collective-permute-start(bf16[128,2048]{1,0:T(8,128)(2,1)} %collective-permute-done.9.rest_10_), channel_id=1, source_target_pairs={{0,4},{1,5},{2,6},{3,7},{4,8},{5,9},{6,10},{7,11},{8,12},{9,13},{1... | collective-permute-start | bytes 1572872 | tf_op jit(solution)/shard_map/ppermute | solution.py:487
  143.3 13.0 %collective-permute-start.7 = (bf16[128,2048]{1,0:T(8,128)(2,1)}, bf16[128,2048]{1,0:T(8,128)(2,1)}, u32[]{:S(2)}, u32[]{:S(2)}) collective-permute-start(bf16[128,2048]{1,0:T(8,128)(2,1)} %get-tuple-element.8.rest_6_), channel_id=1, source_target_pairs={{0,2},{1,3},{2,0},{3,1},{4,6},{5,7},{6,4},{7,5},{8,10},{9,11},{10,... | collective-permute-start | bytes 1572872 | tf_op jit(solution)/shard_map/ppermute | solution.py:488
  143.6 17.5 %collective-permute-start.6 = (bf16[128,2048]{1,0:T(8,128)(2,1)}, bf16[128,2048]{1,0:T(8,128)(2,1)}, u32[]{:S(2)}, u32[]{:S(2)}) collective-permute-start(bf16[128,2048]{1,0:T(8,128)(2,1)} %get-tuple-element.8.rest_6_), channel_id=1, source_target_pairs={{0,1},{1,0},{2,3},{3,2},{4,5},{5,4},{6,7},{7,6},{8,9},{9,8},{10,11... | collective-permute-start | bytes 1572872 | tf_op jit(solution)/shard_map/ppermute | solution.py:489
  145.2 22.0 %collective-permute-start.11 = (bf16[128,2048]{1,0:T(8,128)(2,1)}, bf16[128,2048]{1,0:T(8,128)(2,1)}, u32[]{:S(2)}, u32[]{:S(2)}) collective-permute-start(bf16[128,2048]{1,0:T(8,128)(2,1)} %collective-permute-done.9.rest_10_), channel_id=1, source_target_pairs={{0,2},{1,3},{2,0},{3,1},{4,6},{5,7},{6,4},{7,5},{8,10},{9,11},{10,... | collective-permute-start | bytes 1572872 | tf_op jit(solution)/shard_map/ppermute | solution.py:488
  153.9 24.5 %collective-permute-start.15 = (bf16[128,2048]{1,0:T(8,128)(2,1)}, bf16[128,2048]{1,0:T(8,128)(2,1)}, u32[]{:S(2)}, u32[]{:S(2)}) collective-permute-start(bf16[128,2048]{1,0:T(8,128)(2,1)} %collective-permute-done.13.rest_14_), channel_id=1, source_target_pairs={{0,2},{1,3},{2,0},{3,1},{4,6},{5,7},{6,4},{7,5},{8,10},{9,11},{10,... | collective-permute-start | bytes 1572872 | tf_op jit(solution)/shard_map/ppermute | solution.py:488
  154.2 28.4 %collective-permute-start.10 = (bf16[128,2048]{1,0:T(8,128)(2,1)}, bf16[128,2048]{1,0:T(8,128)(2,1)}, u32[]{:S(2)}, u32[]{:S(2)}) collective-permute-start(bf16[128,2048]{1,0:T(8,128)(2,1)} %collective-permute-done.9.rest_10_), channel_id=1, source_target_pairs={{0,1},{1,0},{2,3},{3,2},{4,5},{5,4},{6,7},{7,6},{8,9},{9,8},{10,11... | collective-permute-start | bytes 1572872 | tf_op jit(solution)/shard_map/ppermute | solution.py:489
  156.3 26.6 %collective-permute-start.8 = (bf16[128,2048]{1,0:T(8,128)(2,1)}, bf16[128,2048]{1,0:T(8,128)(2,1)}, u32[]{:S(2)}, u32[]{:S(2)}) collective-permute-start(bf16[128,2048]{1,0:T(8,128)(2,1)} %collective-permute-done.7.rest_8_), channel_id=1, source_target_pairs={{0,1},{1,0},{2,3},{3,2},{4,5},{5,4},{6,7},{7,6},{8,9},{9,8},{10,11... | collective-permute-start | bytes 1572872 | tf_op jit(solution)/shard_map/ppermute | solution.py:490
  161.2 19.9 %copy-start.1 = (bf16[128,128]{1,0:T(8,128)(2,1)}, bf16[128,128]{1,0:T(8,128)(2,1)S(1)}, u32[]{:S(2)}) copy-start(bf16[128,128]{1,0:T(8,128)(2,1)S(1)} %slice.11.refs_0_) | copy-start | bytes 98308
  161.2 19.3 %collective-permute-start.1 = (bf16[128,128]{1,0:T(8,128)(2,1)S(1)}, bf16[128,128]{1,0:T(8,128)(2,1)S(1)}, u32[]{:S(2)}, u32[]{:S(2)}) collective-permute-start(bf16[128,128]{1,0:T(8,128)(2,1)S(1)} %slice.11.refs_0_), channel_id=1, source_target_pairs={{0,4},{1,5},{2,6},{3,7},{4,8},{5,9},{6,10},{7,11},{8,12},{9,13},{1... | collective-permute-start | bytes 98312 | tf_op jit(solution)/shard_map/ppermute | solution.py:519
  167.1 13.4 %collective-permute-start.2 = (bf16[128,128]{1,0:T(8,128)(2,1)S(1)}, bf16[128,128]{1,0:T(8,128)(2,1)S(1)}, u32[]{:S(2)}, u32[]{:S(2)}) collective-permute-start(bf16[128,128]{1,0:T(8,128)(2,1)S(1)} %slice.11.refs_0_), channel_id=1, source_target_pairs={{0,8},{1,9},{2,10},{3,11},{4,12},{5,13},{6,14},{7,15},{16,24},{17,... | collective-permute-start | bytes 98312 | tf_op jit(solution)/shard_map/ppermute | solution.py:519
  178.4 11.0 %collective-permute-start.14 = (bf16[128,2048]{1,0:T(8,128)(2,1)}, bf16[128,2048]{1,0:T(8,128)(2,1)}, u32[]{:S(2)}, u32[]{:S(2)}) collective-permute-start(bf16[128,2048]{1,0:T(8,128)(2,1)} %collective-permute-done.13.rest_14_), channel_id=1, source_target_pairs={{0,1},{1,0},{2,3},{3,2},{4,5},{5,4},{6,7},{7,6},{8,9},{9,8},{10,11... | collective-permute-start | bytes 1572872 | tf_op jit(solution)/shard_map/ppermute | solution.py:489
  180.5 0.6 copy-start.5
  180.5 8.9 %collective-permute-start.12 = (bf16[128,2048]{1,0:T(8,128)(2,1)}, bf16[128,2048]{1,0:T(8,128)(2,1)}, u32[]{:S(2)}, u32[]{:S(2)}) collective-permute-start(bf16[128,2048]{1,0:T(8,128)(2,1)} %collective-permute-done.11.rest_12_), channel_id=1, source_target_pairs={{0,1},{1,0},{2,3},{3,2},{4,5},{5,4},{6,7},{7,6},{8,9},{9,8},{10,11... | collective-permute-start | bytes 1572872 | tf_op jit(solution)/shard_map/ppermute | solution.py:490
  180.6 0.6 copy-start.6
  180.6 8.8 %collective-permute-start.16 = (bf16[128,2048]{1,0:T(8,128)(2,1)}, bf16[128,2048]{1,0:T(8,128)(2,1)}, u32[]{:S(2)}, u32[]{:S(2)}) collective-permute-start(bf16[128,2048]{1,0:T(8,128)(2,1)} %collective-permute-done.15.rest_16_), channel_id=1, source_target_pairs={{0,1},{1,0},{2,3},{3,2},{4,5},{5,4},{6,7},{7,6},{8,9},{9,8},{10,11... | collective-permute-start | bytes 1572872 | tf_op jit(solution)/shard_map/ppermute | solution.py:490
  182.6 4.1 %collective-permute-start.4 = (bf16[3,128,128]{2,1,0:T(8,128)(2,1)}, bf16[3,128,128]{2,1,0:T(8,128)(2,1)S(1)}, u32[]{:S(2)}, u32[]{:S(2)}) collective-permute-start(bf16[3,128,128]{2,1,0:T(8,128)(2,1)} %join.1.rest_2_), channel_id=1, source_target_pairs={{0,2},{1,3},{2,0},{3,1},{4,6},{5,7},{6,4},{7,5},{8,10},{9,11},{10,... | collective-permute-start | bytes 294920 | tf_op jit(solution)/shard_map/ppermute | solution.py:521
  182.9 6.5 %collective-permute-start.3 = (bf16[3,128,128]{2,1,0:T(8,128)(2,1)}, bf16[3,128,128]{2,1,0:T(8,128)(2,1)S(1)}, u32[]{:S(2)}, u32[]{:S(2)}) collective-permute-start(bf16[3,128,128]{2,1,0:T(8,128)(2,1)} %join.1.rest_2_), channel_id=1, source_target_pairs={{0,1},{1,0},{2,3},{3,2},{4,5},{5,4},{6,7},{7,6},{8,9},{9,8},{10,11... | collective-permute-start | bytes 294920 | tf_op jit(solution)/shard_map/ppermute | solution.py:522
  186.7 2.7 %copy-start.2 = (bf16[3,128,128]{2,1,0:T(8,128)(2,1)}, bf16[3,128,128]{2,1,0:T(8,128)(2,1)S(1)}, u32[]{:S(2)}) copy-start(bf16[3,128,128]{2,1,0:T(8,128)(2,1)S(1)} %collective-permute-done.4.rest_4_) | copy-start | bytes 294916
  186.7 2.6 %collective-permute-start.5 = (bf16[3,128,128]{2,1,0:T(8,128)(2,1)S(1)}, bf16[3,128,128]{2,1,0:T(8,128)(2,1)S(1)}, u32[]{:S(2)}, u32[]{:S(2)}) collective-permute-start(bf16[3,128,128]{2,1,0:T(8,128)(2,1)S(1)} %collective-permute-done.4.rest_4_), channel_id=1, source_target_pairs={{0,1},{1,0},{2,3},{3,2},{4,5},{5,4},{6,7},{7,6},{8,9},{9,8},{10,11... | collective-permute-start | bytes 294920 | tf_op jit(solution)/shard_map/ppermute | solution.py:523
  189.4 0.6 copy-start.3
  190.0 0.6 copy-start.4
